TPU v7x, 128 devices: a whole 4x4x4 slice. The times are simulated.
128 devices in a mesh: users: 16 (over y, x), seq: 8 (over z, core).
Axes of the slice: x: 4, y: 4, z: 4, core: 2. Of those that a mesh axis runs over, the one named last changes fastest.
Arguments:
- item_table: bfloat16 [262144, 512], P(('users', 'seq')), may hold values from -6 to 6
- item_ids: int32 [16, 3072], P('users', 'seq'), may hold values from 0 to 262143, as said below
- segment_ids: int32 [16, 3072], P('users', 'seq'), may hold values from 0 to 2, never falling along the last dimension, each value on 1 to 1536 neighbouring positions
- weight_in: bfloat16 [512, 2048], replicated, may hold values from -0.25 to 0.25
- weight_out: bfloat16 [512, 512], replicated, may hold values from -0.25 to 0.25
- gain_in: float32 [512], replicated, may hold values from 0.5 to 1.5
- gain_mid: float32 [512], replicated, may hold values from 0.5 to 1.5
- cotangent: bfloat16 [16, 3072, 512], P('users', 'seq'), may hold values from -6 to 6
Outputs:
- layer_out: bfloat16 [16, 3072, 512], P('users', 'seq')
- table_grad: float32 [262144, 512], P(('users', 'seq'))
- weight_in_grad: float32 [512, 2048], replicated
- weight_out_grad: float32 [512, 512], replicated
Inputs may be any that keep to these rules, and one draw needn't show every extreme that they name: `item_ids`: row r is held by device r // 2048 counted over users then seq. The 384 events of one device name rows of at most 6 events for each holding device, and in every draw each device has exactly 6 events whose rows one device holds.
All inputs are finite; a program needn't handle non-finite values.
Results may differ from a plain program's by a relative error of at most 0.006.
The roundings to bfloat16 on the way count: a program that leaves them out, or rounds other values in their place, can miss the bound.
Values may be sent and summed in bfloat16 or wider, within the bound.
No kernel may reach another device: no remote copies, remote signals or barrier semaphores. Data moves between devices by JAX's collectives and lax.ppermute only.
A program may use at most 128 MiB of HBM per device.

v0:
```python
import jax
import jax.numpy as jnp
from jax import lax
from jax.sharding import PartitionSpec as P

HEADS = 8
HEAD_DIM = 64


epsilon = 1e-05


def cut_along(x, dim, peers):
    before, after = (x.shape[:dim], x.shape[dim + 1 :])
    return jnp.moveaxis(x.reshape(*before, peers, -1, *after), dim, 0)


def laid_out(tiles, dim):
    tiles = jnp.moveaxis(tiles, 0, dim)
    dims = tiles.shape
    return tiles.reshape(*dims[:dim], dims[dim] * dims[dim + 1], *dims[dim + 2 :])


def exchange_both(x, axis, axes, splits, concats):
    sizes = [lax.axis_size(a) for a in axes]
    tiles = cut_along(x, splits[0], sizes[0])
    tiles = jnp.moveaxis(cut_along(tiles, splits[1] + 1, sizes[1]), 0, 1)
    inside = tiles.shape[2:]
    tiles = tiles.reshape(-1, *inside)
    tiles = lax.all_to_all(tiles, axis, split_axis=0, concat_axis=0, tiled=True)
    tiles = laid_out(tiles.reshape(*sizes, *inside), concats[0] + 1)
    return laid_out(tiles, concats[1])


def sent_together(arrays, axis, dim, along):
    both = jnp.concatenate(arrays, axis=along)
    whole, at, finished = (lax.psum_scatter(both, axis, scatter_dimension=dim, tiled=True), 0, [])
    for a in arrays:
        finished.append(lax.slice_in_dim(whole, at, at + a.shape[along], axis=along))
        at += a.shape[along]
    return tuple(finished)


def normalize(values):
    centred = values - jnp.mean(values, axis=-1, keepdims=True)
    inverse = lax.rsqrt(jnp.mean(centred * centred, axis=-1, keepdims=True) + epsilon)
    return (centred * inverse, inverse)


def norm_back(grad_hat, normed, inverse):
    return inverse * (
        grad_hat
        - jnp.mean(grad_hat, axis=-1, keepdims=True)
        - normed * jnp.mean(grad_hat * normed, axis=-1, keepdims=True)
    )


def silu_slope(values):
    sigma = jax.nn.sigmoid(values)
    return sigma * (1.0 + values * (1.0 - sigma))


def split_heads(matrix):
    return matrix.reshape(matrix.shape[0], HEADS, HEAD_DIM).transpose(1, 0, 2)


def join_heads(stacked):
    return stacked.transpose(1, 0, 2).reshape(stacked.shape[1], HEADS * HEAD_DIM)


def head_scores(query, keys, visible):
    scores = jnp.einsum(
        "qd,kd->qk", query, keys, preferred_element_type=jnp.float32
    ) * HEAD_DIM ** (-0.5)
    weights = jnp.where(visible, jax.nn.silu(scores), 0.0).astype(jnp.bfloat16)
    return (scores, weights)


def score_grads(scores, upstream, values, visible):
    dweights = jnp.einsum("qd,kd->qk", upstream, values, preferred_element_type=jnp.float32)
    return (jnp.where(visible, dweights * silu_slope(scores), 0.0) * HEAD_DIM ** (-0.5)).astype(
        jnp.bfloat16
    )


def key_side(weights, dscores, head_query, head_up):
    grad_k = jnp.einsum("qk,qd->kd", dscores, head_query, preferred_element_type=jnp.float32)
    grad_v = jnp.einsum("qk,qd->kd", weights, head_up, preferred_element_type=jnp.float32)
    return (grad_k, grad_v)


def body(item_table, item_ids, segment_ids, weight_in, weight_out, gain_in, gain_mid, cotangent):
    events = item_ids[0]
    segments = segment_ids[0]
    upstream = cotangent[0]
    count = events.shape[0]
    shard_rows = item_table.shape[0]
    width = item_table.shape[1]
    devices = lax.axis_size(("users", "seq"))
    user_groups = lax.axis_size("users")
    seq_groups = lax.axis_size("seq")
    capacity = 2 * count // devices
    owner_index = events // shard_rows
    owner_hits = (owner_index[:, None] == jnp.arange(devices, dtype=jnp.int32)[None, :]).astype(
        jnp.int32
    )
    arrival = jnp.sum(jnp.cumsum(owner_hits, axis=0) * owner_hits, axis=1) - 1
    slot_of = owner_index * capacity + arrival
    wanted = jnp.zeros((devices * capacity,), jnp.int32).at[slot_of].set(events % shard_rows)
    asked = lax.all_to_all(
        lax.all_to_all(
            wanted.reshape(user_groups, seq_groups, capacity),
            "users",
            split_axis=0,
            concat_axis=0,
            tiled=True,
        ),
        "seq",
        split_axis=1,
        concat_axis=1,
        tiled=True,
    )
    asked = asked.reshape(-1)
    served = item_table[asked]
    returned = exchange_both(
        served.reshape(user_groups, seq_groups, capacity, width),
        ("users", "seq"),
        ("users", "seq"),
        (0, 1),
        (0, 1),
    )
    fetched = returned.reshape(devices * capacity, width)[slot_of]
    fetched_f = fetched.astype(jnp.float32)
    normed_in, inverse_in = normalize(fetched_f)
    normed_b = (normed_in * gain_in).astype(jnp.bfloat16)
    hidden_pre = jnp.dot(normed_b, weight_in, preferred_element_type=jnp.float32)
    hidden = jax.nn.silu(hidden_pre)
    gate_part = hidden[:, :width]
    value_b = hidden[:, width : 2 * width].astype(jnp.bfloat16)
    query_b = hidden[:, 2 * width : 3 * width].astype(jnp.bfloat16)
    key_b = hidden[:, 3 * width :].astype(jnp.bfloat16)
    key_all, value_all, segment_all = (
        lax.all_gather(key_b, "seq", axis=0, tiled=True),
        lax.all_gather(value_b, "seq", axis=0, tiled=True),
        lax.all_gather(segments, "seq", axis=0, tiled=True),
    )
    seq_rank = lax.axis_index("seq")
    local_pos = seq_rank * count + jnp.arange(count, dtype=jnp.int32)
    whole_pos = jnp.arange(key_all.shape[0], dtype=jnp.int32)
    visible = (whole_pos[None, :] <= local_pos[:, None]) & (
        segment_all[None, :] == segments[:, None]
    )

    def forward_head(triple):
        head_query, head_key, head_value = triple
        scores, weights = head_scores(head_query, head_key, visible)
        return jnp.dot(weights, head_value, preferred_element_type=jnp.float32)

    query_heads = split_heads(query_b)
    key_heads = split_heads(key_all)
    value_heads = split_heads(value_all)
    mixed = join_heads(lax.map(forward_head, (query_heads, key_heads, value_heads)))
    normed_mid, inverse_mid = normalize(mixed)
    scaled_mid = normed_mid * gain_mid
    gated = (scaled_mid * gate_part).astype(jnp.bfloat16)
    layer = (fetched_f + jnp.dot(gated, weight_out, preferred_element_type=jnp.float32)).astype(
        jnp.bfloat16
    )
    grad_wout = jnp.einsum("td,te->de", gated, upstream, preferred_element_type=jnp.float32)
    grad_gated = jnp.einsum("te,de->td", upstream, weight_out, preferred_element_type=jnp.float32)
    grad_gate = grad_gated * scaled_mid
    grad_mixed = norm_back(grad_gated * gate_part * gain_mid, normed_mid, inverse_mid).astype(
        jnp.bfloat16
    )
    upstream_heads = split_heads(grad_mixed)

    def backward_head(quad):
        head_query, head_key, head_value, head_up = quad
        scores, weights = head_scores(head_query, head_key, visible)
        dscores = score_grads(scores, head_up, head_value, visible)
        grad_q = jnp.dot(dscores, head_key, preferred_element_type=jnp.float32)
        grad_k, grad_v = key_side(weights, dscores, head_query, head_up)
        return (grad_q, grad_k, grad_v)

    stacked_q, stacked_k, stacked_v = lax.map(
        backward_head, (query_heads, key_heads, value_heads, upstream_heads)
    )
    grad_query = join_heads(stacked_q)
    grad_key, grad_value = tuple(
        (
            part.astype(jnp.float32)
            for part in sent_together(
                (
                    join_heads(stacked_k).astype(jnp.bfloat16),
                    join_heads(stacked_v).astype(jnp.bfloat16),
                ),
                "seq",
                0,
                1,
            )
        )
    )
    grad_hidden = jnp.concatenate([grad_gate, grad_value, grad_query, grad_key], axis=1)
    grad_pre = (grad_hidden * silu_slope(hidden_pre)).astype(jnp.bfloat16)
    grad_win = jnp.einsum("td,tf->df", normed_b, grad_pre, preferred_element_type=jnp.float32)
    grad_normed = jnp.einsum("tf,df->td", grad_pre, weight_in, preferred_element_type=jnp.float32)
    grad_rows = norm_back(grad_normed * gain_in, normed_in, inverse_in) + upstream.astype(
        jnp.float32
    )
    weight_in_grad, weight_out_grad = lax.psum((grad_win, grad_wout), ("users", "seq"))
    outgoing = jnp.zeros((devices * capacity, width), jnp.float32).at[slot_of].set(grad_rows)
    incoming = exchange_both(
        outgoing.reshape(user_groups, seq_groups, capacity, width).astype(jnp.bfloat16),
        ("users", "seq"),
        ("users", "seq"),
        (0, 1),
        (0, 1),
    ).astype(jnp.float32)
    table_grad = (
        jnp.zeros((shard_rows, width), jnp.float32)
        .at[asked]
        .add(incoming.reshape(devices * capacity, width))
    )
    return (layer[None], table_grad, weight_in_grad, weight_out_grad)


def solution(mesh):
    in_specs = (
        P(("users", "seq"), None),
        P("users", "seq"),
        P("users", "seq"),
        P(),
        P(),
        P(),
        P(),
        P("users", "seq", None),
    )
    out_specs = (P("users", "seq", None), P(("users", "seq"), None), P(), P())
    return jax.shard_map(body, mesh=mesh, in_specs=in_specs, out_specs=out_specs, check_vma=False)
```

profile of v0, /device:TPU:1, one launch (start us, length us, event | category | flops | bytes accessed | tf_op | source)
XLA Modules:
  0.0 537.5 jit_solution(542985124928383671)
XLA Ops:
  12.5 13.9 %all_to_all.20 = s32[16,8,6]{2,1,0:T(8,128)S(1)} all-to-all(s32[16,8,6]{2,1,0:T(8,128)S(1)} %reshape.270), channel_id=1, replica_groups=mesh['users'=16,'seq'=8] {'users'}, dimensions={0} | all-to-all | bytes 6144 | tf_op jit(solution)/shard_map/all_to_all | solution.py:111
  26.5 11.9 %all_to_all.21 = s32[16,8,6]{0,2,1:T(8,128)S(1)} all-to-all(s32[16,8,6]{0,2,1:T(8,128)S(1)} %copy.40), channel_id=1, replica_groups=mesh['users'=16,'seq'=8] {'seq'}, dimensions={1} | all-to-all | bytes 6144 | tf_op jit(solution)/shard_map/all_to_all | solution.py:110
  39.4 4.6 gather_fusion
  45.2 4.2 all-to-all-start.2
  49.4 19.1 %all-to-all-done.2 = bf16[128,1,1,6,512]{4,3,2,1,0:T(8,128)(2,1)S(1)} async-done(((bf16[128,1,1,6,512]{4,3,2,1,0:T(8,128)(2,1)}), bf16[128,1,1,6,512]{4,3,2,1,0:T(8,128)(2,1)S(1)}, u32[]{:S(2)}, u32[]{:S(2)}) %all-to-all-start.2) | async-done | bytes 786464 | tf_op jit(solution)/shard_map/all_to_all | solution.py:30
  79.2 12.5 %all-gather = s32[1,3072]{1,0:T(1,128)S(1)} all-gather(s32[1,384]{1,0:T(1,128)S(1)} %copy-done.17), channel_id=2, replica_groups=mesh['users'=16,'seq'=8] {'seq'}, dimensions={1}, use_global_device_ids=true | all-gather | bytes 13824 | tf_op jit(solution)/shard_map/all_gather | solution.py:145
  93.1 10.0 %all-gather.4.cloned.1.call-done = bf16[3072,512]{1,0:T(8,128)(2,1)} async-done(((bf16[384,512]{1,0:T(8,128)(2,1)}), bf16[3072,512]{1,0:T(8,128)(2,1)}) %all-gather.4.cloned.1.call-update) | async-done | bytes 3145744 | tf_op jit(solution)/shard_map/all_gather | solution.py:143
  103.1 4.7 copy.44
  107.8 6.6 %copy.47 = bf16[8,3072,64]{2,1,0:T(8,128)(2,1)} copy(bf16[8,3072,64]{1,2,0:T(8,128)(2,1)} %bitcast.190) | data formatting | bytes 6291456
  114.4 18.7 %all-gather.6.cloned.1.call-done = bf16[3072,512]{1,0:T(8,128)(2,1)} async-done(((bf16[384,512]{1,0:T(8,128)(2,1)}), bf16[3072,512]{1,0:T(8,128)(2,1)}) %all-gather.6.cloned.1.call-update) | async-done | bytes 3145744 | tf_op jit(solution)/shard_map/all_gather | solution.py:144
  133.1 4.7 copy.45
  137.8 6.6 %copy.48 = bf16[8,3072,64]{2,1,0:T(8,128)(2,1)} copy(bf16[8,3072,64]{1,2,0:T(8,128)(2,1)} %bitcast.191) | data formatting | bytes 6291456
  144.4 29.8 %while.26 = (s32[]{:T(128)}, f32[8,384,64]{1,2,0:T(8,128)S(1)}, bf16[8,384,64]{2,1,0:T(8,128)(2,1)}, bf16[8,3072,64]{2,1,0:T(8,128)(2,1)}, bf16[8,3072,64]{2,1,0...) while((s32[]{:T(128)}, f32[8,384,64]{1,2,0:T(8,128)S(1)}, ...), condition=%wide.region_7.8_spmd.clone, body=%wide.region_6.7_spmd.clone.sunk | while | flops 313786368 | bytes 1787997 | solution.py:162
  180.9 112.8 %while.27 = (s32[]{:T(128)}, f32[8,384,64]{1,2,0:T(8,128)}, bf16[8,3072,64]{1,2,0:T(8,128)(2,1)}, bf16[8,3072,64]{1,2,0:T(8,128)(2,1)}, bf16[8,384,64]{1,2,0:T(8...) while((s32[]{:T(128)}, f32[8,384,64]{1,2,0:T(8,128)}, ...), condition=%wide.region_13.14_spmd.clone, body=%wide.region_12.13_spmd.clone.sunk | while | flops 783286272 | bytes 25594996 | solution.py:185
  225.2 4.0 multiply_convert_fusion.4
  293.7 4.7 copy.55
  298.5 4.6 copy.56
  303.1 6.4 %pad_maximum_fusion = bf16[3072,1024]{1,0:T(8,128)(2,1)} fusion(bf16[3072,512]{1,0:T(8,128)(2,1)} %copy.56, bf16[3072,512]{1,0:T(8,128)(2,1)} %copy.55), kind=kLoop, calls=%fused_computation.60 | loop fusion | flops 12582912 | bytes 12582912 | tf_op jit(solution)/shard_map/concatenate | solution.py:36
  313.3 37.7 %reduce-scatter.2.cloned.1.call-done = bf16[384,1024]{1,0:T(8,128)(2,1)} async-done(((bf16[3072,1024]{1,0:T(8,128)(2,1)}), bf16[384,1024]{1,0:T(8,128)(2,1)}) %reduce-scatter.2.cloned.1.call-update) | async-done | bytes 786448 | tf_op jit(solution)/shard_map/reduce_scatter | solution.py:37
  370.0 8.5 %all-to-all-start.3 = ((bf16[128,1,1,6,512]{4,3,2,1,0:T(8,128)(2,1)}), bf16[128,1,1,6,512]{4,3,2,1,0:T(8,128)(2,1)S(1)}, u32[]{:S(2)}, u32[]{:S(2)}) async-start(bf16[128,1,1,6,512]{4,3,2,1,0:T(8,128)(2,1)} %bitcast.31), calls=%async_computation.4 | async-start | bytes 2097152 | tf_op jit(solution)/shard_map/all_to_all | solution.py:30
  380.9 19.1 %all-to-all-done.3 = bf16[128,1,1,6,512]{4,3,2,1,0:T(8,128)(2,1)S(1)} async-done(((bf16[128,1,1,6,512]{4,3,2,1,0:T(8,128)(2,1)}), bf16[128,1,1,6,512]{4,3,2,1,0:T(8,128)(2,1)S(1)}, u32[]{:S(2)}, u32[]{:S(2)}) %all-to-all-start.3) | async-done | bytes 786464 | tf_op jit(solution)/shard_map/all_to_all | solution.py:30
  401.3 9.5 %scatter_custom_fusion.2 = f32[2048,512]{1,0:T(8,128)} fusion(s32[768]{0:T(1024)} %copy-done.15, f32[768,512]{1,0:T(8,128)} %reshape.319, f32[]{:T(128)} %constant.103.clone.1), kind=kCustom, calls=%fused_computation.65 | custom fusion | flops 393216 | bytes 4194816 | tf_op jit(solution)/shard_map/scatter-add | solution.py:222
  410.8 114.4 %all-reduce.3.cloned.1.call-done = (f32[512,2048]{1,0:T(8,128)}, f32[512,512]{1,0:T(8,128)}) async-done(((f32[512,2048]{1,0:T(8,128)}, f32[512,512]{1,0:T(8,128)}), (f32[512,2048]{1,0:T(8,128)}, f32[512,512]{1,0:T(8,128)})) %all-reduce.3.cloned.1.call-update) | async-done | bytes 5242896 | tf_op jit(solution)/shard_map/psum | solution.py:210
  525.2 4.8 copy.89
  (153 shorter events, 192.0 us)
Async XLA Ops:
  7.2 66.2 %copy-start = (bf16[512,2048]{1,0:T(8,128)(2,1)S(1)}, bf16[512,2048]{1,0:T(8,128)(2,1)}, u32[]{:S(2)}) copy-start(bf16[512,2048]{1,0:T(8,128)(2,1)} %param.15) | copy-start | bytes 6291460
  9.5 39.9 %copy-start.16 = (s32[384]{0:T(512)}, s32[384]{0:T(512)S(1)}, u32[]{:S(2)}) copy-start(s32[384]{0:T(512)S(1)} %fusion.96) | copy-start | bytes 4612
  45.2 23.3 %all-to-all-start.2 = ((bf16[128,1,1,6,512]{4,3,2,1,0:T(8,128)(2,1)}), bf16[128,1,1,6,512]{4,3,2,1,0:T(8,128)(2,1)S(1)}, u32[]{:S(2)}, u32[]{:S(2)}) async-start(bf16[128,1,1,6,512]{4,3,2,1,0:T(8,128)(2,1)} %bitcast.193), calls=%async_computation.2 | async-start | bytes 2097152 | tf_op jit(solution)/shard_map/all_to_all | solution.py:30
  49.3 24.1 %copy-start.11 = (f32[512]{0:T(512)S(1)}, f32[512]{0:T(512)}, u32[]{:S(2)}) copy-start(f32[512]{0:T(512)} %param.17) | copy-start | bytes 6148
  49.3 53.8 %all-gather.4.cloned.1.call-start = ((), (), s32[]{:S(2)}) async-start(), calls=%async_computation.5 | async-start | bytes 3538944 | tf_op jit(solution)/shard_map/all_gather | solution.py:143
  68.5 1.0 copy-start.5
  72.9 4.4 copy-start.1
  73.1 4.3 copy-start.9
  73.4 4.0 copy-start.13
  77.4 1.8 copy-start.17
  78.4 54.7 %all-gather.6.cloned.1.call-start = ((), (), s32[]{:S(2)}) async-start(), calls=%async_computation.6 | async-start | bytes 3538944 | tf_op jit(solution)/shard_map/all_gather | solution.py:144
  79.1 271.9 %reduce-scatter.2.cloned.1.call-start = ((), (), s32[]{:S(2)}) async-start(), calls=%async_computation.7 | async-start | bytes 7077888 | tf_op jit(solution)/shard_map/reduce_scatter | solution.py:37
  174.3 1.4 copy-start.6
  174.3 1.4 copy-start.18
  175.5 3.2 copy-start.3
  178.7 133.1 %copy-start.7 = (bf16[384,512]{1,0:T(8,128)(2,1)}, bf16[384,512]{1,0:T(8,128)(2,1)S(1)}, u32[]{:S(2)}) copy-start(bf16[384,512]{1,0:T(8,128)(2,1)S(1)} %get-tuple-element.222) | copy-start | bytes 1179652
  309.5 215.7 %all-reduce.3.cloned.1.call-start = ((), (), s32[]{:S(2)}) async-start(), calls=%async_computation.8 | async-start | bytes 10485760 | tf_op jit(solution)/shard_map/psum | solution.py:210
  352.4 4.2 copy-start.2
  352.4 4.2 copy-start.10
  352.4 4.2 copy-start.12
  352.4 4.2 copy-start.14
  355.4 1.1 copy-start.4
  370.0 29.9 %all-to-all-start.3 = ((bf16[128,1,1,6,512]{4,3,2,1,0:T(8,128)(2,1)}), bf16[128,1,1,6,512]{4,3,2,1,0:T(8,128)(2,1)S(1)}, u32[]{:S(2)}, u32[]{:S(2)}) async-start(bf16[128,1,1,6,512]{4,3,2,1,0:T(8,128)(2,1)} %bitcast.31), calls=%async_computation.4 | async-start | bytes 2097152 | tf_op jit(solution)/shard_map/all_to_all | solution.py:30
  525.2 4.8 copy-start.8
  (1 other events, 0.6 us)
Sparse Core Ops, SparseCore 0:
  78.5 24.5 all-gather.3
  105.4 27.6 all-gather.5
  309.6 41.3 reduce-scatter.1
  360.1 165.0 all-reduce.2
where the time goes:
time: 540 us; the launch traced here: 538 us
  waiting for transfers between devices  220 us (41%)
  matrix products  160 us (30%)
  local copies, waits for them, and re-layouts  63.6 us (12%)
  blocking collectives  38.3 us (7%)
  other arithmetic  28.8 us (5%)
  between operations  14.2 us (3%)
  starting transfers between devices  12.8 us (2%)
    psum x1, waiting for transfers between devices, body(): lax.psum((grad_win, grad_wout), ('users', 'seq'))  114 us
    all_to_all x2, waiting for transfers between devices, exchange_both(): tiles = lax.all_to_all(tiles, axis, split_axis=0, concat_axis=0, tiled=True)  38.2 us
    reduce_scatter x1, waiting for transfers between devices, sent_together(): lax.psum_scatter(both, axis, scatter_dimension=dim, tiled=True)  37.7 us
    dot_general x8, matrix products, score_grads(): jnp.einsum('qd,kd->qk', upstream, values, preferred_element_type=jnp.floa...  31.6 us
    dot_general x8, matrix products, forward_head(): return jnp.dot(weights, head_value, preferred_element_type=jnp.float32)  29.7 us
    dot_general x8, matrix products, key_side(): jnp.einsum('qk,qd->kd', weights, head_up, preferred_element_type=jnp.floa...  26.7 us
    unnamed x43, local copies, waits for them, and re-layouts  22.9 us
    dot_general x8, matrix products, backward_head(): grad_q = jnp.dot(dscores, head_key, preferred_element_type=jnp.float32)  20.8 us
  transfers between devices with their start and end apart: 6, of which 6 were waited for; matrix products, arithmetic and copies ran while one was open for 7% of the time, Pallas kernels for 0%

commit v1 on v0

v1 whole, which is shorter than its diff:
```python
import functools
import jax
import jax.numpy as jnp
from jax import lax
from jax.experimental import pallas as pl
from jax.experimental.pallas import tpu as pltpu
from jax.sharding import PartitionSpec as P

HEADS = 8
HEAD_DIM = 64
SLOTS = 8
CAP = 6
BLOCK = 512
EPSILON = 1e-05
BOTH = ("users", "seq")
ORDER = (0, 2, 1, 3)

f32 = jnp.float32
bf16 = jnp.bfloat16
i32 = jnp.int32


def iota(shape, dim):
    return lax.broadcasted_iota(i32, shape, dim)


def mm(a, b):
    return jnp.dot(a, b, preferred_element_type=f32)


def mm_nt(a, b):
    return lax.dot_general(a, b, (((1,), (1,)), ((), ())), preferred_element_type=f32)


def call(kernel, out_shape, args, *, name, grid=None, in_specs=None, out_specs=None, scratch=(), flops=0, moved=0):
    params = dict(vmem_limit_bytes=60 * 1024 * 1024)
    extra = {}
    if grid is not None:
        params["dimension_semantics"] = ("arbitrary",) * len(grid)
        extra["grid"] = grid
    if in_specs is not None:
        extra["in_specs"] = in_specs
    if out_specs is not None:
        extra["out_specs"] = out_specs
    return pl.pallas_call(
        kernel,
        out_shape=out_shape,
        scratch_shapes=scratch,
        name=name,
        compiler_params=pltpu.CompilerParams(**params),
        cost_estimate=pl.CostEstimate(flops=flops, bytes_accessed=moved, transcendentals=0),
        **extra,
    )(*args)


def normalize(values):
    centred = values - jnp.mean(values, axis=-1, keepdims=True)
    inverse = lax.rsqrt(jnp.mean(centred * centred, axis=-1, keepdims=True) + EPSILON)
    return centred * inverse, inverse


def slots_kernel(shard_rows, ids_ref, seg_ref, wanted_ref, row_ref, col_ref):
    devices, lanes = wanted_ref.shape
    count = ids_ref.shape[1]
    ids = ids_ref[...]
    owner = lax.shift_right_logical(ids, shard_rows.bit_length() - 1)
    local = (ids & (shard_rows - 1)).astype(f32)
    held = owner == iota((devices, count), 0)
    hit = jnp.where(held, 1.0, 0.0)
    earlier = jnp.where(iota((count, count), 0) < iota((count, count), 1), 1.0, 0.0)
    rank = mm(hit.astype(bf16), earlier.astype(bf16))
    marked = jnp.where(held, rank, -1.0)
    lane = iota((devices, lanes), 1)
    wanted = jnp.zeros((devices, lanes), f32)
    for c in range(CAP):
        column = jnp.sum(jnp.where(marked == float(c), local, 0.0), axis=1, keepdims=True)
        wanted = jnp.where(lane == c, column, wanted)
    seg = seg_ref[...]
    below1 = jnp.sum(jnp.where(seg < 1, 1.0, 0.0), axis=1, keepdims=True)
    below2 = jnp.sum(jnp.where(seg < 2, 1.0, 0.0), axis=1, keepdims=True)
    wanted = jnp.where(lane == CAP, below1, wanted)
    wanted = jnp.where(lane == CAP + 1, below2, wanted)
    wanted_ref[...] = wanted.astype(i32)
    slot = owner.astype(f32) * float(SLOTS) + jnp.sum(hit * rank, axis=0, keepdims=True)
    row_ref[...] = jnp.broadcast_to(slot, row_ref.shape).astype(i32)
    col_ref[...] = jnp.transpose(jnp.broadcast_to(slot, (lanes, count))).astype(i32)


def serve_kernel(asked_ref, table_ref, served_ref, row_ref, bounds_ref, col_ref):
    step = pl.program_id(0)
    block = served_ref.shape[0]
    devices, lanes = asked_ref.shape

    @pl.when(step == 0)
    def _():
        asked = asked_ref[...].astype(f32)
        wide = jnp.broadcast_to(asked[:, None, :], (devices, SLOTS, lanes))
        sub = iota((devices, SLOTS, lanes), 1)
        lane = iota((devices, SLOTS, lanes), 2)
        column = jnp.sum(jnp.where(sub == lane, wide, 0.0), axis=2, keepdims=True)
        column = jnp.where(iota((devices, SLOTS, 1), 1) < CAP, column, -1.0)
        column = jnp.broadcast_to(column, (devices, SLOTS, lanes)).reshape(devices * SLOTS, lanes)
        col_ref[...] = column
        row_ref[...] = jnp.transpose(column)[: row_ref.shape[0]].astype(i32)
        group = lax.axis_index("users")
        mine = lax.div(iota((devices, lanes), 0), SLOTS) == group
        bounds = jnp.sum(jnp.where(mine, asked, 0.0), axis=0, keepdims=True)
        bounds_ref[...] = jnp.broadcast_to(bounds, bounds_ref.shape).astype(i32)

    column = col_ref[pl.ds(pl.multiple_of(step * block, block), block), :].astype(i32)
    parts = []
    for at in range(table_ref.shape[0] // lanes):
        parts.append(jnp.where(column == iota((block, lanes), 1) + at * lanes, 1.0, 0.0).astype(bf16))
    served_ref[...] = mm(jnp.concatenate(parts, axis=1), table_ref[...]).astype(bf16)


def arrange_kernel(got_ref, col_ref, gain_ref, fetched_ref, xin_ref):
    slot = col_ref[...]
    count, lanes = slot.shape
    parts = []
    for at in range(got_ref.shape[0] // lanes):
        parts.append(jnp.where(slot == iota((count, lanes), 1) + at * lanes, 1.0, 0.0).astype(bf16))
    fetched = mm(jnp.concatenate(parts, axis=1), got_ref[...])
    fetched_ref[...] = fetched.astype(bf16)
    normed, _ = normalize(fetched)
    xin_ref[...] = (normed * gain_ref[...]).astype(bf16)


def seg_start(position, one, two):
    return jnp.where(position < one, 0, jnp.where(position < two, one, two))


def visible(i, j, one, two):
    where_q = iota((1, BLOCK), 1) + i * BLOCK
    start = seg_start(where_q, one, two)
    where_k = iota((BLOCK, BLOCK), 0) + j * BLOCK
    return (where_k >= start) & (where_k <= where_q)


def forward_kernel(
    xin_ref, cot_ref, win_ref, wout_ref, gain_ref, bounds_ref,
    q_ref, k_ref, vk_ref, slope_ref, u_ref, dg_ref, mixed_ref, stats_ref,
    q_all, v_all, vk_all,
):
    i = pl.program_id(0)
    one, two = bounds_ref[0, CAP], bounds_ref[0, CAP + 1]
    here = pl.ds(pl.multiple_of(i * BLOCK, BLOCK), BLOCK)
    pre = mm_nt(win_ref[...], xin_ref[...])
    tanh = jnp.tanh(pre * 0.5)
    plus = 1.0 + tanh
    hidden = (0.5 * pre) * plus
    slope_ref[...] = 0.5 * (plus + hidden * (1.0 - tanh))
    d = HEAD_DIM
    u = hidden[:d]
    query = (hidden[d : 2 * d].astype(bf16).astype(f32) * 0.0625).astype(bf16)
    vk = hidden[2 * d :]
    vk_t = vk.astype(bf16)
    turned = jnp.transpose(vk).astype(bf16)
    u_ref[...] = u
    q_ref[...] = query
    k_ref[...] = vk_t[d:]
    vk_ref[...] = turned
    q_all[:d, :] = jnp.zeros((d, BLOCK), bf16)
    q_all[d:, :] = query
    v_all[:, here] = vk_t[:d]
    vk_all[here, :] = turned
    mixed_ref[...] = jnp.zeros(mixed_ref.shape, f32)

    def pair(j, carry):
        there = pl.ds(pl.multiple_of(j * BLOCK, BLOCK), BLOCK)
        half = mm(vk_all[there, :], q_all[...])
        weights = half + half * jnp.tanh(half)
        weights = jnp.where(visible(i, j, one, two), weights, 0.0).astype(bf16)
        mixed_ref[...] += mm(v_all[:, there], weights)
        return carry

    first = lax.div(seg_start(i * BLOCK, one, two), BLOCK)
    lax.fori_loop(first, i + 1, pair, 0)
    dg = mm_nt(wout_ref[...], cot_ref[...])
    dg_ref[...] = dg
    mixed = mixed_ref[...]
    e = dg * u * gain_ref[:, :1]
    mean = jnp.sum(mixed, axis=0, keepdims=True) * (1.0 / d)
    centred = mixed - mean
    stats_ref[0:1, :] = mean
    stats_ref[1:2, :] = jnp.sum(centred * centred, axis=0, keepdims=True)
    stats_ref[2:3, :] = jnp.sum(e, axis=0, keepdims=True)
    stats_ref[3:4, :] = jnp.sum(e * centred, axis=0, keepdims=True)


def middle_kernel(stats_ref, mixed_ref, dg_ref, u_ref, slope_ref, gain_ref, gated_ref, dm_ref, dpre_ref):
    width = HEADS * HEAD_DIM
    stats = stats_ref[...]
    means = [stats[h, 0:1] for h in range(HEADS)]
    mean = functools.reduce(jnp.add, means) * (1.0 / HEADS)
    var, m_e, m_em = 0.0, 0.0, 0.0
    for h in range(HEADS):
        off = means[h] - mean
        var = var + stats[h, 1:2] + HEAD_DIM * off * off
        m_e = m_e + stats[h, 2:3]
        m_em = m_em + stats[h, 3:4] + off * stats[h, 2:3]
    inverse = lax.rsqrt(var * (1.0 / width) + EPSILON)
    m_e = m_e * (1.0 / width)
    m_eh = m_em * inverse * (1.0 / width)
    gain = gain_ref[:, :1]
    hat = (mixed_ref[...] - mean) * inverse
    scaled = hat * gain
    u = u_ref[...]
    dg = dg_ref[...]
    gated_ref[0] = (scaled * u).astype(bf16)
    e = dg * u * gain
    dm = (inverse * (e - m_e - hat * m_eh)).astype(bf16)
    dm_ref[...] = (dm.astype(f32) * 0.0625).astype(bf16)
    dpre_ref[0] = (dg * scaled * slope_ref[...]).astype(bf16)


def backward_kernel(
    steps, q_ref, k_ref, vk_ref, dm_ref, bounds_ref, xin_ref, cot_ref, slope_ref, gated_ref, dpu_ref,
    dpre_ref, dw_ref, dq_all, dk_all, dv_all, win_acc, wout_acc,
):
    g = pl.program_id(0)
    one, two = bounds_ref[0, CAP], bounds_ref[0, CAP + 1]
    d = HEAD_DIM

    @pl.when(g == 0)
    def _():
        dk_all[...] = jnp.zeros(dk_all.shape, f32)
        dv_all[...] = jnp.zeros(dv_all.shape, f32)
        dq_all[...] = jnp.zeros(dq_all.shape, f32)
        win_acc[...] = jnp.zeros(win_acc.shape, f32)
        wout_acc[...] = jnp.zeros(wout_acc.shape, f32)

    @pl.when(g < steps)
    def _():
        here = pl.ds(pl.multiple_of(g * BLOCK, BLOCK), BLOCK)
        blank = jnp.zeros((d, BLOCK), bf16)
        query = q_ref[:, here]
        up = dm_ref[:, here]
        query2 = jnp.concatenate([blank, query], axis=0)
        up2 = jnp.concatenate([up, blank], axis=0)

        def pair(j, carry):
            there = pl.ds(pl.multiple_of(j * BLOCK, BLOCK), BLOCK)
            vk = vk_ref[there, :]
            half = mm(vk, query2)
            upper = mm(vk, up2)
            tanh = jnp.tanh(half)
            plus = 1.0 + tanh
            weights = half * plus
            dscores = upper * (plus + weights * (1.0 - tanh))
            seen = visible(g, j, one, two)
            weights = jnp.where(seen, weights, 0.0).astype(bf16)
            dscores = jnp.where(seen, dscores, 0.0).astype(bf16)
            dv_all[:, there] += mm_nt(up, weights)
            dk_all[:, there] += mm_nt(query, dscores)
            dq_all[:, here] += mm(k_ref[:, there], dscores)
            return carry

        first = lax.div(seg_start(g * BLOCK, one, two), BLOCK)
        lax.fori_loop(first, g + 1, pair, 0)

    @pl.when(g >= steps)
    def _():
        s = g - steps
        count = xin_ref.shape[0]
        here = pl.ds(pl.multiple_of(s * count, count), count)
        slope = slope_ref[...]
        dpre = jnp.concatenate(
            [
                dpu_ref[0],
                (dq_all[:, here] * slope[d : 2 * d]).astype(bf16),
                (dv_all[:, here] * 16.0 * slope[2 * d : 3 * d]).astype(bf16),
                (dk_all[:, here] * 16.0 * slope[3 * d :]).astype(bf16),
            ],
            axis=0,
        )
        dpre_ref[0] = dpre
        win_acc[...] += mm(dpre, xin_ref[...])
        wout_acc[...] += mm(gated_ref[0], cot_ref[...])

    @pl.when(g == pl.num_programs(0) - 1)
    def _():
        parts = dw_ref.shape[0]
        turned = jnp.transpose(win_acc[...])
        rows = turned.shape[0] // parts
        for p in range(parts):
            dw_ref[p, :rows, :] = turned[p * rows : (p + 1) * rows]
            dw_ref[p, rows:, :] = wout_acc[8 * (p // 2) : 8 * (p // 2) + 8, 256 * (p % 2) : 256 * (p % 2) + 256]


def rows_kernel(dpre_ref, win_ref, gain_ref, fetched_ref, cot_ref, row_ref, out_ref, whole):
    d = HEAD_DIM
    width = fetched_ref.shape[1]
    for h in range(HEADS):
        for at, block in enumerate(ORDER):
            whole[block * width + h * d : block * width + (h + 1) * d, :] = dpre_ref[h, at * d : (at + 1) * d, :]
    dxin = jnp.transpose(mm(win_ref[...], whole[...]))
    normed, inverse = normalize(fetched_ref[...].astype(f32))
    f = dxin * gain_ref[...]
    drow = inverse * (
        f - jnp.mean(f, axis=-1, keepdims=True) - normed * jnp.mean(f * normed, axis=-1, keepdims=True)
    ) + cot_ref[...].astype(f32)
    drow = drow.astype(bf16)
    slots = out_ref.shape[0]
    count = drow.shape[0]
    pick = jnp.where(row_ref[0:1, :] == iota((slots, count), 0), 1.0, 0.0).astype(bf16)
    out_ref[...] = mm(pick, drow).astype(bf16)


def table_kernel(row_ref, got_ref, out_ref):
    block = out_ref.shape[0]
    slots = got_ref.shape[0]
    at = pl.program_id(0) * block
    pick = jnp.where(row_ref[0:1, :] == iota((block, slots), 0) + at, 1.0, 0.0).astype(bf16)
    out_ref[...] = mm(pick, got_ref[...])


def weights_kernel(got_ref, win_ref, wout_ref):
    d = HEAD_DIM
    rows, columns = win_ref.shape
    width = columns // 4
    for at, block in enumerate(ORDER):
        for pair in range(HEADS // 2):
            left = got_ref[0, 2 * pair, :rows, at * d : (at + 1) * d]
            right = got_ref[0, 2 * pair + 1, :rows, at * d : (at + 1) * d]
            start = block * width + pair * 2 * d
            win_ref[:, start : start + 2 * d] = jnp.concatenate([left, right], axis=1)
    for h in range(HEADS):
        wout_ref[h, 0] = got_ref[0, h, rows:, :]


def exchange(x, axis):
    return lax.all_to_all(x, axis, split_axis=0, concat_axis=0, tiled=True)


def struct(shape, dtype):
    return jax.ShapeDtypeStruct(shape, dtype)


def body(item_table, item_ids, segment_ids, weight_in, weight_out, gain_in, gain_mid, cotangent):
    shard_rows, width = item_table.shape
    count = item_ids.shape[1]
    users, seq = lax.axis_size("users"), lax.axis_size("seq")
    devices = users * seq
    length = count * seq
    d = HEAD_DIM
    slots = devices * SLOTS
    upstream = cotangent[0]
    gain_row = gain_in.reshape(1, width)
    head = lax.axis_index("seq")

    cot_all = lax.all_gather(upstream, "seq", axis=0, tiled=True)
    wanted, slot_row, slot_col = call(
        functools.partial(slots_kernel, shard_rows),
        (struct((devices, 128), i32), struct((8, count), i32), struct((count, 128), i32)),
        (item_ids, segment_ids),
        name="slots", flops=2 * devices * count * count, moved=1 << 19,
    )
    asked = exchange(wanted.reshape(devices, 1, 128), BOTH).reshape(devices, 128)
    steps = 4
    whole = lambda *shape: pl.BlockSpec(shape, lambda g: (0,) * len(shape))
    smem = pl.BlockSpec(memory_space=pltpu.SMEM)
    served, asked_row, bounds = call(
        serve_kernel,
        (struct((slots, width), bf16), struct((8, slots), i32), struct((8, 128), i32)),
        (asked, item_table),
        name="serve", grid=(steps,),
        in_specs=[whole(devices, 128), whole(shard_rows, width)],
        out_specs=[pl.BlockSpec((slots // steps, width), lambda g: (g, 0)), whole(8, slots), whole(8, 128)],
        scratch=[pltpu.VMEM((slots, 128), f32)],
        flops=2 * slots * shard_rows * width, moved=4 << 20,
    )
    got = exchange(served.reshape(devices, SLOTS, width), BOTH).reshape(slots, width)
    fetched, xin = call(
        arrange_kernel,
        (struct((count, width), bf16), struct((count, width), bf16)),
        (got, slot_col, gain_row),
        name="arrange", flops=2 * count * slots * width, moved=2 << 20,
    )
    xin_all = lax.all_gather(xin, "seq", axis=0, tiled=True)

    mine = lax.dynamic_index_in_dim(weight_in.reshape(width, 4, HEADS, d), head, 2, keepdims=False)
    win_t = jnp.stack([mine[:, b] for b in ORDER], axis=1).reshape(width, 4 * d).T
    wout_h = lax.dynamic_slice_in_dim(weight_out, head * d, d, axis=0)
    gain_h = jnp.broadcast_to(lax.dynamic_slice_in_dim(gain_mid, head * d, d)[:, None], (d, 128))

    blocks = length // BLOCK
    lane = lambda rows: pl.BlockSpec((rows, BLOCK), lambda g: (0, g))
    rowed = lambda columns: pl.BlockSpec((BLOCK, columns), lambda g: (g, 0))
    q_t, k_t, vk, slope, u, dg, mixed, stats = call(
        forward_kernel,
        (
            struct((d, length), bf16), struct((d, length), bf16), struct((length, 2 * d), bf16),
            struct((4 * d, length), f32), struct((d, length), f32), struct((d, length), f32),
            struct((d, length), f32), struct((4, length), f32),
        ),
        (xin_all, cot_all, win_t, wout_h, gain_h, bounds),
        name="forward", grid=(blocks,),
        in_specs=[rowed(width), rowed(width), whole(4 * d, width), whole(d, width), whole(d, 128), smem],
        out_specs=[lane(d), lane(d), rowed(2 * d), lane(4 * d), lane(d), lane(d), lane(d), lane(4)],
        scratch=[pltpu.VMEM((2 * d, BLOCK), bf16), pltpu.VMEM((d, length), bf16), pltpu.VMEM((length, 2 * d), bf16)],
        flops=1 << 33, moved=12 << 20,
    )
    stats_all = lax.all_gather(stats, "seq", axis=0, tiled=False)

    part = lambda rows: pl.BlockSpec((rows, count), lambda g: (0, g))
    gated, dm, dpre_u = call(
        middle_kernel,
        (struct((seq, d, count), bf16), struct((d, length), bf16), struct((seq, d, count), bf16)),
        (stats_all, mixed, dg, u, slope, gain_h),
        name="middle", grid=(seq,),
        in_specs=[pl.BlockSpec((seq, 4, count), lambda g: (0, 0, g)), part(d), part(d), part(d), part(d), whole(d, 128)],
        out_specs=[
            pl.BlockSpec((1, d, count), lambda g: (g, 0, 0)), part(d), pl.BlockSpec((1, d, count), lambda g: (g, 0, 0)),
        ],
        flops=1 << 24, moved=5 << 20,
    )
    gated_mine = exchange(gated, "seq").reshape(width, count)
    layer = (
        fetched.astype(f32)
        + lax.dot_general(gated_mine, weight_out, (((0,), (0,)), ((), ())), preferred_element_type=f32)
    ).astype(bf16)

    late = lambda g: jnp.maximum(g - blocks, 0)
    dpre, dw = call(
        functools.partial(backward_kernel, blocks),
        (struct((seq, 4 * d, count), bf16), struct((users, width // users + 8, 4 * d), f32)),
        (q_t, k_t, vk, dm, bounds, xin_all, cot_all, slope, gated, dpre_u),
        name="backward", grid=(blocks + seq,),
        in_specs=[
            whole(d, length), whole(d, length), whole(length, 2 * d), whole(d, length), smem,
            pl.BlockSpec((count, width), lambda g: (late(g), 0)),
            pl.BlockSpec((count, width), lambda g: (late(g), 0)),
            pl.BlockSpec((4 * d, count), lambda g: (0, late(g))),
            pl.BlockSpec((1, d, count), lambda g: (late(g), 0, 0)),
            pl.BlockSpec((1, d, count), lambda g: (late(g), 0, 0)),
        ],
        out_specs=[pl.BlockSpec((1, 4 * d, count), lambda g: (late(g), 0, 0)), whole(users, width // users + 8, 4 * d)],
        scratch=[pltpu.VMEM((d, length), f32)] * 3 + [pltpu.VMEM((4 * d, width), f32), pltpu.VMEM((d, width), f32)],
        flops=1 << 35, moved=16 << 20,
    )
    dw_sum = jnp.sum(exchange(dw, "users"), axis=0)
    dw_all = lax.all_gather(dw_sum, BOTH, axis=0, tiled=False)
    dpre_mine = exchange(dpre, "seq")
    outgoing = call(
        rows_kernel,
        struct((slots, width), bf16),
        (dpre_mine, weight_in, gain_row, fetched, upstream, slot_row),
        name="rows", scratch=[pltpu.VMEM((4 * width, count), bf16)],
        flops=2 * count * width * 4 * width, moved=6 << 20,
    )
    incoming = exchange(outgoing.reshape(devices, SLOTS, width), BOTH).reshape(slots, width)
    tiles = 8
    table_grad = call(
        table_kernel,
        struct((shard_rows, width), f32),
        (asked_row, incoming),
        name="table", grid=(tiles,),
        in_specs=[whole(8, slots), whole(slots, width)],
        out_specs=pl.BlockSpec((shard_rows // tiles, width), lambda g: (g, 0)),
        flops=2 * slots * shard_rows * width, moved=6 << 20,
    )
    rows = width // users
    win_grad, wout_grad = call(
        weights_kernel,
        (struct((width, 4 * width), f32), struct((HEADS, width // d, 8, width), f32)),
        (dw_all.reshape(users, seq, rows + 8, 4 * d),),
        name="weights", grid=(users,),
        in_specs=[pl.BlockSpec((1, seq, rows + 8, 4 * d), lambda g: (g, 0, 0, 0))],
        out_specs=[
            pl.BlockSpec((rows, 4 * width), lambda g: (g, 0)),
            pl.BlockSpec((HEADS, 1, 8, width // 2), lambda g: (0, g // 2, 0, g % 2)),
        ],
        flops=1 << 20, moved=11 << 20,
    )
    return (layer[None], table_grad, win_grad, wout_grad.reshape(width, width))


def solution(mesh):
    in_specs = (
        P(BOTH, None),
        P("users", "seq"),
        P("users", "seq"),
        P(),
        P(),
        P(),
        P(),
        P("users", "seq", None),
    )
    out_specs = (P("users", "seq", None), P(BOTH, None), P(), P())
    return jax.shard_map(body, mesh=mesh, in_specs=in_specs, out_specs=out_specs, check_vma=False)
```

time: 540 us -> 266 us (0.49)
  waiting for transfers between devices: 220 us -> 44.3 us
  matrix products: 160 us -> 1.14 us
  Pallas kernels: 0 us -> 75.3 us
  blocking collectives: 38.3 us -> 112 us
  local copies, waits for them, and re-layouts: 63.6 us -> 6.56 us
  other arithmetic: 28.8 us -> 1.45 us
    dot_general x54 -> x1, matrix products: 160 us -> 1.14 us  [body(): lax.dot_general(gated_mine, weight_out, (((0,), (0,)), ((), ())), preferr...]
    psum x1 -> x0, waiting for transfers between devices: 114 us -> none  [body(): lax.psum((grad_win, grad_wout), ('users', 'seq'))]
    pallas_call x0 -> x9, Pallas kernels: none -> 75.3 us  [call(): pl.pallas_call(kernel, out_shape=out_shape, scratch_shapes=scratch, name=...]
    all_to_all x2 -> x4, blocking collectives: 25.8 us -> 97.9 us  [exchange(): return lax.all_to_all(x, axis, split_axis=0, concat_axis=0, tiled=True)]
    reduce_scatter x1 -> x0, waiting for transfers between devices: 37.7 us -> none  [sent_together(): lax.psum_scatter(both, axis, scatter_dimension=dim, tiled=True)]
    unnamed x43 -> x9, local copies, waits for them, and re-layouts: 22.9 us -> 3.49 us
    all_to_all x2, waiting for transfers between devices: 38.2 us -> 24.6 us  [exchange(): return lax.all_to_all(x, axis, split_axis=0, concat_axis=0, tiled=True)]
    convert_element_type x5 -> x0, local copies, waits for them, and re-layouts: 12.9 us -> none  [the longest x1 4.74 us: body(): join_heads(stacked_k).astype(jnp.bfloat16)]
  transfers between devices with their start and end apart: 6 -> 5, of which waited for: 6 -> 3; matrix products, arithmetic and copies ran while one was open for 7% -> 3% of each run, Pallas kernels for 0% -> 9%
where the time goes in v1:
time: 266 us; the launch traced here: 264 us
  blocking collectives  112 us (42%)
  Pallas kernels  75.3 us (28%)
  waiting for transfers between devices  44.3 us (17%)
  between operations  13.8 us (5%)
  starting transfers between devices  9.54 us (4%)
  local copies, waits for them, and re-layouts  6.56 us (2%)
    all_to_all x4, blocking collectives, exchange(): return lax.all_to_all(x, axis, split_axis=0, concat_axis=0, tiled=True)  97.9 us
    pallas_call x9, Pallas kernels, call(): pl.pallas_call(kernel, out_shape=out_shape, scratch_shapes=scratch, name=...  75.3 us
    all_to_all x2, waiting for transfers between devices, exchange(): return lax.all_to_all(x, axis, split_axis=0, concat_axis=0, tiled=True)  24.6 us
    all_gather x1, waiting for transfers between devices, body(): xin_all = lax.all_gather(xin, 'seq', axis=0, tiled=True)  19 us
    all_gather x1, blocking collectives, body(): stats_all = lax.all_gather(stats, 'seq', axis=0, tiled=False)  14.3 us
    all_to_all x2, starting transfers between devices, exchange(): return lax.all_to_all(x, axis, split_axis=0, concat_axis=0, tiled=True)  9.42 us
  transfers between devices with their start and end apart: 5, of which 3 were waited for; matrix products, arithmetic and copies ran while one was open for 3% of the time, Pallas kernels for 9%

profile of v1, /device:TPU:1, one launch (start us, length us, event | category | flops | bytes accessed | tf_op | source)
XLA Modules:
  0.0 264.4 jit_solution(14368423571145360641)
XLA Ops:
  8.0 1.8 slots.1
  9.8 21.3 %all_to_all.30 = s32[128,1,128]{2,1,0:T(1,128)} all-to-all(s32[128,1,128]{2,1,0:T(1,128)} %bitcast.35), channel_id=1, replica_groups=mesh['users'=16,'seq'=8] {'users','seq'}, dimensions={0} | all-to-all | bytes 131072 | tf_op jit(solution)/shard_map/all_to_all | solution.py:333
  31.1 5.6 %serve.1 = (bf16[1024,512]{1,0:T(8,128)(2,1)}, s32[8,1024]{1,0:T(8,128)}, s32[8,128]{1,0:T(8,128)}) custom-call(s32[128,128]{1,0:T(8,128)} %bitcast.34, bf16[2048,512]{1,0:T(8,128)(2,1)} %table_ref.1), custom_call_target="tpu_custom_call" | custom-call | flops 2147483648 | bytes 4194304 | tf_op jit(solution)/shard_map/serve/pallas_call | solution.py:45
  36.7 24.9 %all_to_all.31 = bf16[128,8,512]{2,1,0:T(8,128)(2,1)} all-to-all(bf16[128,8,512]{2,1,0:T(8,128)(2,1)} %bitcast.31), channel_id=1, replica_groups=mesh['users'=16,'seq'=8] {'users','seq'}, dimensions={0} | all-to-all | bytes 2097152 | tf_op jit(solution)/shard_map/all_to_all | solution.py:333
  61.7 2.8 %arrange.1 = (bf16[384,512]{1,0:T(8,128)(2,1)}, bf16[384,512]{1,0:T(8,128)(2,1)}) custom-call(bf16[1024,512]{1,0:T(8,128)(2,1)} %bitcast.32, s32[384,128]{1,0:T(8,128)} %get-tuple-element.29.col_ref, f32[1,512]{1,0:T(1,128)} %bitcast.37), custom_call_target="tpu_custom_call" | custom-call | flops 402653184 | bytes 2097152 | tf_op jit(solution)/shard_map/arrange/pallas_call | solution.py:45
  64.6 2.5 copy.15
  68.5 1.0 dynamic-slice_bitcast_fusion
  69.5 0.8 pad_maximum_fusion
  70.3 19.0 %all-gather.8.cloned.1.call-done.xin_ref = bf16[3072,512]{1,0:T(8,128)(2,1)} async-done(((bf16[384,512]{1,0:T(8,128)(2,1)}), bf16[3072,512]{1,0:T(8,128)(2,1)}) %all-gather.8.cloned.1.call-update) | async-done | bytes 3145744 | tf_op jit(solution)/shard_map/all_gather | solution.py:380
  89.9 13.1 %forward.1 = (bf16[64,3072]{1,0:T(8,128)(2,1)}, bf16[64,3072]{1,0:T(8,128)(2,1)}, bf16[3072,128]{1,0:T(8,128)(2,1)}, f32[256,3072]{1,0:T(8,128)}, f32[64,3072]{1...) custom-call(bf16[3072,512]{1,0:T(8,128)(2,1)} %all-gather.8.cloned.1.call-done.xin_ref, ...), custom_call_target="tpu_custom_call" | custom-call | flops 8589934592 | bytes 12582912 | tf_op jit(solution)/shard_map/forward/pallas_call | solution.py:45
  103.0 14.3 %all-gather.3.stats_ref = f32[8,4,3072]{2,1,0:T(4,128)} all-gather(f32[1,4,3072]{2,1,0:T(4,128)} %bitcast.36), channel_id=3, replica_groups=mesh['users'=16,'seq'=8] {'seq'}, dimensions={0}, use_global_device_ids=true | all-gather | bytes 442368 | tf_op jit(solution)/shard_map/all_gather | solution.py:404
  117.4 6.2 %middle.1 = (bf16[8,64,384]{2,1,0:T(8,128)(2,1)}, bf16[64,3072]{1,0:T(8,128)(2,1)}, bf16[8,64,384]{2,1,0:T(8,128)(2,1)}) custom-call(f32[8,4,3072]{2,1,0:T(4,128)} %all-gather.3.stats_ref, f32[64,3072]{1,0:T(8,128)} %get-tuple-element.34.mixed_ref, f32[64,3072]{1,0:T(8,128)} %get-tuple-element.35.dg_ref, f32[64,3072]{1,0:T(8,128)} %get-tuple-element.36.u_ref, ...), custom_call_target="tpu_custom_call" | custom-call | flops 16777216 | bytes 5242880 | tf_op jit(solution)/shard_map/middle/pallas_call | solution.py:45
  123.6 22.2 %backward.1 = (bf16[8,256,384]{2,1,0:T(8,128)(2,1)}, f32[16,40,256]{2,1,0:T(8,128)}) custom-call(bf16[64,3072]{1,0:T(8,128)(2,1)} %get-tuple-element.40.q_ref, bf16[64,3072]{1,0:T(8,128)(2,1)} %get-tuple-element.41.k_ref, bf16[3072,128]{1,0:T(8,128)(2,1)} %get-tuple-element.42.vk_ref, bf16[64,3072]{1,0:T(8,128)(2,1)} %get-tuple-element.43.dm_ref, ...), custom_call_target="tpu_custom_call" | custom-call | flops 34359738368 | bytes 16777216 | tf_op jit(solution)/shard_map/backward/pallas_call | solution.py:45
  145.7 25.1 %all_to_all.32 = f32[16,40,256]{2,1,0:T(8,128)S(1)} all-to-all(f32[16,40,256]{2,1,0:T(8,128)} %get-tuple-element.47), channel_id=1, replica_groups=mesh['users'=16,'seq'=8] {'users'}, dimensions={0} | all-to-all | bytes 1310720 | tf_op jit(solution)/shard_map/all_to_all | solution.py:333
  171.6 26.6 %all_to_all.33.dpre_ref = bf16[8,256,384]{2,1,0:T(8,128)(2,1)} all-to-all(bf16[8,256,384]{2,1,0:T(8,128)(2,1)} %get-tuple-element.45), channel_id=1, replica_groups=mesh['users'=16,'seq'=8] {'seq'}, dimensions={0} | all-to-all | bytes 3145728 | tf_op jit(solution)/shard_map/all_to_all | solution.py:333
  198.1 4.4 %all-to-all-start.2 = ((bf16[8,64,384]{2,1,0:T(8,128)(2,1)}), bf16[8,64,384]{2,1,0:T(8,128)(2,1)S(1)}, u32[]{:S(2)}, u32[]{:S(2)}) async-start(bf16[8,64,384]{2,1,0:T(8,128)(2,1)} %get-tuple-element.38.gated_ref), calls=%async_computation.2 | async-start | bytes 786432 | tf_op jit(solution)/shard_map/all_to_all | solution.py:333
  202.5 5.7 %rows.1 = bf16[1024,512]{1,0:T(8,128)(2,1)} custom-call(bf16[8,256,384]{2,1,0:T(8,128)(2,1)} %all_to_all.33.dpre_ref, bf16[512,2048]{1,0:T(8,128)(2,1)} %win_ref.1, f32[1,512]{1,0:T(1,128)} %bitcast.38, bf16[384,512]{1,0:T(8,128)(2,1)} %get-tuple-element.30.fetched_ref, bf16[384,512]{1,0:T(8,128)(2,1)} %bitcast.28, s32[8,384]{1,0:T(8,128)} %get-tuple-element.46.row_ref), custom_call_target="tpu_custom_call" | custom-call | flops 805306368 | bytes 6291456 | tf_op jit(solution)/shard_map/rows/pallas_call | solution.py:45
  208.2 2.7 %all-to-all-done.2 = bf16[8,64,384]{2,1,0:T(8,128)(2,1)S(1)} async-done(((bf16[8,64,384]{2,1,0:T(8,128)(2,1)}), bf16[8,64,384]{2,1,0:T(8,128)(2,1)S(1)}, u32[]{:S(2)}, u32[]{:S(2)}) %all-to-all-start.2) | async-done | bytes 393248 | tf_op jit(solution)/shard_map/all_to_all | solution.py:333
  210.9 5.0 %all-to-all-start.4 = ((bf16[128,8,512]{2,1,0:T(8,128)(2,1)}), bf16[128,8,512]{2,1,0:T(8,128)(2,1)S(1)}, u32[]{:S(2)}, u32[]{:S(2)}) async-start(bf16[128,8,512]{2,1,0:T(8,128)(2,1)} %bitcast.26), calls=%async_computation.4 | async-start | bytes 2097152 | tf_op jit(solution)/shard_map/all_to_all | solution.py:333
  215.9 1.1 fusion.1
  217.1 22.0 %all-to-all-done.4 = bf16[128,8,512]{2,1,0:T(8,128)(2,1)S(1)} async-done(((bf16[128,8,512]{2,1,0:T(8,128)(2,1)}), bf16[128,8,512]{2,1,0:T(8,128)(2,1)S(1)}, u32[]{:S(2)}, u32[]{:S(2)}) %all-to-all-start.4) | async-done | bytes 1048608 | tf_op jit(solution)/shard_map/all_to_all | solution.py:333
  239.0 1.0 copy-done.3
  240.0 6.7 %table.1 = f32[2048,512]{1,0:T(8,128)} custom-call(s32[8,1024]{1,0:T(8,128)} %get-tuple-element.39.row_ref, bf16[1024,512]{1,0:T(8,128)(2,1)} %bitcast.30), custom_call_target="tpu_custom_call" | custom-call | flops 2147483648 | bytes 6291456 | tf_op jit(solution)/shard_map/table/pallas_call | solution.py:45
  246.7 11.2 %weights.1 = (f32[512,2048]{1,0:T(8,128)}, f32[8,8,8,512]{3,2,1,0:T(8,128)}) custom-call(f32[16,8,40,256]{3,2,1,0:T(8,128)} %bitcast.25), custom_call_target="tpu_custom_call" | custom-call | flops 1048576 | bytes 11534336 | tf_op jit(solution)/shard_map/weights/pallas_call | solution.py:45
  (20 shorter events, 3.6 us)
Async XLA Ops:
  7.2 60.7 %copy-start = (bf16[512,512]{1,0:T(8,128)(2,1)S(1)}, bf16[512,512]{1,0:T(8,128)(2,1)}, u32[]{:S(2)}) copy-start(bf16[512,512]{1,0:T(8,128)(2,1)} %param.12) | copy-start | bytes 1572868
  7.2 63.1 %all-gather.10.cloned.1.call-start = ((), (), s32[]{:S(2)}) async-start(), calls=%async_computation.7 | async-start | bytes 3538944 | tf_op jit(solution)/shard_map/all_gather | solution.py:352
  7.9 81.3 %all-gather.8.cloned.1.call-start = ((), (), s32[]{:S(2)}) async-start(), calls=%async_computation.6 | async-start | bytes 3538944 | tf_op jit(solution)/shard_map/all_gather | solution.py:380
  36.7 27.8 %copy-start.1 = (bf16[512,2048]{1,0:T(8,128)(2,1)S(1)}, bf16[512,2048]{1,0:T(8,128)(2,1)}, u32[]{:S(2)}) copy-start(bf16[512,2048]{1,0:T(8,128)(2,1)} %win_ref.1) | copy-start | bytes 6291460
  64.5 182.1 %all-gather.12.cloned.1.call-start = ((), (), s32[]{:S(2)}) async-start(), calls=%async_computation.8 | async-start | bytes 5283840 | tf_op jit(solution)/shard_map/all_gather | solution.py:443
  198.1 12.8 %all-to-all-start.2 = ((bf16[8,64,384]{2,1,0:T(8,128)(2,1)}), bf16[8,64,384]{2,1,0:T(8,128)(2,1)S(1)}, u32[]{:S(2)}, u32[]{:S(2)}) async-start(bf16[8,64,384]{2,1,0:T(8,128)(2,1)} %get-tuple-element.38.gated_ref), calls=%async_computation.2 | async-start | bytes 786432 | tf_op jit(solution)/shard_map/all_to_all | solution.py:333
  202.5 13.4 %copy-start.2 = (bf16[384,512]{1,0:T(8,128)(2,1)S(1)}, bf16[384,512]{1,0:T(8,128)(2,1)}, u32[]{:S(2)}) copy-start(bf16[384,512]{1,0:T(8,128)(2,1)} %get-tuple-element.30.fetched_ref) | copy-start | bytes 1179652
  210.9 28.1 %all-to-all-start.4 = ((bf16[128,8,512]{2,1,0:T(8,128)(2,1)}), bf16[128,8,512]{2,1,0:T(8,128)(2,1)S(1)}, u32[]{:S(2)}, u32[]{:S(2)}) async-start(bf16[128,8,512]{2,1,0:T(8,128)(2,1)} %bitcast.26), calls=%async_computation.4 | async-start | bytes 2097152 | tf_op jit(solution)/shard_map/all_to_all | solution.py:333
  239.0 1.0 copy-start.3
Sparse Core Ops, SparseCore 0:
  9.7 32.1 all-gather.9
  64.6 24.5 all-gather.7
  171.7 72.0 all-gather.11

commit v2 on v1

--- a/solution.py
+++ b/solution.py
@@ -5,6 +5,7 @@
 from jax.experimental import pallas as pl
 from jax.experimental.pallas import tpu as pltpu
 from jax.sharding import PartitionSpec as P
+
 
 HEADS = 8
 HEAD_DIM = 64
@@ -32,7 +33,7 @@
     return lax.dot_general(a, b, (((1,), (1,)), ((), ())), preferred_element_type=f32)
 
 
-def call(kernel, out_shape, args, *, name, grid=None, in_specs=None, out_specs=None, scratch=(), flops=0, moved=0):
+def call(kernel, out_shape, args, *, grid=None, in_specs=None, out_specs=None, scratch=(), flops=0, moved=0):
     params = dict(vmem_limit_bytes=60 * 1024 * 1024)
     extra = {}
     if grid is not None:
@@ -46,7 +47,6 @@
         kernel,
         out_shape=out_shape,
         scratch_shapes=scratch,
-        name=name,
         compiler_params=pltpu.CompilerParams(**params),
         cost_estimate=pl.CostEstimate(flops=flops, bytes_accessed=moved, transcendentals=0),
         **extra,
@@ -105,7 +105,8 @@
         group = lax.axis_index("users")
         mine = lax.div(iota((devices, lanes), 0), SLOTS) == group
         bounds = jnp.sum(jnp.where(mine, asked, 0.0), axis=0, keepdims=True)
-        bounds_ref[...] = jnp.broadcast_to(bounds, bounds_ref.shape).astype(i32)
+        bounds = jnp.broadcast_to(bounds, bounds_ref.shape).astype(i32)
+        bounds_ref[...] = jnp.where(iota(bounds_ref.shape, 1) == SLOTS, lax.axis_index("seq"), bounds)
 
     column = col_ref[pl.ds(pl.multiple_of(step * block, block), block), :].astype(i32)
     parts = []
@@ -188,9 +189,8 @@
     stats_ref[3:4, :] = jnp.sum(e * centred, axis=0, keepdims=True)
 
 
-def middle_kernel(stats_ref, mixed_ref, dg_ref, u_ref, slope_ref, gain_ref, gated_ref, dm_ref, dpre_ref):
+def middle(stats, mixed, dg, u, gain):
     width = HEADS * HEAD_DIM
-    stats = stats_ref[...]
     means = [stats[h, 0:1] for h in range(HEADS)]
     mean = functools.reduce(jnp.add, means) * (1.0 / HEADS)
     var, m_e, m_em = 0.0, 0.0, 0.0
@@ -202,24 +202,23 @@
     inverse = lax.rsqrt(var * (1.0 / width) + EPSILON)
     m_e = m_e * (1.0 / width)
     m_eh = m_em * inverse * (1.0 / width)
-    gain = gain_ref[:, :1]
-    hat = (mixed_ref[...] - mean) * inverse
+    hat = (mixed - mean) * inverse
     scaled = hat * gain
-    u = u_ref[...]
-    dg = dg_ref[...]
-    gated_ref[0] = (scaled * u).astype(bf16)
     e = dg * u * gain
-    dm = (inverse * (e - m_e - hat * m_eh)).astype(bf16)
-    dm_ref[...] = (dm.astype(f32) * 0.0625).astype(bf16)
-    dpre_ref[0] = (dg * scaled * slope_ref[...]).astype(bf16)
+    up = (inverse * (e - m_e - hat * m_eh)).astype(bf16)
+    return (scaled * u).astype(bf16), (up.astype(f32) * 0.0625).astype(bf16), dg * scaled
 
 
 def backward_kernel(
-    steps, q_ref, k_ref, vk_ref, dm_ref, bounds_ref, xin_ref, cot_ref, slope_ref, gated_ref, dpu_ref,
-    dpre_ref, dw_ref, dq_all, dk_all, dv_all, win_acc, wout_acc,
+    steps, bounds_ref, q_ref, k_ref, vk_ref, stats_ref, mixed_ref, dg_ref, u_ref, gain_ref, xin_ref, cot_ref, slope_ref,
+    *rest,
 ):
+    outs, (dw_ref, k_all, vk_all, gated_all, du_all, dq_all, dk_all, dv_all, win_acc, wout_acc, sent, sems) = (
+        rest[:HEADS],
+        rest[HEADS:],
+    )
     g = pl.program_id(0)
-    one, two = bounds_ref[0, CAP], bounds_ref[0, CAP + 1]
+    one, two, me = bounds_ref[0, CAP], bounds_ref[0, CAP + 1], bounds_ref[0, SLOTS]
     d = HEAD_DIM
 
     @pl.when(g == 0)
@@ -234,14 +233,18 @@
     def _():
         here = pl.ds(pl.multiple_of(g * BLOCK, BLOCK), BLOCK)
         blank = jnp.zeros((d, BLOCK), bf16)
-        query = q_ref[:, here]
-        up = dm_ref[:, here]
+        gated, up, du = middle(stats_ref[...], mixed_ref[...], dg_ref[...], u_ref[...], gain_ref[:, :1])
+        gated_all[:, here] = gated
+        du_all[:, here] = du
+        k_all[:, here] = k_ref[...]
+        vk_all[here, :] = vk_ref[...]
+        query = q_ref[...]
         query2 = jnp.concatenate([blank, query], axis=0)
         up2 = jnp.concatenate([up, blank], axis=0)
 
         def pair(j, carry):
             there = pl.ds(pl.multiple_of(j * BLOCK, BLOCK), BLOCK)
-            vk = vk_ref[there, :]
+            vk = vk_all[there, :]
             half = mm(vk, query2)
             upper = mm(vk, up2)
             tanh = jnp.tanh(half)
@@ -253,7 +256,7 @@
             dscores = jnp.where(seen, dscores, 0.0).astype(bf16)
             dv_all[:, there] += mm_nt(up, weights)
             dk_all[:, there] += mm_nt(query, dscores)
-            dq_all[:, here] += mm(k_ref[:, there], dscores)
+            dq_all[:, here] += mm(k_all[:, there], dscores)
             return carry
 
         first = lax.div(seg_start(g * BLOCK, one, two), BLOCK)
@@ -263,20 +266,28 @@
     def _():
         s = g - steps
         count = xin_ref.shape[0]
-        here = pl.ds(pl.multiple_of(s * count, count), count)
+        here = pl.ds(pl.multiple_of(lax.rem(me + s, HEADS) * count, 128), count)
         slope = slope_ref[...]
+        gated = gated_all[:, here]
         dpre = jnp.concatenate(
             [
-                dpu_ref[0],
+                (du_all[:, here] * slope[:d]).astype(bf16),
                 (dq_all[:, here] * slope[d : 2 * d]).astype(bf16),
                 (dv_all[:, here] * 16.0 * slope[2 * d : 3 * d]).astype(bf16),
                 (dk_all[:, here] * 16.0 * slope[3 * d :]).astype(bf16),
             ],
             axis=0,
         )
-        dpre_ref[0] = dpre
+        sent[s, : 4 * d, :] = dpre
+        sent[s, 4 * d :, :] = gated
+        for at in range(HEADS):
+
+            @pl.when(s == at)
+            def _():
+                pltpu.make_async_copy(sent.at[at], outs[at], sems.at[at]).start()
+
         win_acc[...] += mm(dpre, xin_ref[...])
-        wout_acc[...] += mm(gated_ref[0], cot_ref[...])
+        wout_acc[...] += mm(gated, cot_ref[...])
 
     @pl.when(g == pl.num_programs(0) - 1)
     def _():
@@ -286,14 +297,21 @@
         for p in range(parts):
             dw_ref[p, :rows, :] = turned[p * rows : (p + 1) * rows]
             dw_ref[p, rows:, :] = wout_acc[8 * (p // 2) : 8 * (p // 2) + 8, 256 * (p % 2) : 256 * (p % 2) + 256]
-
-
-def rows_kernel(dpre_ref, win_ref, gain_ref, fetched_ref, cot_ref, row_ref, out_ref, whole):
+        for at in range(HEADS):
+            pltpu.make_async_copy(sent.at[at], outs[at], sems.at[at]).wait()
+
+
+def rows_kernel(*refs):
+    got = refs[:HEADS]
+    win_ref, gain_ref, fetched_ref, cot_ref, row_ref, out_ref, gated_ref, whole = refs[HEADS:]
     d = HEAD_DIM
     width = fetched_ref.shape[1]
-    for h in range(HEADS):
+    me = lax.axis_index("seq")
+    for s in range(HEADS):
+        at_head = pl.multiple_of(lax.rem(me + HEADS - s, HEADS) * d, d)
         for at, block in enumerate(ORDER):
-            whole[block * width + h * d : block * width + (h + 1) * d, :] = dpre_ref[h, at * d : (at + 1) * d, :]
+            whole[pl.ds(block * width + at_head, d), :] = got[s][at * d : (at + 1) * d, :]
+        gated_ref[pl.ds(at_head, d), :] = got[s][4 * d :, :]
     dxin = jnp.transpose(mm(win_ref[...], whole[...]))
     normed, inverse = normalize(fetched_ref[...].astype(f32))
     f = dxin * gain_ref[...]
@@ -317,16 +335,19 @@
 
 def weights_kernel(got_ref, win_ref, wout_ref):
     d = HEAD_DIM
-    rows, columns = win_ref.shape
-    width = columns // 4
-    for at, block in enumerate(ORDER):
-        for pair in range(HEADS // 2):
-            left = got_ref[0, 2 * pair, :rows, at * d : (at + 1) * d]
-            right = got_ref[0, 2 * pair + 1, :rows, at * d : (at + 1) * d]
-            start = block * width + pair * 2 * d
-            win_ref[:, start : start + 2 * d] = jnp.concatenate([left, right], axis=1)
-    for h in range(HEADS):
-        wout_ref[h, 0] = got_ref[0, h, rows:, :]
+    parts = got_ref.shape[1]
+    rows = win_ref.shape[0] // parts
+    width = win_ref.shape[1] // 4
+    for p in range(parts):
+        here = slice(p * rows, (p + 1) * rows)
+        for at, block in enumerate(ORDER):
+            for pair in range(HEADS // 2):
+                left = got_ref[2 * pair, p, :rows, at * d : (at + 1) * d].astype(f32)
+                right = got_ref[2 * pair + 1, p, :rows, at * d : (at + 1) * d].astype(f32)
+                start = block * width + pair * 2 * d
+                win_ref[here, start : start + 2 * d] = jnp.concatenate([left, right], axis=1)
+        for h in range(HEADS):
+            wout_ref[h, p // 2, :, 256 * (p % 2) : 256 * (p % 2) + 256] = got_ref[h, p, rows:, :].astype(f32)
 
 
 def exchange(x, axis):
@@ -337,7 +358,7 @@
     return jax.ShapeDtypeStruct(shape, dtype)
 
 
-def body(item_table, item_ids, segment_ids, weight_in, weight_out, gain_in, gain_mid, cotangent):
+def layer_step(item_table, item_ids, segment_ids, weight_in, weight_out, gain_in, gain_mid, cotangent):
     shard_rows, width = item_table.shape
     count = item_ids.shape[1]
     users, seq = lax.axis_size("users"), lax.axis_size("seq")
@@ -354,7 +375,7 @@
         functools.partial(slots_kernel, shard_rows),
         (struct((devices, 128), i32), struct((8, count), i32), struct((count, 128), i32)),
         (item_ids, segment_ids),
-        name="slots", flops=2 * devices * count * count, moved=1 << 19,
+        flops=2 * devices * count * count, moved=1 << 19,
     )
     asked = exchange(wanted.reshape(devices, 1, 128), BOTH).reshape(devices, 128)
     steps = 4
@@ -364,7 +385,7 @@
         serve_kernel,
         (struct((slots, width), bf16), struct((8, slots), i32), struct((8, 128), i32)),
         (asked, item_table),
-        name="serve", grid=(steps,),
+        grid=(steps,),
         in_specs=[whole(devices, 128), whole(shard_rows, width)],
         out_specs=[pl.BlockSpec((slots // steps, width), lambda g: (g, 0)), whole(8, slots), whole(8, 128)],
         scratch=[pltpu.VMEM((slots, 128), f32)],
@@ -375,7 +396,7 @@
         arrange_kernel,
         (struct((count, width), bf16), struct((count, width), bf16)),
         (got, slot_col, gain_row),
-        name="arrange", flops=2 * count * slots * width, moved=2 << 20,
+        flops=2 * count * slots * width, moved=2 << 20,
     )
     xin_all = lax.all_gather(xin, "seq", axis=0, tiled=True)
 
@@ -395,7 +416,7 @@
             struct((d, length), f32), struct((4, length), f32),
         ),
         (xin_all, cot_all, win_t, wout_h, gain_h, bounds),
-        name="forward", grid=(blocks,),
+        grid=(blocks,),
         in_specs=[rowed(width), rowed(width), whole(4 * d, width), whole(d, width), whole(d, 128), smem],
         out_specs=[lane(d), lane(d), rowed(2 * d), lane(4 * d), lane(d), lane(d), lane(d), lane(4)],
         scratch=[pltpu.VMEM((2 * d, BLOCK), bf16), pltpu.VMEM((d, length), bf16), pltpu.VMEM((length, 2 * d), bf16)],
@@ -403,75 +424,83 @@
     )
     stats_all = lax.all_gather(stats, "seq", axis=0, tiled=False)
 
-    part = lambda rows: pl.BlockSpec((rows, count), lambda g: (0, g))
-    gated, dm, dpre_u = call(
-        middle_kernel,
-        (struct((seq, d, count), bf16), struct((d, length), bf16), struct((seq, d, count), bf16)),
-        (stats_all, mixed, dg, u, slope, gain_h),
-        name="middle", grid=(seq,),
-        in_specs=[pl.BlockSpec((seq, 4, count), lambda g: (0, 0, g)), part(d), part(d), part(d), part(d), whole(d, 128)],
-        out_specs=[
-            pl.BlockSpec((1, d, count), lambda g: (g, 0, 0)), part(d), pl.BlockSpec((1, d, count), lambda g: (g, 0, 0)),
-        ],
-        flops=1 << 24, moved=5 << 20,
-    )
-    gated_mine = exchange(gated, "seq").reshape(width, count)
+    late = lambda g, b: lax.rem(b[0, SLOTS] + jnp.maximum(g - blocks, 0), seq)
+    early = lambda g: jnp.minimum(g, blocks - 1)
+    fixed = lambda *shape: pl.BlockSpec(shape, lambda g, b: (0,) * len(shape))
+    lanes = lambda rows: pl.BlockSpec((rows, BLOCK), lambda g, b: (0, early(g)))
+    rows = width // users
+    result = pl.pallas_call(
+        functools.partial(backward_kernel, blocks),
+        out_shape=[struct((5 * d, count), bf16)] * HEADS + [struct((users, rows + 8, 4 * d), f32)],
+        grid_spec=pltpu.PrefetchScalarGridSpec(
+            num_scalar_prefetch=1,
+            grid=(blocks + seq,),
+            in_specs=[
+                lanes(d), lanes(d), pl.BlockSpec((BLOCK, 2 * d), lambda g, b: (early(g), 0)),
+                pl.BlockSpec((seq, 4, BLOCK), lambda g, b: (0, 0, early(g))),
+                lanes(d), lanes(d), lanes(d), fixed(d, 128),
+                pl.BlockSpec((count, width), lambda g, b: (late(g, b), 0)),
+                pl.BlockSpec((count, width), lambda g, b: (late(g, b), 0)),
+                pl.BlockSpec((4 * d, count), lambda g, b: (0, late(g, b))),
+            ],
+            out_specs=[pl.BlockSpec(memory_space=pl.ANY)] * HEADS + [fixed(users, rows + 8, 4 * d)],
+            scratch_shapes=[
+                pltpu.VMEM((d, length), bf16), pltpu.VMEM((length, 2 * d), bf16), pltpu.VMEM((d, length), bf16),
+                pltpu.VMEM((d, length), f32), pltpu.VMEM((d, length), f32), pltpu.VMEM((d, length), f32),
+                pltpu.VMEM((d, length), f32), pltpu.VMEM((4 * d, width), f32), pltpu.VMEM((d, width), f32),
+                pltpu.VMEM((HEADS, 5 * d, count), bf16), pltpu.SemaphoreType.DMA((HEADS,)),
+            ],
+        ),
+        name="backward",
+        compiler_params=pltpu.CompilerParams(
+            vmem_limit_bytes=60 * 1024 * 1024, dimension_semantics=("arbitrary",)
+        ),
+        cost_estimate=pl.CostEstimate(flops=1 << 35, bytes_accessed=16 << 20, transcendentals=0),
+    )(bounds, q_t, k_t, vk, stats_all, mixed, dg, u, gain_h, xin_all, cot_all, slope)
+    dw = result[HEADS]
+    pieces = [result[0]]
+    for s in range(1, seq):
+        pieces.append(lax.ppermute(result[s], "seq", [(i, (i + s) % seq) for i in range(seq)]))
+    dw_got = exchange(dw, "users")
+    dw_sum = jnp.sum(dw_got, axis=0).astype(bf16)
+    dw_wide = jnp.broadcast_to(dw_sum[None], (users, rows + 8, 4 * d))
+    dw_head = exchange(dw_wide, "users")
+    dw_all = lax.all_gather(dw_head, "seq", axis=0, tiled=False)
+    outgoing, gated_mine = call(
+        rows_kernel,
+        (struct((slots, width), bf16), struct((width, count), bf16)),
+        (*pieces, weight_in, gain_row, fetched, upstream, slot_row),
+        scratch=[pltpu.VMEM((4 * width, count), bf16)],
+        flops=2 * count * width * 4 * width, moved=6 << 20,
+    )
     layer = (
         fetched.astype(f32)
         + lax.dot_general(gated_mine, weight_out, (((0,), (0,)), ((), ())), preferred_element_type=f32)
     ).astype(bf16)
-
-    late = lambda g: jnp.maximum(g - blocks, 0)
-    dpre, dw = call(
-        functools.partial(backward_kernel, blocks),
-        (struct((seq, 4 * d, count), bf16), struct((users, width // users + 8, 4 * d), f32)),
-        (q_t, k_t, vk, dm, bounds, xin_all, cot_all, slope, gated, dpre_u),
-        name="backward", grid=(blocks + seq,),
-        in_specs=[
-            whole(d, length), whole(d, length), whole(length, 2 * d), whole(d, length), smem,
-            pl.BlockSpec((count, width), lambda g: (late(g), 0)),
-            pl.BlockSpec((count, width), lambda g: (late(g), 0)),
-            pl.BlockSpec((4 * d, count), lambda g: (0, late(g))),
-            pl.BlockSpec((1, d, count), lambda g: (late(g), 0, 0)),
-            pl.BlockSpec((1, d, count), lambda g: (late(g), 0, 0)),
-        ],
-        out_specs=[pl.BlockSpec((1, 4 * d, count), lambda g: (late(g), 0, 0)), whole(users, width // users + 8, 4 * d)],
-        scratch=[pltpu.VMEM((d, length), f32)] * 3 + [pltpu.VMEM((4 * d, width), f32), pltpu.VMEM((d, width), f32)],
-        flops=1 << 35, moved=16 << 20,
-    )
-    dw_sum = jnp.sum(exchange(dw, "users"), axis=0)
-    dw_all = lax.all_gather(dw_sum, BOTH, axis=0, tiled=False)
-    dpre_mine = exchange(dpre, "seq")
-    outgoing = call(
-        rows_kernel,
-        struct((slots, width), bf16),
-        (dpre_mine, weight_in, gain_row, fetched, upstream, slot_row),
-        name="rows", scratch=[pltpu.VMEM((4 * width, count), bf16)],
-        flops=2 * count * width * 4 * width, moved=6 << 20,
-    )
-    incoming = exchange(outgoing.reshape(devices, SLOTS, width), BOTH).reshape(slots, width)
+    incoming = exchange(outgoing.reshape(devices, SLOTS, width), BOTH)
+    incoming = incoming.reshape(slots, width)
     tiles = 8
     table_grad = call(
         table_kernel,
         struct((shard_rows, width), f32),
         (asked_row, incoming),
-        name="table", grid=(tiles,),
+        grid=(tiles,),
         in_specs=[whole(8, slots), whole(slots, width)],
         out_specs=pl.BlockSpec((shard_rows // tiles, width), lambda g: (g, 0)),
         flops=2 * slots * shard_rows * width, moved=6 << 20,
     )
-    rows = width // users
+    group = 4
     win_grad, wout_grad = call(
         weights_kernel,
         (struct((width, 4 * width), f32), struct((HEADS, width // d, 8, width), f32)),
-        (dw_all.reshape(users, seq, rows + 8, 4 * d),),
-        name="weights", grid=(users,),
-        in_specs=[pl.BlockSpec((1, seq, rows + 8, 4 * d), lambda g: (g, 0, 0, 0))],
+        (dw_all,),
+        grid=(users // group,),
+        in_specs=[pl.BlockSpec((seq, group, rows + 8, 4 * d), lambda g: (0, g, 0, 0))],
         out_specs=[
-            pl.BlockSpec((rows, 4 * width), lambda g: (g, 0)),
-            pl.BlockSpec((HEADS, 1, 8, width // 2), lambda g: (0, g // 2, 0, g % 2)),
+            pl.BlockSpec((group * rows, 4 * width), lambda g: (g, 0)),
+            pl.BlockSpec((HEADS, group // 2, 8, width), lambda g: (0, g, 0, 0)),
         ],
-        flops=1 << 20, moved=11 << 20,
+        flops=1 << 20, moved=8 << 20,
     )
     return (layer[None], table_grad, win_grad, wout_grad.reshape(width, width))
 
@@ -488,4 +517,4 @@
         P("users", "seq", None),
     )
     out_specs = (P("users", "seq", None), P(BOTH, None), P(), P())
-    return jax.shard_map(body, mesh=mesh, in_specs=in_specs, out_specs=out_specs, check_vma=False)
+    return jax.shard_map(layer_step, mesh=mesh, in_specs=in_specs, out_specs=out_specs, check_vma=False)

time: 266 us -> 266 us (level)
  waiting for transfers between devices: 44.3 us -> 65.3 us
  blocking collectives: 112 us -> 95.9 us
  Pallas kernels: 75.3 us -> 64.4 us
  starting transfers between devices: 9.54 us -> 14.8 us
    ppermute x0 -> x7, waiting for transfers between devices: none -> 28.8 us  [layer_step(): lax.ppermute(result[s], 'seq', [(i, (i + s) % seq) for i in range(seq)])]
    all_to_all x4, blocking collectives: 97.9 us -> 81.6 us  [exchange(): return lax.all_to_all(x, axis, split_axis=0, concat_axis=0, tiled=True)]
    pallas_call x9 -> x8, Pallas kernels: 75.3 us -> 64.4 us  [the longest x7 40.8 us: call(): pl.pallas_call(kernel, out_shape=out_shape, scratch_shapes=scratch, compi...]
    ppermute x0 -> x7, starting transfers between devices: none -> 9.99 us  [layer_step(): lax.ppermute(result[s], 'seq', [(i, (i + s) % seq) for i in range(seq)])]
    all_to_all x2 -> x1, waiting for transfers between devices: 24.6 us -> 16.9 us  [exchange(): return lax.all_to_all(x, axis, split_axis=0, concat_axis=0, tiled=True)]
    all_to_all x2 -> x1, starting transfers between devices: 9.42 us -> 4.74 us  [exchange(): return lax.all_to_all(x, axis, split_axis=0, concat_axis=0, tiled=True)]
  transfers between devices with their start and end apart: 5 -> 11, of which waited for: 3 -> 8; matrix products, arithmetic and copies ran while one was open for 3% -> 3% of each run, Pallas kernels for 9% -> 9%
where the time goes in v2:
time: 266 us; the launch traced here: 265 us
  blocking collectives  95.9 us (36%)
  waiting for transfers between devices  65.3 us (25%)
  Pallas kernels  64.4 us (24%)
  starting transfers between devices  14.8 us (6%)
  between operations  13.9 us (5%)
  local copies, waits for them, and re-layouts  7.28 us (3%)
    all_to_all x4, blocking collectives, exchange(): return lax.all_to_all(x, axis, split_axis=0, concat_axis=0, tiled=True)  81.6 us
    pallas_call x7, Pallas kernels, call(): pl.pallas_call(kernel, out_shape=out_shape, scratch_shapes=scratch, compi...  40.8 us
    ppermute x7, waiting for transfers between devices, layer_step(): lax.ppermute(result[s], 'seq', [(i, (i + s) % seq) for i in range(seq)])  28.8 us
    pallas_call x1, Pallas kernels, layer_step(): pl.pallas_call(functools.partial(backward_kernel, blocks), out_shape=[str...  23.6 us
    all_gather x1, waiting for transfers between devices, layer_step(): xin_all = lax.all_gather(xin, 'seq', axis=0, tiled=True)  19 us
    all_to_all x1, waiting for transfers between devices, exchange(): return lax.all_to_all(x, axis, split_axis=0, concat_axis=0, tiled=True)  16.9 us
    all_gather x1, blocking collectives, layer_step(): stats_all = lax.all_gather(stats, 'seq', axis=0, tiled=False)  14.4 us
    ppermute x7, starting transfers between devices, layer_step(): lax.ppermute(result[s], 'seq', [(i, (i + s) % seq) for i in range(seq)])  9.99 us
  transfers between devices with their start and end apart: 11, of which 8 were waited for; matrix products, arithmetic and copies ran while one was open for 3% of the time, Pallas kernels for 9%

profile of v2, /device:TPU:1, one launch (start us, length us, event | category | flops | bytes accessed | tf_op | source)
XLA Modules:
  0.0 264.7 jit_solution(15175551802377277923)
XLA Ops:
  8.0 1.8 shard_map.111
  9.8 21.3 %all_to_all.25 = s32[128,1,128]{2,1,0:T(1,128)} all-to-all(s32[128,1,128]{2,1,0:T(1,128)} %bitcast.33), channel_id=1, replica_groups=mesh['users'=16,'seq'=8] {'users','seq'}, dimensions={0} | all-to-all | bytes 131072 | tf_op jit(solution)/shard_map/all_to_all | solution.py:354
  31.1 5.6 %shard_map.112 = (bf16[1024,512]{1,0:T(8,128)(2,1)}, s32[8,1024]{1,0:T(8,128)}, s32[8,128]{1,0:T(8,128)}) custom-call(s32[128,128]{1,0:T(8,128)} %bitcast.32, bf16[2048,512]{1,0:T(8,128)(2,1)} %table_ref.1), custom_call_target="tpu_custom_call" | custom-call | flops 2147483648 | bytes 4194304 | tf_op jit(solution)/shard_map/pallas_call | solution.py:46
  36.7 24.9 %all_to_all.26 = bf16[128,8,512]{2,1,0:T(8,128)(2,1)} all-to-all(bf16[128,8,512]{2,1,0:T(8,128)(2,1)} %bitcast.29), channel_id=1, replica_groups=mesh['users'=16,'seq'=8] {'users','seq'}, dimensions={0} | all-to-all | bytes 2097152 | tf_op jit(solution)/shard_map/all_to_all | solution.py:354
  61.6 2.8 %shard_map.113 = (bf16[384,512]{1,0:T(8,128)(2,1)}, bf16[384,512]{1,0:T(8,128)(2,1)}) custom-call(bf16[1024,512]{1,0:T(8,128)(2,1)} %bitcast.30, s32[384,128]{1,0:T(8,128)} %get-tuple-element.35.col_ref, f32[1,512]{1,0:T(1,128)} %bitcast.35), custom_call_target="tpu_custom_call" | custom-call | flops 402653184 | bytes 2097152 | tf_op jit(solution)/shard_map/pallas_call | solution.py:46
  64.6 2.5 copy.15
  70.2 19.0 %all-gather.8.cloned.1.call-done.xin_ref = bf16[3072,512]{1,0:T(8,128)(2,1)} async-done(((bf16[384,512]{1,0:T(8,128)(2,1)}), bf16[3072,512]{1,0:T(8,128)(2,1)}) %all-gather.8.cloned.1.call-update) | async-done | bytes 3145744 | tf_op jit(solution)/shard_map/all_gather | solution.py:401
  89.9 13.1 %shard_map.114 = (bf16[64,3072]{1,0:T(8,128)(2,1)}, bf16[64,3072]{1,0:T(8,128)(2,1)}, bf16[3072,128]{1,0:T(8,128)(2,1)}, f32[256,3072]{1,0:T(8,128)}, f32[64,307...) custom-call(bf16[3072,512]{1,0:T(8,128)(2,1)} %all-gather.8.cloned.1.call-done.xin_ref, ...), custom_call_target="tpu_custom_call" | custom-call | flops 8589934592 | bytes 12582912 | tf_op jit(solution)/shard_map/pallas_call | solution.py:46
  103.0 14.4 %all-gather.3.stats_ref = f32[8,4,3072]{2,1,0:T(4,128)} all-gather(f32[1,4,3072]{2,1,0:T(4,128)} %bitcast.34), channel_id=3, replica_groups=mesh['users'=16,'seq'=8] {'seq'}, dimensions={0}, use_global_device_ids=true | all-gather | bytes 442368 | tf_op jit(solution)/shard_map/all_gather | solution.py:425
  117.4 23.6 %backward.1 = (bf16[320,384]{1,0:T(8,128)(2,1)}, bf16[320,384]{1,0:T(8,128)(2,1)}, bf16[320,384]{1,0:T(8,128)(2,1)}, bf16[320,384]{1,0:T(8,128)(2,1)}, bf16[320,...) custom-call(s32[8,128]{1,0:T(8,128)} %get-tuple-element.37.bounds_re, ...), custom_call_target="tpu_custom_call" | custom-call | flops 34359738368 | bytes 16777216 | tf_op jit(solution)/shard_map/backward/pallas_call | solution.py:432
  141.0 24.0 %all_to_all.27 = f32[16,40,256]{2,1,0:T(8,128)S(1)} all-to-all(f32[16,40,256]{2,1,0:T(8,128)} %get-tuple-element.59), channel_id=1, replica_groups=mesh['users'=16,'seq'=8] {'users'}, dimensions={0} | all-to-all | bytes 1310720 | tf_op jit(solution)/shard_map/all_to_all | solution.py:354
  165.1 11.3 %all_to_all.28 = bf16[16,40,256]{2,1,0:T(8,128)(2,1)} all-to-all(bf16[16,40,256]{2,1,0:T(8,128)(2,1)S(1)} %broadcast_in_dim.8), channel_id=1, replica_groups=mesh['users'=16,'seq'=8] {'users'}, dimensions={0} | all-to-all | bytes 655360 | tf_op jit(solution)/shard_map/all_to_all | solution.py:354
  176.5 2.4 collective-permute-start
  179.6 2.1 collective-permute-start.2
  182.7 2.5 collective-permute-start.4
  186.5 10.5 %collective-permute-done.1.refs_2_ = bf16[320,384]{1,0:T(8,128)(2,1)S(1)} collective-permute-done((bf16[320,384]{1,0:T(8,128)(2,1)S(1)}, bf16[320,384]{1,0:T(8,128)(2,1)S(1)}, u32[]{:S(2)}, u32[]{:S(2)}) %collective-permute-start.1) | collective-permute-done | bytes 245792 | tf_op jit(solution)/shard_map/ppermute | solution.py:463
  197.0 7.3 %collective-permute-done.2.refs_3_ = bf16[320,384]{1,0:T(8,128)(2,1)S(1)} collective-permute-done((bf16[320,384]{1,0:T(8,128)(2,1)S(1)}, bf16[320,384]{1,0:T(8,128)(2,1)S(1)}, u32[]{:S(2)}, u32[]{:S(2)}) %collective-permute-start.2) | collective-permute-done | bytes 245792 | tf_op jit(solution)/shard_map/ppermute | solution.py:463
  204.3 8.9 %collective-permute-done.3.refs_4_ = bf16[320,384]{1,0:T(8,128)(2,1)S(1)} collective-permute-done((bf16[320,384]{1,0:T(8,128)(2,1)S(1)}, bf16[320,384]{1,0:T(8,128)(2,1)S(1)}, u32[]{:S(2)}, u32[]{:S(2)}) %collective-permute-start.3) | collective-permute-done | bytes 245792 | tf_op jit(solution)/shard_map/ppermute | solution.py:463
  216.0 6.0 %shard_map.115 = (bf16[1024,512]{1,0:T(8,128)(2,1)}, bf16[512,384]{1,0:T(8,128)(2,1)}) custom-call(bf16[320,384]{1,0:T(8,128)(2,1)} %get-tuple-element.47.refs_0_, bf16[320,384]{1,0:T(8,128)(2,1)} %copy-done.4, bf16[320,384]{1,0:T(8,128)(2,1)} %copy-done.5, bf16[320,384]{1,0:T(8,128)(2,1)} %copy-done.6, bf16[320,384]{1,0:T(8,128)(2,1)} %copy-done.7, ...), custom_call_target="tpu_custom_call" | custom-call | flops 805306368 | bytes 6291456 | tf_op jit(solution)/shard_map/pallas_call | solution.py:46
  222.0 4.7 %all-to-all-start.2 = ((bf16[128,8,512]{2,1,0:T(8,128)(2,1)}), bf16[128,8,512]{2,1,0:T(8,128)(2,1)S(1)}, u32[]{:S(2)}, u32[]{:S(2)}) async-start(bf16[128,8,512]{2,1,0:T(8,128)(2,1)} %bitcast.27), calls=%async_computation.2 | async-start | bytes 2097152 | tf_op jit(solution)/shard_map/all_to_all | solution.py:354
  226.8 2.1 fusion.1
  228.9 16.9 %all-to-all-done.2 = bf16[128,8,512]{2,1,0:T(8,128)(2,1)S(1)} async-done(((bf16[128,8,512]{2,1,0:T(8,128)(2,1)}), bf16[128,8,512]{2,1,0:T(8,128)(2,1)S(1)}, u32[]{:S(2)}, u32[]{:S(2)}) %all-to-all-start.2) | async-done | bytes 1048608 | tf_op jit(solution)/shard_map/all_to_all | solution.py:354
  246.8 6.6 %shard_map.116 = f32[2048,512]{1,0:T(8,128)} custom-call(s32[8,1024]{1,0:T(8,128)} %get-tuple-element.57.row_ref, bf16[1024,512]{1,0:T(8,128)(2,1)} %bitcast.28), custom_call_target="tpu_custom_call" | custom-call | flops 2147483648 | bytes 6291456 | tf_op jit(solution)/shard_map/pallas_call | solution.py:46
  253.4 4.8 %shard_map.117 = (f32[512,2048]{1,0:T(8,128)}, f32[8,8,8,512]{3,2,1,0:T(8,128)}) custom-call(bf16[8,16,40,256]{3,2,1,0:T(8,128)(2,1)} %bitcast.25), custom_call_target="tpu_custom_call" | custom-call | flops 1048576 | bytes 8388608 | tf_op jit(solution)/shard_map/pallas_call | solution.py:46
  (60 shorter events, 11.5 us)
Async XLA Ops:
  7.2 60.7 %copy-start = (bf16[512,512]{1,0:T(8,128)(2,1)S(1)}, bf16[512,512]{1,0:T(8,128)(2,1)}, u32[]{:S(2)}) copy-start(bf16[512,512]{1,0:T(8,128)(2,1)} %param.12) | copy-start | bytes 1572868
  7.2 63.1 %all-gather.10.cloned.1.call-start = ((), (), s32[]{:S(2)}) async-start(), calls=%async_computation.6 | async-start | bytes 3538944 | tf_op jit(solution)/shard_map/all_gather | solution.py:373
  7.9 81.3 %all-gather.8.cloned.1.call-start = ((), (), s32[]{:S(2)}) async-start(), calls=%async_computation.5 | async-start | bytes 3538944 | tf_op jit(solution)/shard_map/all_gather | solution.py:401
  36.7 27.8 %copy-start.1 = (bf16[512,2048]{1,0:T(8,128)(2,1)S(1)}, bf16[512,2048]{1,0:T(8,128)(2,1)}, u32[]{:S(2)}) copy-start(bf16[512,2048]{1,0:T(8,128)(2,1)} %refs_8_.1) | copy-start | bytes 6291460
  64.5 188.9 %all-gather.12.cloned.1.call-start = ((), (), s32[]{:S(2)}) async-start(), calls=%async_computation.7 | async-start | bytes 2949120 | tf_op jit(solution)/shard_map/all_gather | solution.py:468
  141.0 35.5 %copy-start.17 = (bf16[320,384]{1,0:T(8,128)(2,1)S(1)}, bf16[320,384]{1,0:T(8,128)(2,1)}, u32[]{:S(2)}) copy-start(bf16[320,384]{1,0:T(8,128)(2,1)} %get-tuple-element.48) | copy-start | bytes 737284
  141.0 37.9 %copy-start.16 = (bf16[320,384]{1,0:T(8,128)(2,1)S(1)}, bf16[320,384]{1,0:T(8,128)(2,1)}, u32[]{:S(2)}) copy-start(bf16[320,384]{1,0:T(8,128)(2,1)} %get-tuple-element.49) | copy-start | bytes 737284
  141.0 38.6 %copy-start.15 = (bf16[320,384]{1,0:T(8,128)(2,1)S(1)}, bf16[320,384]{1,0:T(8,128)(2,1)}, u32[]{:S(2)}) copy-start(bf16[320,384]{1,0:T(8,128)(2,1)} %get-tuple-element.50) | copy-start | bytes 737284
  141.0 40.6 %copy-start.14 = (bf16[320,384]{1,0:T(8,128)(2,1)S(1)}, bf16[320,384]{1,0:T(8,128)(2,1)}, u32[]{:S(2)}) copy-start(bf16[320,384]{1,0:T(8,128)(2,1)} %get-tuple-element.51) | copy-start | bytes 737284
  141.0 41.6 %copy-start.13 = (bf16[320,384]{1,0:T(8,128)(2,1)S(1)}, bf16[320,384]{1,0:T(8,128)(2,1)}, u32[]{:S(2)}) copy-start(bf16[320,384]{1,0:T(8,128)(2,1)} %get-tuple-element.52) | copy-start | bytes 737284
  141.0 44.2 %copy-start.12 = (bf16[320,384]{1,0:T(8,128)(2,1)S(1)}, bf16[320,384]{1,0:T(8,128)(2,1)}, u32[]{:S(2)}) copy-start(bf16[320,384]{1,0:T(8,128)(2,1)} %get-tuple-element.53) | copy-start | bytes 737284
  141.0 55.9 %copy-start.11 = (bf16[320,384]{1,0:T(8,128)(2,1)S(1)}, bf16[320,384]{1,0:T(8,128)(2,1)}, u32[]{:S(2)}) copy-start(bf16[320,384]{1,0:T(8,128)(2,1)} %get-tuple-element.54) | copy-start | bytes 737284
  176.5 8.7 %collective-permute-start = (bf16[320,384]{1,0:T(8,128)(2,1)S(1)}, bf16[320,384]{1,0:T(8,128)(2,1)S(1)}, u32[]{:S(2)}, u32[]{:S(2)}) collective-permute-start(bf16[320,384]{1,0:T(8,128)(2,1)S(1)} %copy-done.17), channel_id=1, source_target_pairs={{0,1},{1,2},{2,3},{3,4},{4,5},{5,6},{6,7},{7,0},{8,9},{9,10},{10,1... | collective-permute-start | bytes 737288 | tf_op jit(solution)/shard_map/ppermute | solution.py:463
  178.9 18.1 %collective-permute-start.1 = (bf16[320,384]{1,0:T(8,128)(2,1)S(1)}, bf16[320,384]{1,0:T(8,128)(2,1)S(1)}, u32[]{:S(2)}, u32[]{:S(2)}) collective-permute-start(bf16[320,384]{1,0:T(8,128)(2,1)S(1)} %copy-done.16), channel_id=1, source_target_pairs={{0,2},{1,3},{2,4},{3,5},{4,6},{5,7},{6,0},{7,1},{8,10},{9,11},{10,... | collective-permute-start | bytes 737288 | tf_op jit(solution)/shard_map/ppermute | solution.py:463
  179.6 24.7 %collective-permute-start.2 = (bf16[320,384]{1,0:T(8,128)(2,1)S(1)}, bf16[320,384]{1,0:T(8,128)(2,1)S(1)}, u32[]{:S(2)}, u32[]{:S(2)}) collective-permute-start(bf16[320,384]{1,0:T(8,128)(2,1)S(1)} %copy-done.15), channel_id=1, source_target_pairs={{0,3},{1,4},{2,5},{3,6},{4,7},{5,0},{6,1},{7,2},{8,11},{9,12},{10,... | collective-permute-start | bytes 737288 | tf_op jit(solution)/shard_map/ppermute | solution.py:463
  181.6 31.6 %collective-permute-start.3 = (bf16[320,384]{1,0:T(8,128)(2,1)S(1)}, bf16[320,384]{1,0:T(8,128)(2,1)S(1)}, u32[]{:S(2)}, u32[]{:S(2)}) collective-permute-start(bf16[320,384]{1,0:T(8,128)(2,1)S(1)} %copy-done.14), channel_id=1, source_target_pairs={{0,4},{1,5},{2,6},{3,7},{4,0},{5,1},{6,2},{7,3},{8,12},{9,13},{10,... | collective-permute-start | bytes 737288 | tf_op jit(solution)/shard_map/ppermute | solution.py:463
  182.7 31.2 %collective-permute-start.4 = (bf16[320,384]{1,0:T(8,128)(2,1)S(1)}, bf16[320,384]{1,0:T(8,128)(2,1)S(1)}, u32[]{:S(2)}, u32[]{:S(2)}) collective-permute-start(bf16[320,384]{1,0:T(8,128)(2,1)S(1)} %copy-done.13), channel_id=1, source_target_pairs={{0,5},{1,6},{2,7},{3,0},{4,1},{5,2},{6,3},{7,4},{8,13},{9,14},{10,... | collective-permute-start | bytes 737288 | tf_op jit(solution)/shard_map/ppermute | solution.py:463
  185.2 30.1 %copy-start.4 = (bf16[320,384]{1,0:T(8,128)(2,1)}, bf16[320,384]{1,0:T(8,128)(2,1)S(1)}, u32[]{:S(2)}) copy-start(bf16[320,384]{1,0:T(8,128)(2,1)S(1)} %collective-permute-done.refs_1_) | copy-start | bytes 737284
  185.2 28.7 %collective-permute-start.5 = (bf16[320,384]{1,0:T(8,128)(2,1)S(1)}, bf16[320,384]{1,0:T(8,128)(2,1)S(1)}, u32[]{:S(2)}, u32[]{:S(2)}) collective-permute-start(bf16[320,384]{1,0:T(8,128)(2,1)S(1)} %copy-done.12), channel_id=1, source_target_pairs={{0,6},{1,7},{2,0},{3,1},{4,2},{5,3},{6,4},{7,5},{8,14},{9,15},{10,... | collective-permute-start | bytes 737288 | tf_op jit(solution)/shard_map/ppermute | solution.py:463
  197.0 18.3 %copy-start.5 = (bf16[320,384]{1,0:T(8,128)(2,1)}, bf16[320,384]{1,0:T(8,128)(2,1)S(1)}, u32[]{:S(2)}) copy-start(bf16[320,384]{1,0:T(8,128)(2,1)S(1)} %collective-permute-done.1.refs_2_) | copy-start | bytes 737284
  197.0 18.3 %collective-permute-start.6 = (bf16[320,384]{1,0:T(8,128)(2,1)S(1)}, bf16[320,384]{1,0:T(8,128)(2,1)S(1)}, u32[]{:S(2)}, u32[]{:S(2)}) collective-permute-start(bf16[320,384]{1,0:T(8,128)(2,1)S(1)} %copy-done.11), channel_id=1, source_target_pairs={{0,7},{1,0},{2,1},{3,2},{4,3},{5,4},{6,5},{7,6},{8,15},{9,8},{10,9... | collective-permute-start | bytes 737288 | tf_op jit(solution)/shard_map/ppermute | solution.py:463
  204.3 11.0 %copy-start.6 = (bf16[320,384]{1,0:T(8,128)(2,1)}, bf16[320,384]{1,0:T(8,128)(2,1)S(1)}, u32[]{:S(2)}) copy-start(bf16[320,384]{1,0:T(8,128)(2,1)S(1)} %collective-permute-done.2.refs_3_) | copy-start | bytes 737284
  216.0 10.8 %copy-start.2 = (bf16[384,512]{1,0:T(8,128)(2,1)S(1)}, bf16[384,512]{1,0:T(8,128)(2,1)}, u32[]{:S(2)}) copy-start(bf16[384,512]{1,0:T(8,128)(2,1)} %get-tuple-element.36.refs_10_) | copy-start | bytes 1179652
  222.0 23.8 %all-to-all-start.2 = ((bf16[128,8,512]{2,1,0:T(8,128)(2,1)}), bf16[128,8,512]{2,1,0:T(8,128)(2,1)S(1)}, u32[]{:S(2)}, u32[]{:S(2)}) async-start(bf16[128,8,512]{2,1,0:T(8,128)(2,1)} %bitcast.27), calls=%async_computation.2 | async-start | bytes 2097152 | tf_op jit(solution)/shard_map/all_to_all | solution.py:354
  (5 other events, 6.6 us)
Sparse Core Ops, SparseCore 0:
  9.7 32.1 all-gather.9
  64.6 24.5 all-gather.7
  176.6 40.1 all-gather.11

commit v3 on v2

--- a/solution.py
+++ b/solution.py
@@ -11,7 +11,8 @@
 HEAD_DIM = 64
 SLOTS = 8
 CAP = 6
-BLOCK = 512
+BLOCK = 768
+TILE = 256
 EPSILON = 1e-05
 BOTH = ("users", "seq")
 ORDER = (0, 2, 1, 3)
@@ -33,8 +34,8 @@
     return lax.dot_general(a, b, (((1,), (1,)), ((), ())), preferred_element_type=f32)
 
 
-def call(kernel, out_shape, args, *, grid=None, in_specs=None, out_specs=None, scratch=(), flops=0, moved=0):
-    params = dict(vmem_limit_bytes=60 * 1024 * 1024)
+def call(kernel, out_shape, args, *, grid=None, in_specs=None, out_specs=None, scratch=(), flops=0, moved=0, mib=60):
+    params = dict(vmem_limit_bytes=mib * 1024 * 1024)
     extra = {}
     if grid is not None:
         params["dimension_semantics"] = ("arbitrary",) * len(grid)
@@ -86,7 +87,7 @@
     col_ref[...] = jnp.transpose(jnp.broadcast_to(slot, (lanes, count))).astype(i32)
 
 
-def serve_kernel(asked_ref, table_ref, served_ref, row_ref, bounds_ref, col_ref):
+def serve_kernel(asked_ref, table_ref, gain_ref, served_ref, row_ref, bounds_ref, mid_ref, col_ref, turn_ref):
     step = pl.program_id(0)
     block = served_ref.shape[0]
     devices, lanes = asked_ref.shape
@@ -106,7 +107,11 @@
         mine = lax.div(iota((devices, lanes), 0), SLOTS) == group
         bounds = jnp.sum(jnp.where(mine, asked, 0.0), axis=0, keepdims=True)
         bounds = jnp.broadcast_to(bounds, bounds_ref.shape).astype(i32)
-        bounds_ref[...] = jnp.where(iota(bounds_ref.shape, 1) == SLOTS, lax.axis_index("seq"), bounds)
+        me = lax.axis_index("seq")
+        bounds_ref[...] = jnp.where(iota(bounds_ref.shape, 1) == SLOTS, me, bounds)
+        turn_ref[...] = jnp.transpose(jnp.broadcast_to(gain_ref[...], (lanes, gain_ref.shape[1])))
+        d = mid_ref.shape[0]
+        mid_ref[...] = turn_ref[pl.ds(pl.multiple_of(me * d, d), d), :]
 
     column = col_ref[pl.ds(pl.multiple_of(step * block, block), block), :].astype(i32)
     parts = []
@@ -131,16 +136,29 @@
     return jnp.where(position < one, 0, jnp.where(position < two, one, two))
 
 
-def visible(i, j, one, two):
-    where_q = iota((1, BLOCK), 1) + i * BLOCK
+def visible(i, j, one, two, block):
+    where_q = iota((1, block), 1) + i * block
     start = seg_start(where_q, one, two)
-    where_k = iota((BLOCK, BLOCK), 0) + j * BLOCK
+    where_k = iota((block, block), 0) + j * block
     return (where_k >= start) & (where_k <= where_q)
 
 
+def pair_of(p, base, one, two):
+    first = lax.div(seg_start(base * TILE, one, two), TILE)
+    i, j = base, first + p
+    passed = base - first + 1
+    for step in range(1, BLOCK // TILE):
+        first = lax.div(seg_start((base + step) * TILE, one, two), TILE)
+        later = p >= passed
+        i = jnp.where(later, base + step, i)
+        j = jnp.where(later, first + p - passed, j)
+        passed = passed + base + step - first + 1
+    return i, j, passed
+
+
 def forward_kernel(
-    xin_ref, cot_ref, win_ref, wout_ref, gain_ref, bounds_ref,
-    q_ref, k_ref, vk_ref, slope_ref, u_ref, dg_ref, mixed_ref, stats_ref,
+    xin_ref, dg_ref, win_ref, gain_ref, bounds_ref,
+    q_ref, k_ref, vk_ref, slope_ref, u_ref, mixed_ref, stats_ref,
     q_all, v_all, vk_all,
 ):
     i = pl.program_id(0)
@@ -171,22 +189,25 @@
         there = pl.ds(pl.multiple_of(j * BLOCK, BLOCK), BLOCK)
         half = mm(vk_all[there, :], q_all[...])
         weights = half + half * jnp.tanh(half)
-        weights = jnp.where(visible(i, j, one, two), weights, 0.0).astype(bf16)
+        weights = jnp.where(visible(i, j, one, two, BLOCK), weights, 0.0).astype(bf16)
         mixed_ref[...] += mm(v_all[:, there], weights)
         return carry
 
     first = lax.div(seg_start(i * BLOCK, one, two), BLOCK)
     lax.fori_loop(first, i + 1, pair, 0)
-    dg = mm_nt(wout_ref[...], cot_ref[...])
-    dg_ref[...] = dg
+    dg = dg_ref[...]
     mixed = mixed_ref[...]
     e = dg * u * gain_ref[:, :1]
     mean = jnp.sum(mixed, axis=0, keepdims=True) * (1.0 / d)
     centred = mixed - mean
-    stats_ref[0:1, :] = mean
-    stats_ref[1:2, :] = jnp.sum(centred * centred, axis=0, keepdims=True)
-    stats_ref[2:3, :] = jnp.sum(e, axis=0, keepdims=True)
-    stats_ref[3:4, :] = jnp.sum(e * centred, axis=0, keepdims=True)
+    spread = jnp.sum(centred * centred, axis=0, keepdims=True)
+    sum_e = jnp.sum(e, axis=0, keepdims=True)
+    sum_em = jnp.sum(e * centred, axis=0, keepdims=True)
+    for h in range(HEADS):
+        stats_ref[h, 0:1, :] = mean
+        stats_ref[h, 1:2, :] = spread
+        stats_ref[h, 2:3, :] = sum_e
+        stats_ref[h, 3:4, :] = sum_em
 
 
 def middle(stats, mixed, dg, u, gain):
@@ -210,87 +231,103 @@
 
 
 def backward_kernel(
-    steps, bounds_ref, q_ref, k_ref, vk_ref, stats_ref, mixed_ref, dg_ref, u_ref, gain_ref, xin_ref, cot_ref, slope_ref,
+    steps, bounds_ref, q_ref, k_ref, vk_ref, stats_ref, mixed_ref, dg_ref, u_ref, gain_ref, xin_hbm, cot_hbm, slope_hbm,
     *rest,
 ):
-    outs, (dw_ref, k_all, vk_all, gated_all, du_all, dq_all, dk_all, dv_all, win_acc, wout_acc, sent, sems) = (
-        rest[:HEADS],
-        rest[HEADS:],
-    )
+    outs, rest = rest[:HEADS], rest[HEADS:]
+    dw_ref, k_all, vk_all, gated_all, du_all, dq_all, dk_all, dv_all, win_acc, wout_acc, sent, sems = rest[:12]
+    query2, up2, half0, upper0, half1, upper1, xin_ref, cot_ref, slope_ref, loaded = rest[12:]
+    loads = [
+        pltpu.make_async_copy(source, target, loaded.at[at])
+        for at, (source, target) in enumerate(((xin_hbm, xin_ref), (cot_hbm, cot_ref), (slope_hbm, slope_ref)))
+    ]
     g = pl.program_id(0)
     one, two, me = bounds_ref[0, CAP], bounds_ref[0, CAP + 1], bounds_ref[0, SLOTS]
     d = HEAD_DIM
 
     @pl.when(g == 0)
     def _():
+        for load in loads:
+            load.start()
         dk_all[...] = jnp.zeros(dk_all.shape, f32)
         dv_all[...] = jnp.zeros(dv_all.shape, f32)
         dq_all[...] = jnp.zeros(dq_all.shape, f32)
         win_acc[...] = jnp.zeros(win_acc.shape, f32)
         wout_acc[...] = jnp.zeros(wout_acc.shape, f32)
+        query2[...] = jnp.zeros(query2.shape, bf16)
+        up2[...] = jnp.zeros(up2.shape, bf16)
 
     @pl.when(g < steps)
     def _():
         here = pl.ds(pl.multiple_of(g * BLOCK, BLOCK), BLOCK)
-        blank = jnp.zeros((d, BLOCK), bf16)
         gated, up, du = middle(stats_ref[...], mixed_ref[...], dg_ref[...], u_ref[...], gain_ref[:, :1])
         gated_all[:, here] = gated
         du_all[:, here] = du
         k_all[:, here] = k_ref[...]
         vk_all[here, :] = vk_ref[...]
-        query = q_ref[...]
-        query2 = jnp.concatenate([blank, query], axis=0)
-        up2 = jnp.concatenate([up, blank], axis=0)
-
-        def pair(j, carry):
-            there = pl.ds(pl.multiple_of(j * BLOCK, BLOCK), BLOCK)
-            vk = vk_all[there, :]
-            half = mm(vk, query2)
-            upper = mm(vk, up2)
+        query2[d:, :] = q_ref[...]
+        up2[:d, :] = up
+        base = g * (BLOCK // TILE)
+        total = pair_of(0, base, one, two)[2]
+
+        def front(i, j):
+            at = pl.ds(pl.multiple_of((i - base) * TILE, TILE), TILE)
+            vk = vk_all[pl.ds(pl.multiple_of(j * TILE, TILE), TILE), :]
+            return mm(vk, query2[:, at]), mm(vk, up2[:, at])
+
+        def back(i, j, half, upper, live):
+            at = pl.ds(pl.multiple_of((i - base) * TILE, TILE), TILE)
+            here = pl.ds(pl.multiple_of(i * TILE, TILE), TILE)
+            there = pl.ds(pl.multiple_of(j * TILE, TILE), TILE)
             tanh = jnp.tanh(half)
             plus = 1.0 + tanh
             weights = half * plus
             dscores = upper * (plus + weights * (1.0 - tanh))
-            seen = visible(g, j, one, two)
+            seen = visible(i, jnp.where(live, j, dq_all.shape[1]), one, two, TILE)
             weights = jnp.where(seen, weights, 0.0).astype(bf16)
             dscores = jnp.where(seen, dscores, 0.0).astype(bf16)
-            dv_all[:, there] += mm_nt(up, weights)
-            dk_all[:, there] += mm_nt(query, dscores)
+            dv_all[:, there] += mm_nt(up2[:d, at], weights)
+            dk_all[:, there] += mm_nt(query2[d:, at], dscores)
             dq_all[:, here] += mm(k_all[:, there], dscores)
+
+        half0[...], upper0[...] = front(*pair_of(0, base, one, two)[:2])
+
+        def two_pairs(t, carry):
+            p = 2 * t
+            now, odd, after = [
+                pair_of(jnp.minimum(p + step, total - 1), base, one, two)[:2] for step in range(3)
+            ]
+            half1[...], upper1[...] = front(*odd)
+            back(*now, half0[...], upper0[...], True)
+            half0[...], upper0[...] = front(*after)
+            back(*odd, half1[...], upper1[...], p + 1 < total)
             return carry
 
-        first = lax.div(seg_start(g * BLOCK, one, two), BLOCK)
-        lax.fori_loop(first, g + 1, pair, 0)
-
-    @pl.when(g >= steps)
+        lax.fori_loop(0, lax.div(total + 1, 2), two_pairs, 0)
+
+    @pl.when(g == steps)
     def _():
-        s = g - steps
-        count = xin_ref.shape[0]
-        here = pl.ds(pl.multiple_of(lax.rem(me + s, HEADS) * count, 128), count)
-        slope = slope_ref[...]
-        gated = gated_all[:, here]
-        dpre = jnp.concatenate(
-            [
-                (du_all[:, here] * slope[:d]).astype(bf16),
-                (dq_all[:, here] * slope[d : 2 * d]).astype(bf16),
-                (dv_all[:, here] * 16.0 * slope[2 * d : 3 * d]).astype(bf16),
-                (dk_all[:, here] * 16.0 * slope[3 * d :]).astype(bf16),
-            ],
-            axis=0,
-        )
-        sent[s, : 4 * d, :] = dpre
-        sent[s, 4 * d :, :] = gated
-        for at in range(HEADS):
-
-            @pl.when(s == at)
-            def _():
-                pltpu.make_async_copy(sent.at[at], outs[at], sems.at[at]).start()
-
-        win_acc[...] += mm(dpre, xin_ref[...])
-        wout_acc[...] += mm(gated, cot_ref[...])
-
-    @pl.when(g == pl.num_programs(0) - 1)
-    def _():
+        for load in loads:
+            load.wait()
+        count = sent.shape[2]
+        for s in range(HEADS):
+            start = pl.multiple_of(lax.rem(me + s, HEADS) * count, 128)
+            here = pl.ds(start, count)
+            gated = gated_all[:, here]
+            dpre = jnp.concatenate(
+                [
+                    (du_all[:, here] * slope_ref[:d, here]).astype(bf16),
+                    (dq_all[:, here] * slope_ref[d : 2 * d, here]).astype(bf16),
+                    (dv_all[:, here] * 16.0 * slope_ref[2 * d : 3 * d, here]).astype(bf16),
+                    (dk_all[:, here] * 16.0 * slope_ref[3 * d :, here]).astype(bf16),
+                ],
+                axis=0,
+            )
+            sent[s, : 4 * d, :] = dpre
+            sent[s, 4 * d :, :] = gated
+            pltpu.make_async_copy(sent.at[s], outs[s], sems.at[s]).start()
+            win_acc[...] += mm(dpre, xin_ref[here, :])
+            wout_acc[...] += mm(gated, cot_ref[here, :])
         parts = dw_ref.shape[0]
         turned = jnp.transpose(win_acc[...])
         rows = turned.shape[0] // parts
@@ -381,14 +418,16 @@
     steps = 4
     whole = lambda *shape: pl.BlockSpec(shape, lambda g: (0,) * len(shape))
     smem = pl.BlockSpec(memory_space=pltpu.SMEM)
-    served, asked_row, bounds = call(
+    served, asked_row, bounds, gain_h = call(
         serve_kernel,
-        (struct((slots, width), bf16), struct((8, slots), i32), struct((8, 128), i32)),
-        (asked, item_table),
+        (struct((slots, width), bf16), struct((8, slots), i32), struct((8, 128), i32), struct((d, 128), f32)),
+        (asked, item_table, gain_mid.reshape(1, width)),
         grid=(steps,),
-        in_specs=[whole(devices, 128), whole(shard_rows, width)],
-        out_specs=[pl.BlockSpec((slots // steps, width), lambda g: (g, 0)), whole(8, slots), whole(8, 128)],
-        scratch=[pltpu.VMEM((slots, 128), f32)],
+        in_specs=[whole(devices, 128), whole(shard_rows, width), whole(1, width)],
+        out_specs=[
+            pl.BlockSpec((slots // steps, width), lambda g: (g, 0)), whole(8, slots), whole(8, 128), whole(d, 128),
+        ],
+        scratch=[pltpu.VMEM((slots, 128), f32), pltpu.VMEM((width, 128), f32)],
         flops=2 * slots * shard_rows * width, moved=4 << 20,
     )
     got = exchange(served.reshape(devices, SLOTS, width), BOTH).reshape(slots, width)
@@ -403,28 +442,29 @@
     mine = lax.dynamic_index_in_dim(weight_in.reshape(width, 4, HEADS, d), head, 2, keepdims=False)
     win_t = jnp.stack([mine[:, b] for b in ORDER], axis=1).reshape(width, 4 * d).T
     wout_h = lax.dynamic_slice_in_dim(weight_out, head * d, d, axis=0)
-    gain_h = jnp.broadcast_to(lax.dynamic_slice_in_dim(gain_mid, head * d, d)[:, None], (d, 128))
 
     blocks = length // BLOCK
     lane = lambda rows: pl.BlockSpec((rows, BLOCK), lambda g: (0, g))
     rowed = lambda columns: pl.BlockSpec((BLOCK, columns), lambda g: (g, 0))
-    q_t, k_t, vk, slope, u, dg, mixed, stats = call(
+    dg = mm_nt(wout_h, cot_all)
+    q_t, k_t, vk, slope, u, mixed, stats = call(
         forward_kernel,
         (
             struct((d, length), bf16), struct((d, length), bf16), struct((length, 2 * d), bf16),
-            struct((4 * d, length), f32), struct((d, length), f32), struct((d, length), f32),
-            struct((d, length), f32), struct((4, length), f32),
+            struct((4 * d, length), f32), struct((d, length), f32),
+            struct((d, length), f32), struct((seq, 4, length), f32),
         ),
-        (xin_all, cot_all, win_t, wout_h, gain_h, bounds),
-        grid=(blocks,),
-        in_specs=[rowed(width), rowed(width), whole(4 * d, width), whole(d, width), whole(d, 128), smem],
-        out_specs=[lane(d), lane(d), rowed(2 * d), lane(4 * d), lane(d), lane(d), lane(d), lane(4)],
+        (xin_all, dg, win_t, gain_h, bounds),
+        mib=60, grid=(blocks,),
+        in_specs=[rowed(width), lane(d), whole(4 * d, width), whole(d, 128), smem],
+        out_specs=[lane(d), lane(d), rowed(2 * d), lane(4 * d), lane(d), lane(d),
+            pl.BlockSpec((seq, 4, BLOCK), lambda g: (0, 0, g)),
+        ],
         scratch=[pltpu.VMEM((2 * d, BLOCK), bf16), pltpu.VMEM((d, length), bf16), pltpu.VMEM((length, 2 * d), bf16)],
         flops=1 << 33, moved=12 << 20,
     )
-    stats_all = lax.all_gather(stats, "seq", axis=0, tiled=False)
-
-    late = lambda g, b: lax.rem(b[0, SLOTS] + jnp.maximum(g - blocks, 0), seq)
+    stats_all = exchange(stats, "seq")
+
     early = lambda g: jnp.minimum(g, blocks - 1)
     fixed = lambda *shape: pl.BlockSpec(shape, lambda g, b: (0,) * len(shape))
     lanes = lambda rows: pl.BlockSpec((rows, BLOCK), lambda g, b: (0, early(g)))
@@ -434,14 +474,12 @@
         out_shape=[struct((5 * d, count), bf16)] * HEADS + [struct((users, rows + 8, 4 * d), f32)],
         grid_spec=pltpu.PrefetchScalarGridSpec(
             num_scalar_prefetch=1,
-            grid=(blocks + seq,),
+            grid=(blocks + 1,),
             in_specs=[
                 lanes(d), lanes(d), pl.BlockSpec((BLOCK, 2 * d), lambda g, b: (early(g), 0)),
                 pl.BlockSpec((seq, 4, BLOCK), lambda g, b: (0, 0, early(g))),
                 lanes(d), lanes(d), lanes(d), fixed(d, 128),
-                pl.BlockSpec((count, width), lambda g, b: (late(g, b), 0)),
-                pl.BlockSpec((count, width), lambda g, b: (late(g, b), 0)),
-                pl.BlockSpec((4 * d, count), lambda g, b: (0, late(g, b))),
+                *[pl.BlockSpec(memory_space=pl.ANY)] * 3,
             ],
             out_specs=[pl.BlockSpec(memory_space=pl.ANY)] * HEADS + [fixed(users, rows + 8, 4 * d)],
             scratch_shapes=[
@@ -449,6 +487,10 @@
                 pltpu.VMEM((d, length), f32), pltpu.VMEM((d, length), f32), pltpu.VMEM((d, length), f32),
                 pltpu.VMEM((d, length), f32), pltpu.VMEM((4 * d, width), f32), pltpu.VMEM((d, width), f32),
                 pltpu.VMEM((HEADS, 5 * d, count), bf16), pltpu.SemaphoreType.DMA((HEADS,)),
+                pltpu.VMEM((2 * d, BLOCK), bf16), pltpu.VMEM((2 * d, BLOCK), bf16),
+                *[pltpu.VMEM((TILE, TILE), f32)] * 4,
+                pltpu.VMEM((length, width), bf16), pltpu.VMEM((length, width), bf16), pltpu.VMEM((4 * d, length), f32),
+                pltpu.SemaphoreType.DMA((3,)),
             ],
         ),
         name="backward",
@@ -470,7 +512,7 @@
         rows_kernel,
         (struct((slots, width), bf16), struct((width, count), bf16)),
         (*pieces, weight_in, gain_row, fetched, upstream, slot_row),
-        scratch=[pltpu.VMEM((4 * width, count), bf16)],
+        mib=24, in_specs=[pl.BlockSpec(memory_space=pltpu.VMEM)] * (HEADS + 5), scratch=[pltpu.VMEM((4 * width, count), bf16)],
         flops=2 * count * width * 4 * width, moved=6 << 20,
     )
     layer = (
@@ -484,8 +526,8 @@
         table_kernel,
         struct((shard_rows, width), f32),
         (asked_row, incoming),
-        grid=(tiles,),
-        in_specs=[whole(8, slots), whole(slots, width)],
+        mib=24, grid=(tiles,),
+        in_specs=[whole(8, slots), pl.BlockSpec(memory_space=pltpu.VMEM)],
         out_specs=pl.BlockSpec((shard_rows // tiles, width), lambda g: (g, 0)),
         flops=2 * slots * shard_rows * width, moved=6 << 20,
     )

time: 266 us -> 250 us (0.940)
  Pallas kernels: 64.4 us -> 50.4 us
  blocking collectives: 95.9 us -> 91.1 us
  matrix products: 2.14 us -> 6.12 us
  waiting for transfers between devices: 65.3 us -> 62.5 us
    all_gather x1 -> x0, blocking collectives: 14.4 us -> none  [layer_step(): stats_all = lax.all_gather(stats, 'seq', axis=0, tiled=False)]
    all_to_all x4 -> x5, blocking collectives: 81.6 us -> 91.1 us  [exchange(): return lax.all_to_all(x, axis, split_axis=0, concat_axis=0, tiled=True)]
    pallas_call x7, Pallas kernels: 40.8 us -> 33.4 us  [call(): pl.pallas_call(kernel, out_shape=out_shape, scratch_shapes=scratch, compi...]
    pallas_call x1, Pallas kernels: 23.6 us -> 17 us  [layer_step(): pl.pallas_call(functools.partial(backward_kernel, blocks), out_shape=[str...]
    dot_general x0 -> x1, matrix products: none -> 3.98 us  [mm_nt(): lax.dot_general(a, b, (((1,), (1,)), ((), ())), preferred_element_type=f32)]
  transfers between devices with their start and end apart: 11 -> 11, of which waited for: 8 -> 8; matrix products, arithmetic and copies ran while one was open for 3% -> 4% of each run, Pallas kernels for 9% -> 7%
where the time goes in v3:
time: 250 us; the launch traced here: 249 us
  blocking collectives  91.1 us (36%)
  waiting for transfers between devices  62.5 us (25%)
  Pallas kernels  50.4 us (20%)
  starting transfers between devices  16.4 us (7%)
  between operations  13.9 us (6%)
  local copies, waits for them, and re-layouts  6.2 us (2%)
  matrix products  6.12 us (2%)
    all_to_all x5, blocking collectives, exchange(): return lax.all_to_all(x, axis, split_axis=0, concat_axis=0, tiled=True)  91.1 us
    pallas_call x7, Pallas kernels, call(): pl.pallas_call(kernel, out_shape=out_shape, scratch_shapes=scratch, compi...  33.4 us
    ppermute x7, waiting for transfers between devices, layer_step(): lax.ppermute(result[s], 'seq', [(i, (i + s) % seq) for i in range(seq)])  28.5 us
    pallas_call x1, Pallas kernels, layer_step(): pl.pallas_call(functools.partial(backward_kernel, blocks), out_shape=[str...  17 us
    all_to_all x1, waiting for transfers between devices, exchange(): return lax.all_to_all(x, axis, split_axis=0, concat_axis=0, tiled=True)  16.9 us
    all_gather x1, waiting for transfers between devices, layer_step(): xin_all = lax.all_gather(xin, 'seq', axis=0, tiled=True)  16.4 us
    ppermute x7, starting transfers between devices, layer_step(): lax.ppermute(result[s], 'seq', [(i, (i + s) % seq) for i in range(seq)])  11.4 us
    unnamed x21, local copies, waits for them, and re-layouts  5.19 us
  transfers between devices with their start and end apart: 11, of which 8 were waited for; matrix products, arithmetic and copies ran while one was open for 4% of the time, Pallas kernels for 7%

profile of v3, /device:TPU:1, one launch (start us, length us, event | category | flops | bytes accessed | tf_op | source)
XLA Modules:
  0.0 248.6 jit_solution(7562358504880152089)
XLA Ops:
  9.8 21.3 %all_to_all.30 = s32[128,1,128]{2,1,0:T(1,128)} all-to-all(s32[128,1,128]{2,1,0:T(1,128)} %bitcast.38), channel_id=1, replica_groups=mesh['users'=16,'seq'=8] {'users','seq'}, dimensions={0} | all-to-all | bytes 131072 | tf_op jit(solution)/shard_map/all_to_all | solution.py:391
  31.1 5.6 %shard_map.112 = (bf16[1024,512]{1,0:T(8,128)(2,1)}, s32[8,1024]{1,0:T(8,128)}, s32[8,128]{1,0:T(8,128)}, f32[64,128]{1,0:T(8,128)}) custom-call(s32[128,128]{1,0:T(8,128)} %bitcast.37, bf16[2048,512]{1,0:T(8,128)(2,1)} %table_ref.1, f32[1,512]{1,0:T(1,128)} %bitcast.40), custom_call_target="tpu_custom_call" | custom-call | flops 2147483648 | bytes 4194304 | tf_op jit(solution)/shard_map/pallas_call | solution.py:47
  36.7 24.8 %all_to_all.31 = bf16[128,8,512]{2,1,0:T(8,128)(2,1)} all-to-all(bf16[128,8,512]{2,1,0:T(8,128)(2,1)} %bitcast.34), channel_id=1, replica_groups=mesh['users'=16,'seq'=8] {'users','seq'}, dimensions={0} | all-to-all | bytes 2097152 | tf_op jit(solution)/shard_map/all_to_all | solution.py:391
  61.6 2.8 %shard_map.113 = (bf16[384,512]{1,0:T(8,128)(2,1)}, bf16[384,512]{1,0:T(8,128)(2,1)}) custom-call(bf16[1024,512]{1,0:T(8,128)(2,1)} %bitcast.35, s32[384,128]{1,0:T(8,128)} %get-tuple-element.35.col_ref, f32[1,512]{1,0:T(1,128)} %bitcast.29), custom_call_target="tpu_custom_call" | custom-call | flops 402653184 | bytes 2097152 | tf_op jit(solution)/shard_map/pallas_call | solution.py:47
  64.5 2.5 %copy.15 = bf16[512,2048]{0,1:T(8,128)(2,1)} copy(bf16[512,2048]{1,0:T(8,128)(2,1)S(1)} %copy-done.1) | data formatting | bytes 4194304 | tf_op args[3]
  68.8 4.0 %fusion.2.dg_ref = f32[64,3072]{1,0:T(8,128)} fusion(bf16[512,512]{1,0:T(8,128)(2,1)S(1)} %copy-done, s32[]{:T(128)S(6)} %select_n.7, bf16[1,3072,512]{2,1,0:T(8,128)(2,1)} %all-gather.8.cloned.1.call-done), kind=kOutput, calls=%fused_computation.5 | convolution fusion | flops 201326592 | bytes 3997700 | tf_op jit(solution)/shard_map/dot_general | solution.py:34
  72.7 16.4 %all-gather.6.cloned.1.call-done.xin_ref.xin_hbm = bf16[3072,512]{1,0:T(8,128)(2,1)} async-done(((bf16[384,512]{1,0:T(8,128)(2,1)}), bf16[3072,512]{1,0:T(8,128)(2,1)}) %all-gather.6.cloned.1.call-update) | async-done | bytes 3145744 | tf_op jit(solution)/shard_map/all_gather | solution.py:440
  89.1 10.4 %shard_map.114 = (bf16[64,3072]{1,0:T(8,128)(2,1)}, bf16[64,3072]{1,0:T(8,128)(2,1)}, bf16[3072,128]{1,0:T(8,128)(2,1)}, f32[256,3072]{1,0:T(8,128)}, f32[64,307...) custom-call(bf16[3072,512]{1,0:T(8,128)(2,1)} %all-gather.6.cloned.1.call-done.xin_ref.xin_hbm, ...), custom_call_target="tpu_custom_call" | custom-call | flops 8589934592 | bytes 12582912 | tf_op jit(solution)/shard_map/pallas_call | solution.py:47
  99.6 12.4 %all_to_all.32.stats_ref = f32[8,4,3072]{2,1,0:T(4,128)} all-to-all(f32[8,4,3072]{2,1,0:T(4,128)} %get-tuple-element.43), channel_id=1, replica_groups=mesh['users'=16,'seq'=8] {'seq'}, dimensions={0} | all-to-all | bytes 786432 | tf_op jit(solution)/shard_map/all_to_all | solution.py:391
  111.9 17.0 %backward.1 = (bf16[320,384]{1,0:T(8,128)(2,1)}, bf16[320,384]{1,0:T(8,128)(2,1)}, bf16[320,384]{1,0:T(8,128)(2,1)}, bf16[320,384]{1,0:T(8,128)(2,1)}, bf16[320,...) custom-call(s32[8,128]{1,0:T(8,128)} %get-tuple-element.37.bounds_re, ...), custom_call_target="tpu_custom_call" | custom-call | flops 34359738368 | bytes 16777216 | tf_op jit(solution)/shard_map/backward/pallas_call | solution.py:472
  129.0 21.4 %all_to_all.33 = f32[16,40,256]{2,1,0:T(8,128)} all-to-all(f32[16,40,256]{2,1,0:T(8,128)} %get-tuple-element.59), channel_id=1, replica_groups=mesh['users'=16,'seq'=8] {'users'}, dimensions={0} | all-to-all | bytes 1310720 | tf_op jit(solution)/shard_map/all_to_all | solution.py:391
  151.6 11.2 %all_to_all.34 = bf16[16,40,256]{2,1,0:T(8,128)(2,1)} all-to-all(bf16[16,40,256]{2,1,0:T(8,128)(2,1)S(1)} %broadcast_in_dim.10), channel_id=1, replica_groups=mesh['users'=16,'seq'=8] {'users'}, dimensions={0} | all-to-all | bytes 655360 | tf_op jit(solution)/shard_map/all_to_all | solution.py:391
  162.8 3.6 %collective-permute-start = (bf16[320,384]{1,0:T(8,128)(2,1)}, bf16[320,384]{1,0:T(8,128)(2,1)S(1)}, u32[]{:S(2)}, u32[]{:S(2)}) collective-permute-start(bf16[320,384]{1,0:T(8,128)(2,1)} %get-tuple-element.48), channel_id=1, source_target_pairs={{0,1},{1,2},{2,3},{3,4},{4,5},{5,6},{6,7},{7,0},{8,9},{9,10},{10,1... | collective-permute-start | bytes 737288 | tf_op jit(solution)/shard_map/ppermute | solution.py:505
  166.4 2.1 collective-permute-start.2
  170.0 2.6 %collective-permute-start.4 = (bf16[320,384]{1,0:T(8,128)(2,1)}, bf16[320,384]{1,0:T(8,128)(2,1)S(1)}, u32[]{:S(2)}, u32[]{:S(2)}) collective-permute-start(bf16[320,384]{1,0:T(8,128)(2,1)} %get-tuple-element.52), channel_id=1, source_target_pairs={{0,5},{1,6},{2,7},{3,0},{4,1},{5,2},{6,3},{7,4},{8,13},{9,14},{10,... | collective-permute-start | bytes 737288 | tf_op jit(solution)/shard_map/ppermute | solution.py:505
  174.2 11.4 %collective-permute-done.1.refs_2_ = bf16[320,384]{1,0:T(8,128)(2,1)S(1)} collective-permute-done((bf16[320,384]{1,0:T(8,128)(2,1)}, bf16[320,384]{1,0:T(8,128)(2,1)S(1)}, u32[]{:S(2)}, u32[]{:S(2)}) %collective-permute-start.1) | collective-permute-done | bytes 245792 | tf_op jit(solution)/shard_map/ppermute | solution.py:505
  185.6 6.8 %collective-permute-done.2.refs_3_ = bf16[320,384]{1,0:T(8,128)(2,1)S(1)} collective-permute-done((bf16[320,384]{1,0:T(8,128)(2,1)}, bf16[320,384]{1,0:T(8,128)(2,1)S(1)}, u32[]{:S(2)}, u32[]{:S(2)}) %collective-permute-start.2) | collective-permute-done | bytes 245792 | tf_op jit(solution)/shard_map/ppermute | solution.py:505
  192.4 7.9 %collective-permute-done.3.refs_4_ = bf16[320,384]{1,0:T(8,128)(2,1)S(1)} collective-permute-done((bf16[320,384]{1,0:T(8,128)(2,1)}, bf16[320,384]{1,0:T(8,128)(2,1)S(1)}, u32[]{:S(2)}, u32[]{:S(2)}) %collective-permute-start.3) | collective-permute-done | bytes 245792 | tf_op jit(solution)/shard_map/ppermute | solution.py:505
  203.7 2.5 %shard_map.115 = (bf16[1024,512]{1,0:T(8,128)(2,1)S(1)}, bf16[512,384]{1,0:T(8,128)(2,1)S(1)}) custom-call(bf16[320,384]{1,0:T(8,128)(2,1)S(1)} %copy-done.6, bf16[320,384]{1,0:T(8,128)(2,1)S(1)} %collective-permute-done.refs_1_, bf16[320,384]{1,0:T(8,128)(2,1)S(1)} %collective-permute-done.1.refs_2_, bf16[320,384]{1,0:T(8,128)(2,1)S(1)} %collective-permute-done.2.refs_3_, ...), custom_call_target="tpu_custom_call" | custom-call | flops 805306368 | bytes 6291456 | tf_op jit(solution)/shard_map/pallas_call | solution.py:47
  207.9 4.9 %all-to-all-start.3 = ((bf16[128,8,512]{2,1,0:T(8,128)(2,1)}), bf16[128,8,512]{2,1,0:T(8,128)(2,1)S(1)}, u32[]{:S(2)}, u32[]{:S(2)}) async-start(bf16[128,8,512]{2,1,0:T(8,128)(2,1)} %bitcast.27), calls=%async_computation.3 | async-start | bytes 2097152 | tf_op jit(solution)/shard_map/all_to_all | solution.py:391
  212.8 2.1 fusion.1
  215.0 16.9 %all-to-all-done.3 = bf16[128,8,512]{2,1,0:T(8,128)(2,1)S(1)} async-done(((bf16[128,8,512]{2,1,0:T(8,128)(2,1)}), bf16[128,8,512]{2,1,0:T(8,128)(2,1)S(1)}, u32[]{:S(2)}, u32[]{:S(2)}) %all-to-all-start.3) | async-done | bytes 1048608 | tf_op jit(solution)/shard_map/all_to_all | solution.py:391
  231.9 5.4 %shard_map.116 = f32[2048,512]{1,0:T(8,128)} custom-call(s32[8,1024]{1,0:T(8,128)S(1)} %copy-done.9, bf16[1024,512]{1,0:T(8,128)(2,1)S(1)} %bitcast.28), custom_call_target="tpu_custom_call" | custom-call | flops 2147483648 | bytes 6291456 | tf_op jit(solution)/shard_map/pallas_call | solution.py:47
  237.2 4.8 %shard_map.117 = (f32[512,2048]{1,0:T(8,128)}, f32[8,8,8,512]{3,2,1,0:T(8,128)}) custom-call(bf16[8,16,40,256]{3,2,1,0:T(8,128)(2,1)} %bitcast.33), custom_call_target="tpu_custom_call" | custom-call | flops 1048576 | bytes 8388608 | tf_op jit(solution)/shard_map/pallas_call | solution.py:47
  (42 shorter events, 13.7 us)
Async XLA Ops:
  7.2 61.6 %copy-start = (bf16[512,512]{1,0:T(8,128)(2,1)S(1)}, bf16[512,512]{1,0:T(8,128)(2,1)}, u32[]{:S(2)}) copy-start(bf16[512,512]{1,0:T(8,128)(2,1)} %param.12) | copy-start | bytes 1572868
  7.2 61.6 %all-gather.8.cloned.1.call-start = ((), (), s32[]{:S(2)}) async-start(), calls=%async_computation.7 | async-start | bytes 3538944 | tf_op jit(solution)/shard_map/all_gather | solution.py:410
  7.9 81.2 %all-gather.6.cloned.1.call-start = ((), (), s32[]{:S(2)}) async-start(), calls=%async_computation.6 | async-start | bytes 3538944 | tf_op jit(solution)/shard_map/all_gather | solution.py:440
  36.7 27.8 %copy-start.1 = (bf16[512,2048]{1,0:T(8,128)(2,1)S(1)}, bf16[512,2048]{1,0:T(8,128)(2,1)}, u32[]{:S(2)}) copy-start(bf16[512,2048]{1,0:T(8,128)(2,1)} %refs_8_.1) | copy-start | bytes 6291460
  64.4 172.8 %all-gather.10.cloned.1.call-start = ((), (), s32[]{:S(2)}) async-start(), calls=%async_computation.8 | async-start | bytes 2949120 | tf_op jit(solution)/shard_map/all_gather | solution.py:510
  128.9 73.8 %copy-start.2 = (bf16[1,384,512]{2,1,0:T(8,128)(2,1)S(1)}, bf16[1,384,512]{2,1,0:T(8,128)(2,1)}, u32[]{:S(2)}) copy-start(bf16[1,384,512]{2,1,0:T(8,128)(2,1)} %param.15) | copy-start | bytes 1179652
  128.9 73.8 %copy-start.3 = (bf16[384,512]{1,0:T(8,128)(2,1)S(1)}, bf16[384,512]{1,0:T(8,128)(2,1)}, u32[]{:S(2)}) copy-start(bf16[384,512]{1,0:T(8,128)(2,1)} %get-tuple-element.36.refs_10_) | copy-start | bytes 1179652
  128.9 73.8 %copy-start.7 = (s32[8,384]{1,0:T(8,128)S(1)}, s32[8,384]{1,0:T(8,128)}, u32[]{:S(2)}) copy-start(s32[8,384]{1,0:T(8,128)} %get-tuple-element.55.refs_12_) | copy-start | bytes 36868
  128.9 73.8 %copy-start.8 = (f32[512]{0:T(512)S(1)}, f32[512]{0:T(512)}, u32[]{:S(2)}) copy-start(f32[512]{0:T(512)} %param.13) | copy-start | bytes 6148
  162.8 9.8 %collective-permute-start = (bf16[320,384]{1,0:T(8,128)(2,1)}, bf16[320,384]{1,0:T(8,128)(2,1)S(1)}, u32[]{:S(2)}, u32[]{:S(2)}) collective-permute-start(bf16[320,384]{1,0:T(8,128)(2,1)} %get-tuple-element.48), channel_id=1, source_target_pairs={{0,1},{1,2},{2,3},{3,4},{4,5},{5,6},{6,7},{7,0},{8,9},{9,10},{10,1... | collective-permute-start | bytes 737288 | tf_op jit(solution)/shard_map/ppermute | solution.py:505
  166.4 19.2 %collective-permute-start.1 = (bf16[320,384]{1,0:T(8,128)(2,1)}, bf16[320,384]{1,0:T(8,128)(2,1)S(1)}, u32[]{:S(2)}, u32[]{:S(2)}) collective-permute-start(bf16[320,384]{1,0:T(8,128)(2,1)} %get-tuple-element.49), channel_id=1, source_target_pairs={{0,2},{1,3},{2,4},{3,5},{4,6},{5,7},{6,0},{7,1},{8,10},{9,11},{10,... | collective-permute-start | bytes 737288 | tf_op jit(solution)/shard_map/ppermute | solution.py:505
  166.4 26.0 %collective-permute-start.2 = (bf16[320,384]{1,0:T(8,128)(2,1)}, bf16[320,384]{1,0:T(8,128)(2,1)S(1)}, u32[]{:S(2)}, u32[]{:S(2)}) collective-permute-start(bf16[320,384]{1,0:T(8,128)(2,1)} %get-tuple-element.50), channel_id=1, source_target_pairs={{0,3},{1,4},{2,5},{3,6},{4,7},{5,0},{6,1},{7,2},{8,11},{9,12},{10,... | collective-permute-start | bytes 737288 | tf_op jit(solution)/shard_map/ppermute | solution.py:505
  168.5 31.8 %collective-permute-start.3 = (bf16[320,384]{1,0:T(8,128)(2,1)}, bf16[320,384]{1,0:T(8,128)(2,1)S(1)}, u32[]{:S(2)}, u32[]{:S(2)}) collective-permute-start(bf16[320,384]{1,0:T(8,128)(2,1)} %get-tuple-element.51), channel_id=1, source_target_pairs={{0,4},{1,5},{2,6},{3,7},{4,0},{5,1},{6,2},{7,3},{8,12},{9,13},{10,... | collective-permute-start | bytes 737288 | tf_op jit(solution)/shard_map/ppermute | solution.py:505
  170.0 31.0 %collective-permute-start.4 = (bf16[320,384]{1,0:T(8,128)(2,1)}, bf16[320,384]{1,0:T(8,128)(2,1)S(1)}, u32[]{:S(2)}, u32[]{:S(2)}) collective-permute-start(bf16[320,384]{1,0:T(8,128)(2,1)} %get-tuple-element.52), channel_id=1, source_target_pairs={{0,5},{1,6},{2,7},{3,0},{4,1},{5,2},{6,3},{7,4},{8,13},{9,14},{10,... | collective-permute-start | bytes 737288 | tf_op jit(solution)/shard_map/ppermute | solution.py:505
  172.6 29.5 %collective-permute-start.5 = (bf16[320,384]{1,0:T(8,128)(2,1)}, bf16[320,384]{1,0:T(8,128)(2,1)S(1)}, u32[]{:S(2)}, u32[]{:S(2)}) collective-permute-start(bf16[320,384]{1,0:T(8,128)(2,1)} %get-tuple-element.53), channel_id=1, source_target_pairs={{0,6},{1,7},{2,0},{3,1},{4,2},{5,3},{6,4},{7,5},{8,14},{9,15},{10,... | collective-permute-start | bytes 737288 | tf_op jit(solution)/shard_map/ppermute | solution.py:505
  185.6 17.1 %collective-permute-start.6 = (bf16[320,384]{1,0:T(8,128)(2,1)}, bf16[320,384]{1,0:T(8,128)(2,1)S(1)}, u32[]{:S(2)}, u32[]{:S(2)}) collective-permute-start(bf16[320,384]{1,0:T(8,128)(2,1)} %get-tuple-element.54), channel_id=1, source_target_pairs={{0,7},{1,0},{2,1},{3,2},{4,3},{5,4},{6,5},{7,6},{8,15},{9,8},{10,9... | collective-permute-start | bytes 737288 | tf_op jit(solution)/shard_map/ppermute | solution.py:505
  202.7 0.9 copy-start.6
  203.7 28.2 %copy-start.9 = (s32[8,1024]{1,0:T(8,128)S(1)}, s32[8,1024]{1,0:T(8,128)}, u32[]{:S(2)}) copy-start(s32[8,1024]{1,0:T(8,128)} %get-tuple-element.57.row_ref) | copy-start | bytes 98308
  206.2 1.0 copy-start.4
  207.2 0.7 copy-start.5
  207.9 23.9 %all-to-all-start.3 = ((bf16[128,8,512]{2,1,0:T(8,128)(2,1)}), bf16[128,8,512]{2,1,0:T(8,128)(2,1)S(1)}, u32[]{:S(2)}, u32[]{:S(2)}) async-start(bf16[128,8,512]{2,1,0:T(8,128)(2,1)} %bitcast.27), calls=%async_computation.3 | async-start | bytes 2097152 | tf_op jit(solution)/shard_map/all_to_all | solution.py:391
Sparse Core Ops, SparseCore 0:
  9.7 32.1 all-gather.7
  64.5 24.5 all-gather.5
  162.9 41.2 all-gather.9

commit v4 on v3

--- a/solution.py
+++ b/solution.py
@@ -87,13 +87,23 @@
     col_ref[...] = jnp.transpose(jnp.broadcast_to(slot, (lanes, count))).astype(i32)
 
 
-def serve_kernel(asked_ref, table_ref, gain_ref, served_ref, row_ref, bounds_ref, mid_ref, col_ref, turn_ref):
+def serve_kernel(
+    asked_ref, table_hbm, gain_ref, served_ref, row_ref, bounds_ref, mid_ref, col_ref, turn_ref, table_ref, sems
+):
     step = pl.program_id(0)
     block = served_ref.shape[0]
     devices, lanes = asked_ref.shape
+    chunks = sems.shape[0]
+    tall = table_ref.shape[0] // chunks
+    loads = [
+        pltpu.make_async_copy(table_hbm.at[pl.ds(c * tall, tall)], table_ref.at[pl.ds(c * tall, tall)], sems.at[c])
+        for c in range(chunks)
+    ]
 
     @pl.when(step == 0)
     def _():
+        for load in loads:
+            load.start()
         asked = asked_ref[...].astype(f32)
         wide = jnp.broadcast_to(asked[:, None, :], (devices, SLOTS, lanes))
         sub = iota((devices, SLOTS, lanes), 1)
@@ -114,10 +124,19 @@
         mid_ref[...] = turn_ref[pl.ds(pl.multiple_of(me * d, d), d), :]
 
     column = col_ref[pl.ds(pl.multiple_of(step * block, block), block), :].astype(i32)
-    parts = []
-    for at in range(table_ref.shape[0] // lanes):
-        parts.append(jnp.where(column == iota((block, lanes), 1) + at * lanes, 1.0, 0.0).astype(bf16))
-    served_ref[...] = mm(jnp.concatenate(parts, axis=1), table_ref[...]).astype(bf16)
+    served = None
+    for c in range(chunks):
+        parts = []
+        for at in range(c * tall, (c + 1) * tall, lanes):
+            parts.append(jnp.where(column == iota((block, lanes), 1) + at, 1.0, 0.0).astype(bf16))
+
+        @pl.when(step == 0)
+        def _():
+            loads[c].wait()
+
+        product = mm(jnp.concatenate(parts, axis=1), table_ref[c * tall : (c + 1) * tall, :])
+        served = product if served is None else served + product
+    served_ref[...] = served.astype(bf16)
 
 
 def arrange_kernel(got_ref, col_ref, gain_ref, fetched_ref, xin_ref):
@@ -340,15 +359,26 @@
 
 def rows_kernel(*refs):
     got = refs[:HEADS]
-    win_ref, gain_ref, fetched_ref, cot_ref, row_ref, out_ref, gated_ref, whole = refs[HEADS:]
+    win_ref, gain_ref, fetched_ref, cot_ref, row_ref, out_hbm, gated_hbm, whole, gated_ref, out_ref, sems = refs[HEADS:]
     d = HEAD_DIM
     width = fetched_ref.shape[1]
     me = lax.axis_index("seq")
-    for s in range(HEADS):
+    own = pl.multiple_of(me * d, d)
+    targets = [whole.at[pl.ds(block * width + own, d)] for block in ORDER] + [gated_ref.at[pl.ds(own, d)]]
+    loads = [
+        pltpu.make_async_copy(got[0].at[pl.ds(at * d, d)], target, sems.at[5 + at]) for at, target in enumerate(targets)
+    ]
+    for load in loads:
+        load.start()
+    for s in range(1, HEADS):
         at_head = pl.multiple_of(lax.rem(me + HEADS - s, HEADS) * d, d)
         for at, block in enumerate(ORDER):
             whole[pl.ds(block * width + at_head, d), :] = got[s][at * d : (at + 1) * d, :]
         gated_ref[pl.ds(at_head, d), :] = got[s][4 * d :, :]
+    for load in loads:
+        load.wait()
+    copies = [pltpu.make_async_copy(gated_ref, gated_hbm, sems.at[0])]
+    copies[0].start()
     dxin = jnp.transpose(mm(win_ref[...], whole[...]))
     normed, inverse = normalize(fetched_ref[...].astype(f32))
     f = dxin * gain_ref[...]
@@ -358,8 +388,15 @@
     drow = drow.astype(bf16)
     slots = out_ref.shape[0]
     count = drow.shape[0]
-    pick = jnp.where(row_ref[0:1, :] == iota((slots, count), 0), 1.0, 0.0).astype(bf16)
-    out_ref[...] = mm(pick, drow).astype(bf16)
+    block = slots // 4
+    for at in range(4):
+        pick = jnp.where(row_ref[0:1, :] == iota((block, count), 0) + at * block, 1.0, 0.0).astype(bf16)
+        here = pl.ds(at * block, block)
+        out_ref[here, :] = mm(pick, drow).astype(bf16)
+        copies.append(pltpu.make_async_copy(out_ref.at[here], out_hbm.at[here], sems.at[at + 1]))
+        copies[-1].start()
+    for copy in copies:
+        copy.wait()
 
 
 def table_kernel(row_ref, got_ref, out_ref):
@@ -423,11 +460,14 @@
         (struct((slots, width), bf16), struct((8, slots), i32), struct((8, 128), i32), struct((d, 128), f32)),
         (asked, item_table, gain_mid.reshape(1, width)),
         grid=(steps,),
-        in_specs=[whole(devices, 128), whole(shard_rows, width), whole(1, width)],
+        in_specs=[whole(devices, 128), pl.BlockSpec(memory_space=pl.ANY), whole(1, width)],
         out_specs=[
             pl.BlockSpec((slots // steps, width), lambda g: (g, 0)), whole(8, slots), whole(8, 128), whole(d, 128),
         ],
-        scratch=[pltpu.VMEM((slots, 128), f32), pltpu.VMEM((width, 128), f32)],
+        scratch=[
+            pltpu.VMEM((slots, 128), f32), pltpu.VMEM((width, 128), f32), pltpu.VMEM((shard_rows, width), bf16),
+            pltpu.SemaphoreType.DMA((4,)),
+        ],
         flops=2 * slots * shard_rows * width, moved=4 << 20,
     )
     got = exchange(served.reshape(devices, SLOTS, width), BOTH).reshape(slots, width)
@@ -510,9 +550,14 @@
     dw_all = lax.all_gather(dw_head, "seq", axis=0, tiled=False)
     outgoing, gated_mine = call(
         rows_kernel,
-        (struct((slots, width), bf16), struct((width, count), bf16)),
+        (pltpu.HBM((slots, width), bf16), pltpu.HBM((width, count), bf16)),
         (*pieces, weight_in, gain_row, fetched, upstream, slot_row),
-        mib=24, in_specs=[pl.BlockSpec(memory_space=pltpu.VMEM)] * (HEADS + 5), scratch=[pltpu.VMEM((4 * width, count), bf16)],
+        mib=24, in_specs=[pl.BlockSpec(memory_space=pl.ANY)] + [pl.BlockSpec(memory_space=pltpu.VMEM)] * (HEADS + 4),
+        out_specs=[pl.BlockSpec(memory_space=pltpu.HBM)] * 2,
+        scratch=[
+            pltpu.VMEM((4 * width, count), bf16), pltpu.VMEM((width, count), bf16), pltpu.VMEM((slots, width), bf16),
+            pltpu.SemaphoreType.DMA((10,)),
+        ],
         flops=2 * count * width * 4 * width, moved=6 << 20,
     )
     layer = (

time: 250 us -> 250 us (level)
    unnamed x21 -> x17, local copies, waits for them, and re-layouts: 5.19 us -> 3.48 us
  transfers between devices with their start and end apart: 11 -> 11, of which waited for: 8 -> 8; matrix products, arithmetic and copies ran while one was open for 4% -> 4% of each run, Pallas kernels for 7% -> 8%
where the time goes in v4:
time: 250 us; the launch traced here: 249 us
  blocking collectives  91.2 us (36%)
  waiting for transfers between devices  62.5 us (25%)
  Pallas kernels  52.8 us (21%)
  starting transfers between devices  16.4 us (7%)
  between operations  13.9 us (6%)
  matrix products  6.12 us (2%)
  local copies, waits for them, and re-layouts  4.5 us (2%)
    all_to_all x5, blocking collectives, exchange(): return lax.all_to_all(x, axis, split_axis=0, concat_axis=0, tiled=True)  91.2 us
    pallas_call x7, Pallas kernels, call(): pl.pallas_call(kernel, out_shape=out_shape, scratch_shapes=scratch, compi...  35.8 us
    ppermute x7, waiting for transfers between devices, layer_step(): lax.ppermute(result[s], 'seq', [(i, (i + s) % seq) for i in range(seq)])  28.5 us
    pallas_call x1, Pallas kernels, layer_step(): pl.pallas_call(functools.partial(backward_kernel, blocks), out_shape=[str...  16.9 us
    all_to_all x1, waiting for transfers between devices, exchange(): return lax.all_to_all(x, axis, split_axis=0, concat_axis=0, tiled=True)  16.9 us
    all_gather x1, waiting for transfers between devices, layer_step(): xin_all = lax.all_gather(xin, 'seq', axis=0, tiled=True)  16.4 us
    ppermute x7, starting transfers between devices, layer_step(): lax.ppermute(result[s], 'seq', [(i, (i + s) % seq) for i in range(seq)])  11.4 us
  transfers between devices with their start and end apart: 11, of which 8 were waited for; matrix products, arithmetic and copies ran while one was open for 4% of the time, Pallas kernels for 8%

profile of v4, /device:TPU:1, one launch (start us, length us, event | category | flops | bytes accessed | tf_op | source)
XLA Modules:
  0.0 249.3 jit_solution(8964969425643049654)
XLA Ops:
  9.8 21.2 %all_to_all.30 = s32[128,1,128]{2,1,0:T(1,128)} all-to-all(s32[128,1,128]{2,1,0:T(1,128)} %bitcast.38), channel_id=1, replica_groups=mesh['users'=16,'seq'=8] {'users','seq'}, dimensions={0} | all-to-all | bytes 131072 | tf_op jit(solution)/shard_map/all_to_all | solution.py:428
  31.0 6.9 %shard_map.112 = (bf16[1024,512]{1,0:T(8,128)(2,1)}, s32[8,1024]{1,0:T(8,128)}, s32[8,128]{1,0:T(8,128)}, f32[64,128]{1,0:T(8,128)}) custom-call(s32[128,128]{1,0:T(8,128)} %bitcast.37, bf16[2048,512]{1,0:T(8,128)(2,1)} %table_hbm.1, f32[1,512]{1,0:T(1,128)} %bitcast.40), custom_call_target="tpu_custom_call" | custom-call | flops 2147483648 | bytes 4194304 | tf_op jit(solution)/shard_map/pallas_call | solution.py:47
  37.9 25.1 %all_to_all.31 = bf16[128,8,512]{2,1,0:T(8,128)(2,1)} all-to-all(bf16[128,8,512]{2,1,0:T(8,128)(2,1)} %bitcast.34), channel_id=1, replica_groups=mesh['users'=16,'seq'=8] {'users','seq'}, dimensions={0} | all-to-all | bytes 2097152 | tf_op jit(solution)/shard_map/all_to_all | solution.py:428
  62.9 2.8 %shard_map.113 = (bf16[384,512]{1,0:T(8,128)(2,1)}, bf16[384,512]{1,0:T(8,128)(2,1)}) custom-call(bf16[1024,512]{1,0:T(8,128)(2,1)} %bitcast.35, s32[384,128]{1,0:T(8,128)} %get-tuple-element.35.col_ref, f32[1,512]{1,0:T(1,128)} %bitcast.28), custom_call_target="tpu_custom_call" | custom-call | flops 402653184 | bytes 2097152 | tf_op jit(solution)/shard_map/pallas_call | solution.py:47
  65.8 2.5 %copy.15 = bf16[512,2048]{0,1:T(8,128)(2,1)} copy(bf16[512,2048]{1,0:T(8,128)(2,1)S(1)} %copy-done.1) | data formatting | bytes 4194304 | tf_op args[3]
  70.1 4.0 %fusion.2.dg_ref = f32[64,3072]{1,0:T(8,128)} fusion(bf16[512,512]{1,0:T(8,128)(2,1)S(1)} %copy-done, s32[]{:T(128)S(6)} %select_n.7, bf16[1,3072,512]{2,1,0:T(8,128)(2,1)} %all-gather.8.cloned.1.call-done), kind=kOutput, calls=%fused_computation.5 | convolution fusion | flops 201326592 | bytes 3997700 | tf_op jit(solution)/shard_map/dot_general | solution.py:34
  74.1 16.4 %all-gather.6.cloned.1.call-done.xin_ref.xin_hbm = bf16[3072,512]{1,0:T(8,128)(2,1)} async-done(((bf16[384,512]{1,0:T(8,128)(2,1)}), bf16[3072,512]{1,0:T(8,128)(2,1)}) %all-gather.6.cloned.1.call-update) | async-done | bytes 3145744 | tf_op jit(solution)/shard_map/all_gather | solution.py:480
  90.5 10.4 %shard_map.114 = (bf16[64,3072]{1,0:T(8,128)(2,1)}, bf16[64,3072]{1,0:T(8,128)(2,1)}, bf16[3072,128]{1,0:T(8,128)(2,1)}, f32[256,3072]{1,0:T(8,128)}, f32[64,307...) custom-call(bf16[3072,512]{1,0:T(8,128)(2,1)} %all-gather.6.cloned.1.call-done.xin_ref.xin_hbm, ...), custom_call_target="tpu_custom_call" | custom-call | flops 8589934592 | bytes 12582912 | tf_op jit(solution)/shard_map/pallas_call | solution.py:47
  100.9 12.4 %all_to_all.32.stats_ref = f32[8,4,3072]{2,1,0:T(4,128)} all-to-all(f32[8,4,3072]{2,1,0:T(4,128)} %get-tuple-element.43), channel_id=1, replica_groups=mesh['users'=16,'seq'=8] {'seq'}, dimensions={0} | all-to-all | bytes 786432 | tf_op jit(solution)/shard_map/all_to_all | solution.py:428
  113.3 16.9 %backward.1 = (bf16[320,384]{1,0:T(8,128)(2,1)}, bf16[320,384]{1,0:T(8,128)(2,1)}, bf16[320,384]{1,0:T(8,128)(2,1)}, bf16[320,384]{1,0:T(8,128)(2,1)}, bf16[320,...) custom-call(s32[8,128]{1,0:T(8,128)} %get-tuple-element.37.bounds_re, ...), custom_call_target="tpu_custom_call" | custom-call | flops 34359738368 | bytes 16777216 | tf_op jit(solution)/shard_map/backward/pallas_call | solution.py:512
  130.3 21.4 %all_to_all.33 = f32[16,40,256]{2,1,0:T(8,128)} all-to-all(f32[16,40,256]{2,1,0:T(8,128)} %get-tuple-element.59), channel_id=1, replica_groups=mesh['users'=16,'seq'=8] {'users'}, dimensions={0} | all-to-all | bytes 1310720 | tf_op jit(solution)/shard_map/all_to_all | solution.py:428
  152.9 11.2 %all_to_all.34 = bf16[16,40,256]{2,1,0:T(8,128)(2,1)} all-to-all(bf16[16,40,256]{2,1,0:T(8,128)(2,1)S(1)} %broadcast_in_dim.10), channel_id=1, replica_groups=mesh['users'=16,'seq'=8] {'users'}, dimensions={0} | all-to-all | bytes 655360 | tf_op jit(solution)/shard_map/all_to_all | solution.py:428
  164.1 3.6 %collective-permute-start = (bf16[320,384]{1,0:T(8,128)(2,1)}, bf16[320,384]{1,0:T(8,128)(2,1)S(1)}, u32[]{:S(2)}, u32[]{:S(2)}) collective-permute-start(bf16[320,384]{1,0:T(8,128)(2,1)} %get-tuple-element.48), channel_id=1, source_target_pairs={{0,1},{1,2},{2,3},{3,4},{4,5},{5,6},{6,7},{7,0},{8,9},{9,10},{10,1... | collective-permute-start | bytes 737288 | tf_op jit(solution)/shard_map/ppermute | solution.py:545
  167.7 2.1 collective-permute-start.2
  171.3 2.6 %collective-permute-start.4 = (bf16[320,384]{1,0:T(8,128)(2,1)}, bf16[320,384]{1,0:T(8,128)(2,1)S(1)}, u32[]{:S(2)}, u32[]{:S(2)}) collective-permute-start(bf16[320,384]{1,0:T(8,128)(2,1)} %get-tuple-element.52), channel_id=1, source_target_pairs={{0,5},{1,6},{2,7},{3,0},{4,1},{5,2},{6,3},{7,4},{8,13},{9,14},{10,... | collective-permute-start | bytes 737288 | tf_op jit(solution)/shard_map/ppermute | solution.py:545
  175.5 11.4 %collective-permute-done.1.refs_2_ = bf16[320,384]{1,0:T(8,128)(2,1)S(1)} collective-permute-done((bf16[320,384]{1,0:T(8,128)(2,1)}, bf16[320,384]{1,0:T(8,128)(2,1)S(1)}, u32[]{:S(2)}, u32[]{:S(2)}) %collective-permute-start.1) | collective-permute-done | bytes 245792 | tf_op jit(solution)/shard_map/ppermute | solution.py:545
  186.9 6.8 %collective-permute-done.2.refs_3_ = bf16[320,384]{1,0:T(8,128)(2,1)S(1)} collective-permute-done((bf16[320,384]{1,0:T(8,128)(2,1)}, bf16[320,384]{1,0:T(8,128)(2,1)S(1)}, u32[]{:S(2)}, u32[]{:S(2)}) %collective-permute-start.2) | collective-permute-done | bytes 245792 | tf_op jit(solution)/shard_map/ppermute | solution.py:545
  193.7 7.9 %collective-permute-done.3.refs_4_ = bf16[320,384]{1,0:T(8,128)(2,1)S(1)} collective-permute-done((bf16[320,384]{1,0:T(8,128)(2,1)}, bf16[320,384]{1,0:T(8,128)(2,1)S(1)}, u32[]{:S(2)}, u32[]{:S(2)}) %collective-permute-start.3) | collective-permute-done | bytes 245792 | tf_op jit(solution)/shard_map/ppermute | solution.py:545
  205.0 3.7 %shard_map.115 = (bf16[1024,512]{1,0:T(8,128)(2,1)}, bf16[512,384]{1,0:T(8,128)(2,1)}) custom-call(bf16[320,384]{1,0:T(8,128)(2,1)S(1)} %copy-done.4, bf16[320,384]{1,0:T(8,128)(2,1)S(1)} %collective-permute-done.refs_1_, bf16[320,384]{1,0:T(8,128)(2,1)S(1)} %collective-permute-done.1.refs_2_, bf16[320,384]{1,0:T(8,128)(2,1)S(1)} %collective-permute-done.2.refs_3_, ...), custom_call_target="tpu_custom_call" | custom-call | flops 805306368 | bytes 6291456 | tf_op jit(solution)/shard_map/pallas_call | solution.py:47
  208.7 4.9 %all-to-all-start.3 = ((bf16[128,8,512]{2,1,0:T(8,128)(2,1)}), bf16[128,8,512]{2,1,0:T(8,128)(2,1)S(1)}, u32[]{:S(2)}, u32[]{:S(2)}) async-start(bf16[128,8,512]{2,1,0:T(8,128)(2,1)} %bitcast.33), calls=%async_computation.3 | async-start | bytes 2097152 | tf_op jit(solution)/shard_map/all_to_all | solution.py:428
  213.6 2.1 fusion.1
  215.7 16.9 %all-to-all-done.3 = bf16[128,8,512]{2,1,0:T(8,128)(2,1)S(1)} async-done(((bf16[128,8,512]{2,1,0:T(8,128)(2,1)}), bf16[128,8,512]{2,1,0:T(8,128)(2,1)S(1)}, u32[]{:S(2)}, u32[]{:S(2)}) %all-to-all-start.3) | async-done | bytes 1048608 | tf_op jit(solution)/shard_map/all_to_all | solution.py:428
  232.6 5.4 %shard_map.116 = f32[2048,512]{1,0:T(8,128)} custom-call(s32[8,1024]{1,0:T(8,128)S(1)} %copy-done.7, bf16[1024,512]{1,0:T(8,128)(2,1)S(1)} %bitcast.27), custom_call_target="tpu_custom_call" | custom-call | flops 2147483648 | bytes 6291456 | tf_op jit(solution)/shard_map/pallas_call | solution.py:47
  238.0 4.8 %shard_map.117 = (f32[512,2048]{1,0:T(8,128)}, f32[8,8,8,512]{3,2,1,0:T(8,128)}) custom-call(bf16[8,16,40,256]{3,2,1,0:T(8,128)(2,1)} %bitcast.32), custom_call_target="tpu_custom_call" | custom-call | flops 1048576 | bytes 8388608 | tf_op jit(solution)/shard_map/pallas_call | solution.py:47
  (38 shorter events, 12.0 us)
Async XLA Ops:
  7.2 62.9 %copy-start = (bf16[512,512]{1,0:T(8,128)(2,1)S(1)}, bf16[512,512]{1,0:T(8,128)(2,1)}, u32[]{:S(2)}) copy-start(bf16[512,512]{1,0:T(8,128)(2,1)} %param.12) | copy-start | bytes 1572868
  7.2 62.9 %all-gather.8.cloned.1.call-start = ((), (), s32[]{:S(2)}) async-start(), calls=%async_computation.7 | async-start | bytes 3538944 | tf_op jit(solution)/shard_map/all_gather | solution.py:447
  7.9 82.6 %all-gather.6.cloned.1.call-start = ((), (), s32[]{:S(2)}) async-start(), calls=%async_computation.6 | async-start | bytes 3538944 | tf_op jit(solution)/shard_map/all_gather | solution.py:480
  37.8 28.0 %copy-start.1 = (bf16[512,2048]{1,0:T(8,128)(2,1)S(1)}, bf16[512,2048]{1,0:T(8,128)(2,1)}, u32[]{:S(2)}) copy-start(bf16[512,2048]{1,0:T(8,128)(2,1)} %refs_8_.1) | copy-start | bytes 6291460
  65.8 172.2 %all-gather.10.cloned.1.call-start = ((), (), s32[]{:S(2)}) async-start(), calls=%async_computation.8 | async-start | bytes 2949120 | tf_op jit(solution)/shard_map/all_gather | solution.py:550
  130.2 73.8 %copy-start.2 = (bf16[1,384,512]{2,1,0:T(8,128)(2,1)S(1)}, bf16[1,384,512]{2,1,0:T(8,128)(2,1)}, u32[]{:S(2)}) copy-start(bf16[1,384,512]{2,1,0:T(8,128)(2,1)} %param.15) | copy-start | bytes 1179652
  130.2 73.8 %copy-start.3 = (bf16[384,512]{1,0:T(8,128)(2,1)S(1)}, bf16[384,512]{1,0:T(8,128)(2,1)}, u32[]{:S(2)}) copy-start(bf16[384,512]{1,0:T(8,128)(2,1)} %get-tuple-element.36.refs_10_) | copy-start | bytes 1179652
  130.3 73.8 %copy-start.5 = (s32[8,384]{1,0:T(8,128)S(1)}, s32[8,384]{1,0:T(8,128)}, u32[]{:S(2)}) copy-start(s32[8,384]{1,0:T(8,128)} %get-tuple-element.55.refs_12_) | copy-start | bytes 36868
  130.3 73.8 %copy-start.6 = (f32[512]{0:T(512)S(1)}, f32[512]{0:T(512)}, u32[]{:S(2)}) copy-start(f32[512]{0:T(512)} %param.13) | copy-start | bytes 6148
  164.1 9.8 %collective-permute-start = (bf16[320,384]{1,0:T(8,128)(2,1)}, bf16[320,384]{1,0:T(8,128)(2,1)S(1)}, u32[]{:S(2)}, u32[]{:S(2)}) collective-permute-start(bf16[320,384]{1,0:T(8,128)(2,1)} %get-tuple-element.48), channel_id=1, source_target_pairs={{0,1},{1,2},{2,3},{3,4},{4,5},{5,6},{6,7},{7,0},{8,9},{9,10},{10,1... | collective-permute-start | bytes 737288 | tf_op jit(solution)/shard_map/ppermute | solution.py:545
  167.7 19.2 %collective-permute-start.1 = (bf16[320,384]{1,0:T(8,128)(2,1)}, bf16[320,384]{1,0:T(8,128)(2,1)S(1)}, u32[]{:S(2)}, u32[]{:S(2)}) collective-permute-start(bf16[320,384]{1,0:T(8,128)(2,1)} %get-tuple-element.49), channel_id=1, source_target_pairs={{0,2},{1,3},{2,4},{3,5},{4,6},{5,7},{6,0},{7,1},{8,10},{9,11},{10,... | collective-permute-start | bytes 737288 | tf_op jit(solution)/shard_map/ppermute | solution.py:545
  167.7 26.0 %collective-permute-start.2 = (bf16[320,384]{1,0:T(8,128)(2,1)}, bf16[320,384]{1,0:T(8,128)(2,1)S(1)}, u32[]{:S(2)}, u32[]{:S(2)}) collective-permute-start(bf16[320,384]{1,0:T(8,128)(2,1)} %get-tuple-element.50), channel_id=1, source_target_pairs={{0,3},{1,4},{2,5},{3,6},{4,7},{5,0},{6,1},{7,2},{8,11},{9,12},{10,... | collective-permute-start | bytes 737288 | tf_op jit(solution)/shard_map/ppermute | solution.py:545
  169.8 31.8 %collective-permute-start.3 = (bf16[320,384]{1,0:T(8,128)(2,1)}, bf16[320,384]{1,0:T(8,128)(2,1)S(1)}, u32[]{:S(2)}, u32[]{:S(2)}) collective-permute-start(bf16[320,384]{1,0:T(8,128)(2,1)} %get-tuple-element.51), channel_id=1, source_target_pairs={{0,4},{1,5},{2,6},{3,7},{4,0},{5,1},{6,2},{7,3},{8,12},{9,13},{10,... | collective-permute-start | bytes 737288 | tf_op jit(solution)/shard_map/ppermute | solution.py:545
  171.3 31.0 %collective-permute-start.4 = (bf16[320,384]{1,0:T(8,128)(2,1)}, bf16[320,384]{1,0:T(8,128)(2,1)S(1)}, u32[]{:S(2)}, u32[]{:S(2)}) collective-permute-start(bf16[320,384]{1,0:T(8,128)(2,1)} %get-tuple-element.52), channel_id=1, source_target_pairs={{0,5},{1,6},{2,7},{3,0},{4,1},{5,2},{6,3},{7,4},{8,13},{9,14},{10,... | collective-permute-start | bytes 737288 | tf_op jit(solution)/shard_map/ppermute | solution.py:545
  173.9 29.5 %collective-permute-start.5 = (bf16[320,384]{1,0:T(8,128)(2,1)}, bf16[320,384]{1,0:T(8,128)(2,1)S(1)}, u32[]{:S(2)}, u32[]{:S(2)}) collective-permute-start(bf16[320,384]{1,0:T(8,128)(2,1)} %get-tuple-element.53), channel_id=1, source_target_pairs={{0,6},{1,7},{2,0},{3,1},{4,2},{5,3},{6,4},{7,5},{8,14},{9,15},{10,... | collective-permute-start | bytes 737288 | tf_op jit(solution)/shard_map/ppermute | solution.py:545
  186.9 17.1 %collective-permute-start.6 = (bf16[320,384]{1,0:T(8,128)(2,1)}, bf16[320,384]{1,0:T(8,128)(2,1)S(1)}, u32[]{:S(2)}, u32[]{:S(2)}) collective-permute-start(bf16[320,384]{1,0:T(8,128)(2,1)} %get-tuple-element.54), channel_id=1, source_target_pairs={{0,7},{1,0},{2,1},{3,2},{4,3},{5,4},{6,5},{7,6},{8,15},{9,8},{10,9... | collective-permute-start | bytes 737288 | tf_op jit(solution)/shard_map/ppermute | solution.py:545
  204.1 0.9 copy-start.4
  205.0 27.6 %copy-start.7 = (s32[8,1024]{1,0:T(8,128)S(1)}, s32[8,1024]{1,0:T(8,128)}, u32[]{:S(2)}) copy-start(s32[8,1024]{1,0:T(8,128)} %get-tuple-element.57.row_ref) | copy-start | bytes 98308
  208.7 23.9 %all-to-all-start.3 = ((bf16[128,8,512]{2,1,0:T(8,128)(2,1)}), bf16[128,8,512]{2,1,0:T(8,128)(2,1)S(1)}, u32[]{:S(2)}, u32[]{:S(2)}) async-start(bf16[128,8,512]{2,1,0:T(8,128)(2,1)} %bitcast.33), calls=%async_computation.3 | async-start | bytes 2097152 | tf_op jit(solution)/shard_map/all_to_all | solution.py:428
Sparse Core Ops, SparseCore 0:
  9.7 32.1 all-gather.7
  65.9 24.5 all-gather.5
  164.2 41.2 all-gather.9

commit v5 on v3

--- a/solution.py
+++ b/solution.py
@@ -120,7 +120,7 @@
     served_ref[...] = mm(jnp.concatenate(parts, axis=1), table_ref[...]).astype(bf16)
 
 
-def arrange_kernel(got_ref, col_ref, gain_ref, fetched_ref, xin_ref):
+def arrange_kernel(got_ref, col_ref, gain_ref, fetched_hbm, xin_hbm, fetched_ref, xin_ref, sems):
     slot = col_ref[...]
     count, lanes = slot.shape
     parts = []
@@ -130,6 +130,13 @@
     fetched_ref[...] = fetched.astype(bf16)
     normed, _ = normalize(fetched)
     xin_ref[...] = (normed * gain_ref[...]).astype(bf16)
+    copies = [
+        pltpu.make_async_copy(xin_ref, xin_hbm, sems.at[0]), pltpu.make_async_copy(fetched_ref, fetched_hbm, sems.at[1]),
+    ]
+    for copy in copies:
+        copy.start()
+    for copy in copies:
+        copy.wait()
 
 
 def seg_start(position, one, two):
@@ -340,15 +347,26 @@
 
 def rows_kernel(*refs):
     got = refs[:HEADS]
-    win_ref, gain_ref, fetched_ref, cot_ref, row_ref, out_ref, gated_ref, whole = refs[HEADS:]
+    win_ref, gain_ref, fetched_ref, cot_ref, row_ref, out_hbm, gated_hbm, whole, gated_ref, out_ref, sems = refs[HEADS:]
     d = HEAD_DIM
     width = fetched_ref.shape[1]
     me = lax.axis_index("seq")
-    for s in range(HEADS):
+    own = pl.multiple_of(me * d, d)
+    targets = [whole.at[pl.ds(block * width + own, d)] for block in ORDER] + [gated_ref.at[pl.ds(own, d)]]
+    loads = [
+        pltpu.make_async_copy(got[0].at[pl.ds(at * d, d)], target, sems.at[5 + at]) for at, target in enumerate(targets)
+    ]
+    for load in loads:
+        load.start()
+    for s in range(1, HEADS):
         at_head = pl.multiple_of(lax.rem(me + HEADS - s, HEADS) * d, d)
         for at, block in enumerate(ORDER):
             whole[pl.ds(block * width + at_head, d), :] = got[s][at * d : (at + 1) * d, :]
         gated_ref[pl.ds(at_head, d), :] = got[s][4 * d :, :]
+    for load in loads:
+        load.wait()
+    copies = [pltpu.make_async_copy(gated_ref, gated_hbm, sems.at[0])]
+    copies[0].start()
     dxin = jnp.transpose(mm(win_ref[...], whole[...]))
     normed, inverse = normalize(fetched_ref[...].astype(f32))
     f = dxin * gain_ref[...]
@@ -358,8 +376,15 @@
     drow = drow.astype(bf16)
     slots = out_ref.shape[0]
     count = drow.shape[0]
-    pick = jnp.where(row_ref[0:1, :] == iota((slots, count), 0), 1.0, 0.0).astype(bf16)
-    out_ref[...] = mm(pick, drow).astype(bf16)
+    block = slots // 4
+    for at in range(4):
+        pick = jnp.where(row_ref[0:1, :] == iota((block, count), 0) + at * block, 1.0, 0.0).astype(bf16)
+        here = pl.ds(at * block, block)
+        out_ref[here, :] = mm(pick, drow).astype(bf16)
+        copies.append(pltpu.make_async_copy(out_ref.at[here], out_hbm.at[here], sems.at[at + 1]))
+        copies[-1].start()
+    for copy in copies:
+        copy.wait()
 
 
 def table_kernel(row_ref, got_ref, out_ref):
@@ -433,9 +458,13 @@
     got = exchange(served.reshape(devices, SLOTS, width), BOTH).reshape(slots, width)
     fetched, xin = call(
         arrange_kernel,
-        (struct((count, width), bf16), struct((count, width), bf16)),
+        (pltpu.HBM((count, width), bf16), pltpu.HBM((count, width), bf16)),
         (got, slot_col, gain_row),
-        flops=2 * count * slots * width, moved=2 << 20,
+        mib=24, in_specs=[pl.BlockSpec(memory_space=pltpu.VMEM)] * 3,
+        out_specs=[pl.BlockSpec(memory_space=pltpu.HBM)] * 2,
+        scratch=[
+            pltpu.VMEM((count, width), bf16), pltpu.VMEM((count, width), bf16), pltpu.SemaphoreType.DMA((2,)),
+        ], flops=2 * count * slots * width, moved=2 << 20,
     )
     xin_all = lax.all_gather(xin, "seq", axis=0, tiled=True)
 
@@ -510,9 +539,14 @@
     dw_all = lax.all_gather(dw_head, "seq", axis=0, tiled=False)
     outgoing, gated_mine = call(
         rows_kernel,
-        (struct((slots, width), bf16), struct((width, count), bf16)),
-        (*pieces, weight_in, gain_row, fetched, upstream, slot_row),
-        mib=24, in_specs=[pl.BlockSpec(memory_space=pltpu.VMEM)] * (HEADS + 5), scratch=[pltpu.VMEM((4 * width, count), bf16)],
+        (pltpu.HBM((slots, width), bf16), pltpu.HBM((width, count), bf16)),
+        (pltpu.with_memory_space_constraint(pieces[0], pltpu.HBM), *pieces[1:], weight_in, gain_row, fetched, upstream, slot_row),
+        mib=24, in_specs=[pl.BlockSpec(memory_space=pltpu.HBM)] + [pl.BlockSpec(memory_space=pltpu.VMEM)] * (HEADS + 4),
+        out_specs=[pl.BlockSpec(memory_space=pltpu.HBM)] * 2,
+        scratch=[
+            pltpu.VMEM((4 * width, count), bf16), pltpu.VMEM((width, count), bf16), pltpu.VMEM((slots, width), bf16),
+            pltpu.SemaphoreType.DMA((10,)),
+        ],
         flops=2 * count * width * 4 * width, moved=6 << 20,
     )
     layer = (

time: 250 us -> 247 us (0.988)
  local copies, waits for them, and re-layouts: 6.2 us -> 3.56 us
    unnamed x21 -> x17, local copies, waits for them, and re-layouts: 5.19 us -> 2.55 us
  transfers between devices with their start and end apart: 11 -> 11, of which waited for: 8 -> 8; matrix products, arithmetic and copies ran while one was open for 4% -> 4% of each run, Pallas kernels for 7% -> 8%
where the time goes in v5:
time: 247 us; the launch traced here: 246 us
  blocking collectives  90.6 us (37%)
  waiting for transfers between devices  62.5 us (25%)
  Pallas kernels  50.9 us (21%)
  starting transfers between devices  16.4 us (7%)
  between operations  13.9 us (6%)
  matrix products  6.12 us (2%)
  local copies, waits for them, and re-layouts  3.56 us (1%)
    all_to_all x5, blocking collectives, exchange(): return lax.all_to_all(x, axis, split_axis=0, concat_axis=0, tiled=True)  90.6 us
    pallas_call x7, Pallas kernels, call(): pl.pallas_call(kernel, out_shape=out_shape, scratch_shapes=scratch, compi...  33.9 us
    ppermute x7, waiting for transfers between devices, layer_step(): lax.ppermute(result[s], 'seq', [(i, (i + s) % seq) for i in range(seq)])  28.5 us
    pallas_call x1, Pallas kernels, layer_step(): pl.pallas_call(functools.partial(backward_kernel, blocks), out_shape=[str...  16.9 us
    all_to_all x1, waiting for transfers between devices, exchange(): return lax.all_to_all(x, axis, split_axis=0, concat_axis=0, tiled=True)  16.9 us
    all_gather x1, waiting for transfers between devices, layer_step(): xin_all = lax.all_gather(xin, 'seq', axis=0, tiled=True)  16.4 us
    ppermute x7, starting transfers between devices, layer_step(): lax.ppermute(result[s], 'seq', [(i, (i + s) % seq) for i in range(seq)])  11.4 us
  transfers between devices with their start and end apart: 11, of which 8 were waited for; matrix products, arithmetic and copies ran while one was open for 4% of the time, Pallas kernels for 8%

profile of v5, /device:TPU:1, one launch (start us, length us, event | category | flops | bytes accessed | tf_op | source)
XLA Modules:
  0.0 245.9 jit_solution(5853150710545925527)
XLA Ops:
  8.0 1.8 shard_map.111
  9.8 21.2 %all_to_all.30 = s32[128,1,128]{2,1,0:T(1,128)} all-to-all(s32[128,1,128]{2,1,0:T(1,128)} %bitcast.38), channel_id=1, replica_groups=mesh['users'=16,'seq'=8] {'users','seq'}, dimensions={0} | all-to-all | bytes 131072 | tf_op jit(solution)/shard_map/all_to_all | solution.py:416
  31.0 5.7 %shard_map.112 = (bf16[1024,512]{1,0:T(8,128)(2,1)}, s32[8,1024]{1,0:T(8,128)}, s32[8,128]{1,0:T(8,128)}, f32[64,128]{1,0:T(8,128)}) custom-call(s32[128,128]{1,0:T(8,128)} %bitcast.37, bf16[2048,512]{1,0:T(8,128)(2,1)} %table_ref.1, f32[1,512]{1,0:T(1,128)} %bitcast.40), custom_call_target="tpu_custom_call" | custom-call | flops 2147483648 | bytes 4194304 | tf_op jit(solution)/shard_map/pallas_call | solution.py:47
  36.7 24.4 %all_to_all.31 = bf16[128,8,512]{2,1,0:T(8,128)(2,1)S(1)} all-to-all(bf16[128,8,512]{2,1,0:T(8,128)(2,1)} %bitcast.35), channel_id=1, replica_groups=mesh['users'=16,'seq'=8] {'users','seq'}, dimensions={0} | all-to-all | bytes 2097152 | tf_op jit(solution)/shard_map/all_to_all | solution.py:416
  62.9 2.5 %copy.15 = bf16[512,2048]{0,1:T(8,128)(2,1)} copy(bf16[512,2048]{1,0:T(8,128)(2,1)S(1)} %copy-done.1) | data formatting | bytes 4194304 | tf_op args[3]
  67.1 4.0 %fusion.2.dg_ref = f32[64,3072]{1,0:T(8,128)} fusion(bf16[512,512]{1,0:T(8,128)(2,1)S(1)} %copy-done, s32[]{:T(128)S(6)} %select_n.7, bf16[1,3072,512]{2,1,0:T(8,128)(2,1)} %all-gather.8.cloned.1.call-done), kind=kOutput, calls=%fused_computation.5 | convolution fusion | flops 201326592 | bytes 3997700 | tf_op jit(solution)/shard_map/dot_general | solution.py:34
  71.1 16.4 %all-gather.6.cloned.1.call-done.xin_ref.xin_hbm = bf16[3072,512]{1,0:T(8,128)(2,1)} async-done(((bf16[384,512]{1,0:T(8,128)(2,1)}), bf16[3072,512]{1,0:T(8,128)(2,1)}) %all-gather.6.cloned.1.call-update) | async-done | bytes 3145744 | tf_op jit(solution)/shard_map/all_gather | solution.py:469
  87.5 10.4 %shard_map.114 = (bf16[64,3072]{1,0:T(8,128)(2,1)}, bf16[64,3072]{1,0:T(8,128)(2,1)}, bf16[3072,128]{1,0:T(8,128)(2,1)}, f32[256,3072]{1,0:T(8,128)}, f32[64,307...) custom-call(bf16[3072,512]{1,0:T(8,128)(2,1)} %all-gather.6.cloned.1.call-done.xin_ref.xin_hbm, ...), custom_call_target="tpu_custom_call" | custom-call | flops 8589934592 | bytes 12582912 | tf_op jit(solution)/shard_map/pallas_call | solution.py:47
  97.9 12.4 %all_to_all.32.stats_ref = f32[8,4,3072]{2,1,0:T(4,128)} all-to-all(f32[8,4,3072]{2,1,0:T(4,128)} %get-tuple-element.43), channel_id=1, replica_groups=mesh['users'=16,'seq'=8] {'seq'}, dimensions={0} | all-to-all | bytes 786432 | tf_op jit(solution)/shard_map/all_to_all | solution.py:416
  110.3 16.9 %backward.1 = (bf16[320,384]{1,0:T(8,128)(2,1)}, bf16[320,384]{1,0:T(8,128)(2,1)}, bf16[320,384]{1,0:T(8,128)(2,1)}, bf16[320,384]{1,0:T(8,128)(2,1)}, bf16[320,...) custom-call(s32[8,128]{1,0:T(8,128)} %get-tuple-element.37.bounds_re, ...), custom_call_target="tpu_custom_call" | custom-call | flops 34359738368 | bytes 16777216 | tf_op jit(solution)/shard_map/backward/pallas_call | solution.py:501
  127.3 21.4 %all_to_all.33 = f32[16,40,256]{2,1,0:T(8,128)} all-to-all(f32[16,40,256]{2,1,0:T(8,128)} %get-tuple-element.59), channel_id=1, replica_groups=mesh['users'=16,'seq'=8] {'users'}, dimensions={0} | all-to-all | bytes 1310720 | tf_op jit(solution)/shard_map/all_to_all | solution.py:416
  149.9 11.2 %all_to_all.34 = bf16[16,40,256]{2,1,0:T(8,128)(2,1)} all-to-all(bf16[16,40,256]{2,1,0:T(8,128)(2,1)S(1)} %broadcast_in_dim.10), channel_id=1, replica_groups=mesh['users'=16,'seq'=8] {'users'}, dimensions={0} | all-to-all | bytes 655360 | tf_op jit(solution)/shard_map/all_to_all | solution.py:416
  161.1 3.6 %collective-permute-start = (bf16[320,384]{1,0:T(8,128)(2,1)}, bf16[320,384]{1,0:T(8,128)(2,1)S(1)}, u32[]{:S(2)}, u32[]{:S(2)}) collective-permute-start(bf16[320,384]{1,0:T(8,128)(2,1)} %get-tuple-element.48), channel_id=1, source_target_pairs={{0,1},{1,2},{2,3},{3,4},{4,5},{5,6},{6,7},{7,0},{8,9},{9,10},{10,1... | collective-permute-start | bytes 737288 | tf_op jit(solution)/shard_map/ppermute | solution.py:534
  164.7 2.1 collective-permute-start.2
  168.3 2.6 %collective-permute-start.4 = (bf16[320,384]{1,0:T(8,128)(2,1)}, bf16[320,384]{1,0:T(8,128)(2,1)S(1)}, u32[]{:S(2)}, u32[]{:S(2)}) collective-permute-start(bf16[320,384]{1,0:T(8,128)(2,1)} %get-tuple-element.52), channel_id=1, source_target_pairs={{0,5},{1,6},{2,7},{3,0},{4,1},{5,2},{6,3},{7,4},{8,13},{9,14},{10,... | collective-permute-start | bytes 737288 | tf_op jit(solution)/shard_map/ppermute | solution.py:534
  172.5 11.4 %collective-permute-done.1.refs_2_ = bf16[320,384]{1,0:T(8,128)(2,1)S(1)} collective-permute-done((bf16[320,384]{1,0:T(8,128)(2,1)}, bf16[320,384]{1,0:T(8,128)(2,1)S(1)}, u32[]{:S(2)}, u32[]{:S(2)}) %collective-permute-start.1) | collective-permute-done | bytes 245792 | tf_op jit(solution)/shard_map/ppermute | solution.py:534
  183.9 6.8 %collective-permute-done.2.refs_3_ = bf16[320,384]{1,0:T(8,128)(2,1)S(1)} collective-permute-done((bf16[320,384]{1,0:T(8,128)(2,1)}, bf16[320,384]{1,0:T(8,128)(2,1)S(1)}, u32[]{:S(2)}, u32[]{:S(2)}) %collective-permute-start.2) | collective-permute-done | bytes 245792 | tf_op jit(solution)/shard_map/ppermute | solution.py:534
  190.7 7.9 %collective-permute-done.3.refs_4_ = bf16[320,384]{1,0:T(8,128)(2,1)S(1)} collective-permute-done((bf16[320,384]{1,0:T(8,128)(2,1)}, bf16[320,384]{1,0:T(8,128)(2,1)S(1)}, u32[]{:S(2)}, u32[]{:S(2)}) %collective-permute-start.3) | collective-permute-done | bytes 245792 | tf_op jit(solution)/shard_map/ppermute | solution.py:534
  201.1 4.2 %shard_map.115 = (bf16[1024,512]{1,0:T(8,128)(2,1)}, bf16[512,384]{1,0:T(8,128)(2,1)}) custom-call(bf16[320,384]{1,0:T(8,128)(2,1)} %get-tuple-element.47.refs_0_, bf16[320,384]{1,0:T(8,128)(2,1)S(1)} %collective-permute-done.refs_1_, bf16[320,384]{1,0:T(8,128)(2,1)S(1)} %collective-permute-done.1.refs_2_, ...), custom_call_target="tpu_custom_call" | custom-call | flops 805306368 | bytes 6291456 | tf_op jit(solution)/shard_map/pallas_call | solution.py:47
  205.2 4.9 %all-to-all-start.3 = ((bf16[128,8,512]{2,1,0:T(8,128)(2,1)}), bf16[128,8,512]{2,1,0:T(8,128)(2,1)S(1)}, u32[]{:S(2)}, u32[]{:S(2)}) async-start(bf16[128,8,512]{2,1,0:T(8,128)(2,1)} %bitcast.34), calls=%async_computation.3 | async-start | bytes 2097152 | tf_op jit(solution)/shard_map/all_to_all | solution.py:416
  210.1 2.1 fusion.1
  212.3 16.9 %all-to-all-done.3 = bf16[128,8,512]{2,1,0:T(8,128)(2,1)S(1)} async-done(((bf16[128,8,512]{2,1,0:T(8,128)(2,1)}), bf16[128,8,512]{2,1,0:T(8,128)(2,1)S(1)}, u32[]{:S(2)}, u32[]{:S(2)}) %all-to-all-start.3) | async-done | bytes 1048608 | tf_op jit(solution)/shard_map/all_to_all | solution.py:416
  229.1 5.4 %shard_map.116 = f32[2048,512]{1,0:T(8,128)} custom-call(s32[8,1024]{1,0:T(8,128)S(1)} %copy-done.7, bf16[1024,512]{1,0:T(8,128)(2,1)S(1)} %bitcast.27), custom_call_target="tpu_custom_call" | custom-call | flops 2147483648 | bytes 6291456 | tf_op jit(solution)/shard_map/pallas_call | solution.py:47
  234.5 4.8 %shard_map.117 = (f32[512,2048]{1,0:T(8,128)}, f32[8,8,8,512]{3,2,1,0:T(8,128)}) custom-call(bf16[8,16,40,256]{3,2,1,0:T(8,128)(2,1)} %bitcast.33), custom_call_target="tpu_custom_call" | custom-call | flops 1048576 | bytes 8388608 | tf_op jit(solution)/shard_map/pallas_call | solution.py:47
  (38 shorter events, 10.9 us)
Async XLA Ops:
  7.2 59.9 %copy-start = (bf16[512,512]{1,0:T(8,128)(2,1)S(1)}, bf16[512,512]{1,0:T(8,128)(2,1)}, u32[]{:S(2)}) copy-start(bf16[512,512]{1,0:T(8,128)(2,1)} %param.12) | copy-start | bytes 1572868
  7.2 59.9 %all-gather.8.cloned.1.call-start = ((), (), s32[]{:S(2)}) async-start(), calls=%async_computation.7 | async-start | bytes 3538944 | tf_op jit(solution)/shard_map/all_gather | solution.py:435
  7.9 79.6 %all-gather.6.cloned.1.call-start = ((), (), s32[]{:S(2)}) async-start(), calls=%async_computation.6 | async-start | bytes 3538944 | tf_op jit(solution)/shard_map/all_gather | solution.py:469
  31.0 30.1 %copy-start.5 = (f32[512]{0:T(512)S(1)}, f32[512]{0:T(512)}, u32[]{:S(2)}) copy-start(f32[512]{0:T(512)} %param.13) | copy-start | bytes 6148
  31.0 30.1 %copy-start.6 = (s32[384,128]{1,0:T(8,128)S(1)}, s32[384,128]{1,0:T(8,128)}, u32[]{:S(2)}) copy-start(s32[384,128]{1,0:T(8,128)} %get-tuple-element.35.col_ref) | copy-start | bytes 589828
  36.7 26.2 %copy-start.1 = (bf16[512,2048]{1,0:T(8,128)(2,1)S(1)}, bf16[512,2048]{1,0:T(8,128)(2,1)}, u32[]{:S(2)}) copy-start(bf16[512,2048]{1,0:T(8,128)(2,1)} %refs_8_.1) | copy-start | bytes 6291460
  62.8 171.7 %all-gather.10.cloned.1.call-start = ((), (), s32[]{:S(2)}) async-start(), calls=%async_computation.8 | async-start | bytes 2949120 | tf_op jit(solution)/shard_map/all_gather | solution.py:539
  127.3 73.8 %copy-start.2 = (bf16[1,384,512]{2,1,0:T(8,128)(2,1)S(1)}, bf16[1,384,512]{2,1,0:T(8,128)(2,1)}, u32[]{:S(2)}) copy-start(bf16[1,384,512]{2,1,0:T(8,128)(2,1)} %param.15) | copy-start | bytes 1179652
  127.3 73.8 %copy-start.3 = (bf16[384,512]{1,0:T(8,128)(2,1)S(1)}, bf16[384,512]{1,0:T(8,128)(2,1)}, u32[]{:S(2)}) copy-start(bf16[384,512]{1,0:T(8,128)(2,1)} %get-tuple-element.36.refs_10_) | copy-start | bytes 1179652
  127.3 73.7 %copy-start.4 = (s32[8,384]{1,0:T(8,128)S(1)}, s32[8,384]{1,0:T(8,128)}, u32[]{:S(2)}) copy-start(s32[8,384]{1,0:T(8,128)} %get-tuple-element.55.refs_12_) | copy-start | bytes 36868
  161.1 9.8 %collective-permute-start = (bf16[320,384]{1,0:T(8,128)(2,1)}, bf16[320,384]{1,0:T(8,128)(2,1)S(1)}, u32[]{:S(2)}, u32[]{:S(2)}) collective-permute-start(bf16[320,384]{1,0:T(8,128)(2,1)} %get-tuple-element.48), channel_id=1, source_target_pairs={{0,1},{1,2},{2,3},{3,4},{4,5},{5,6},{6,7},{7,0},{8,9},{9,10},{10,1... | collective-permute-start | bytes 737288 | tf_op jit(solution)/shard_map/ppermute | solution.py:534
  164.7 19.2 %collective-permute-start.1 = (bf16[320,384]{1,0:T(8,128)(2,1)}, bf16[320,384]{1,0:T(8,128)(2,1)S(1)}, u32[]{:S(2)}, u32[]{:S(2)}) collective-permute-start(bf16[320,384]{1,0:T(8,128)(2,1)} %get-tuple-element.49), channel_id=1, source_target_pairs={{0,2},{1,3},{2,4},{3,5},{4,6},{5,7},{6,0},{7,1},{8,10},{9,11},{10,... | collective-permute-start | bytes 737288 | tf_op jit(solution)/shard_map/ppermute | solution.py:534
  164.7 26.0 %collective-permute-start.2 = (bf16[320,384]{1,0:T(8,128)(2,1)}, bf16[320,384]{1,0:T(8,128)(2,1)S(1)}, u32[]{:S(2)}, u32[]{:S(2)}) collective-permute-start(bf16[320,384]{1,0:T(8,128)(2,1)} %get-tuple-element.50), channel_id=1, source_target_pairs={{0,3},{1,4},{2,5},{3,6},{4,7},{5,0},{6,1},{7,2},{8,11},{9,12},{10,... | collective-permute-start | bytes 737288 | tf_op jit(solution)/shard_map/ppermute | solution.py:534
  166.8 31.8 %collective-permute-start.3 = (bf16[320,384]{1,0:T(8,128)(2,1)}, bf16[320,384]{1,0:T(8,128)(2,1)S(1)}, u32[]{:S(2)}, u32[]{:S(2)}) collective-permute-start(bf16[320,384]{1,0:T(8,128)(2,1)} %get-tuple-element.51), channel_id=1, source_target_pairs={{0,4},{1,5},{2,6},{3,7},{4,0},{5,1},{6,2},{7,3},{8,12},{9,13},{10,... | collective-permute-start | bytes 737288 | tf_op jit(solution)/shard_map/ppermute | solution.py:534
  168.3 31.0 %collective-permute-start.4 = (bf16[320,384]{1,0:T(8,128)(2,1)}, bf16[320,384]{1,0:T(8,128)(2,1)S(1)}, u32[]{:S(2)}, u32[]{:S(2)}) collective-permute-start(bf16[320,384]{1,0:T(8,128)(2,1)} %get-tuple-element.52), channel_id=1, source_target_pairs={{0,5},{1,6},{2,7},{3,0},{4,1},{5,2},{6,3},{7,4},{8,13},{9,14},{10,... | collective-permute-start | bytes 737288 | tf_op jit(solution)/shard_map/ppermute | solution.py:534
  170.9 29.5 %collective-permute-start.5 = (bf16[320,384]{1,0:T(8,128)(2,1)}, bf16[320,384]{1,0:T(8,128)(2,1)S(1)}, u32[]{:S(2)}, u32[]{:S(2)}) collective-permute-start(bf16[320,384]{1,0:T(8,128)(2,1)} %get-tuple-element.53), channel_id=1, source_target_pairs={{0,6},{1,7},{2,0},{3,1},{4,2},{5,3},{6,4},{7,5},{8,14},{9,15},{10,... | collective-permute-start | bytes 737288 | tf_op jit(solution)/shard_map/ppermute | solution.py:534
  183.9 17.1 %collective-permute-start.6 = (bf16[320,384]{1,0:T(8,128)(2,1)}, bf16[320,384]{1,0:T(8,128)(2,1)S(1)}, u32[]{:S(2)}, u32[]{:S(2)}) collective-permute-start(bf16[320,384]{1,0:T(8,128)(2,1)} %get-tuple-element.54), channel_id=1, source_target_pairs={{0,7},{1,0},{2,1},{3,2},{4,3},{5,4},{6,5},{7,6},{8,15},{9,8},{10,9... | collective-permute-start | bytes 737288 | tf_op jit(solution)/shard_map/ppermute | solution.py:534
  201.0 28.1 %copy-start.7 = (s32[8,1024]{1,0:T(8,128)S(1)}, s32[8,1024]{1,0:T(8,128)}, u32[]{:S(2)}) copy-start(s32[8,1024]{1,0:T(8,128)} %get-tuple-element.57.row_ref) | copy-start | bytes 98308
  205.2 23.9 %all-to-all-start.3 = ((bf16[128,8,512]{2,1,0:T(8,128)(2,1)}), bf16[128,8,512]{2,1,0:T(8,128)(2,1)S(1)}, u32[]{:S(2)}, u32[]{:S(2)}) async-start(bf16[128,8,512]{2,1,0:T(8,128)(2,1)} %bitcast.34), calls=%async_computation.3 | async-start | bytes 2097152 | tf_op jit(solution)/shard_map/all_to_all | solution.py:416
Sparse Core Ops, SparseCore 0:
  9.7 32.1 all-gather.7
  62.9 24.5 all-gather.5
  161.2 41.2 all-gather.9

commit v6 on v5

--- a/solution.py
+++ b/solution.py
@@ -412,6 +412,37 @@
             wout_ref[h, p // 2, :, 256 * (p % 2) : 256 * (p % 2) + 256] = got_ref[h, p, rows:, :].astype(f32)
 
 
+def finish_kernel(row_ref, rows_ref, got_ref, table_ref, win_ref, wout_ref):
+    table_kernel(row_ref, rows_ref, table_ref)
+    weights_kernel(got_ref, win_ref, wout_ref)
+
+
+def finish(asked_row, incoming, dw_all, shard_rows, tiles):
+    slots, width = incoming.shape
+    seq, users, tall, columns = dw_all.shape
+    rows, group = tall - 8, users // tiles
+    d = HEAD_DIM
+    whole = lambda *shape: pl.BlockSpec(shape, lambda g: (0,) * len(shape))
+    return call(
+        finish_kernel,
+        (
+            struct((shard_rows, width), f32), struct((width, 4 * width), f32), struct((HEADS, width // d, 8, width), f32),
+        ),
+        (asked_row, incoming, pltpu.with_memory_space_constraint(dw_all, pltpu.HBM)),
+        mib=24, grid=(tiles,),
+        in_specs=[
+            whole(8, slots), pl.BlockSpec(memory_space=pltpu.VMEM),
+            pl.BlockSpec((seq, group, tall, columns), lambda g: (0, g, 0, 0)),
+        ],
+        out_specs=[
+            pl.BlockSpec((shard_rows // tiles, width), lambda g: (g, 0)),
+            pl.BlockSpec((group * rows, 4 * width), lambda g: (g, 0)),
+            pl.BlockSpec((HEADS, group // 2, 8, width), lambda g: (0, g, 0, 0)),
+        ],
+        flops=2 * slots * shard_rows * width, moved=15 << 20,
+    )
+
+
 def exchange(x, axis):
     return lax.all_to_all(x, axis, split_axis=0, concat_axis=0, tiled=True)
 
@@ -440,7 +471,7 @@
         flops=2 * devices * count * count, moved=1 << 19,
     )
     asked = exchange(wanted.reshape(devices, 1, 128), BOTH).reshape(devices, 128)
-    steps = 4
+    steps = 1
     whole = lambda *shape: pl.BlockSpec(shape, lambda g: (0,) * len(shape))
     smem = pl.BlockSpec(memory_space=pltpu.SMEM)
     served, asked_row, bounds, gain_h = call(
@@ -555,29 +586,7 @@
     ).astype(bf16)
     incoming = exchange(outgoing.reshape(devices, SLOTS, width), BOTH)
     incoming = incoming.reshape(slots, width)
-    tiles = 8
-    table_grad = call(
-        table_kernel,
-        struct((shard_rows, width), f32),
-        (asked_row, incoming),
-        mib=24, grid=(tiles,),
-        in_specs=[whole(8, slots), pl.BlockSpec(memory_space=pltpu.VMEM)],
-        out_specs=pl.BlockSpec((shard_rows // tiles, width), lambda g: (g, 0)),
-        flops=2 * slots * shard_rows * width, moved=6 << 20,
-    )
-    group = 4
-    win_grad, wout_grad = call(
-        weights_kernel,
-        (struct((width, 4 * width), f32), struct((HEADS, width // d, 8, width), f32)),
-        (dw_all,),
-        grid=(users // group,),
-        in_specs=[pl.BlockSpec((seq, group, rows + 8, 4 * d), lambda g: (0, g, 0, 0))],
-        out_specs=[
-            pl.BlockSpec((group * rows, 4 * width), lambda g: (g, 0)),
-            pl.BlockSpec((HEADS, group // 2, 8, width), lambda g: (0, g, 0, 0)),
-        ],
-        flops=1 << 20, moved=8 << 20,
-    )
+    table_grad, win_grad, wout_grad = finish(asked_row, incoming, dw_all, shard_rows, 4)
     return (layer[None], table_grad, win_grad, wout_grad.reshape(width, width))
 
 

time: 247 us -> 243 us (0.984)
  Pallas kernels: 50.9 us -> 46.8 us
    pallas_call x7 -> x6, Pallas kernels: 33.9 us -> 29.9 us  [call(): pl.pallas_call(kernel, out_shape=out_shape, scratch_shapes=scratch, compi...]
  transfers between devices with their start and end apart: 11 -> 11, of which waited for: 8 -> 8; matrix products, arithmetic and copies ran while one was open for 4% -> 4% of each run, Pallas kernels for 8% -> 5%
where the time goes in v6:
time: 243 us; the launch traced here: 242 us
  blocking collectives  90.6 us (37%)
  waiting for transfers between devices  62.5 us (26%)
  Pallas kernels  46.8 us (19%)
  starting transfers between devices  16.4 us (7%)
  between operations  13.9 us (6%)
  matrix products  6.12 us (3%)
  local copies, waits for them, and re-layouts  3.56 us (1%)
    all_to_all x5, blocking collectives, exchange(): return lax.all_to_all(x, axis, split_axis=0, concat_axis=0, tiled=True)  90.6 us
    pallas_call x6, Pallas kernels, call(): pl.pallas_call(kernel, out_shape=out_shape, scratch_shapes=scratch, compi...  29.9 us
    ppermute x7, waiting for transfers between devices, layer_step(): lax.ppermute(result[s], 'seq', [(i, (i + s) % seq) for i in range(seq)])  28.5 us
    pallas_call x1, Pallas kernels, layer_step(): pl.pallas_call(functools.partial(backward_kernel, blocks), out_shape=[str...  16.9 us
    all_to_all x1, waiting for transfers between devices, exchange(): return lax.all_to_all(x, axis, split_axis=0, concat_axis=0, tiled=True)  16.9 us
    all_gather x1, waiting for transfers between devices, layer_step(): xin_all = lax.all_gather(xin, 'seq', axis=0, tiled=True)  16.4 us
    ppermute x7, starting transfers between devices, layer_step(): lax.ppermute(result[s], 'seq', [(i, (i + s) % seq) for i in range(seq)])  11.4 us
    all_to_all x1, starting transfers between devices, exchange(): return lax.all_to_all(x, axis, split_axis=0, concat_axis=0, tiled=True)  4.88 us
  transfers between devices with their start and end apart: 11, of which 8 were waited for; matrix products, arithmetic and copies ran while one was open for 4% of the time, Pallas kernels for 5%

profile of v6, /device:TPU:1, one launch (start us, length us, event | category | flops | bytes accessed | tf_op | source)
XLA Modules:
  0.0 241.8 jit_solution(3406890369685712921)
XLA Ops:
  8.0 1.8 shard_map.111
  9.8 21.2 %all_to_all.30 = s32[128,1,128]{2,1,0:T(1,128)} all-to-all(s32[128,1,128]{2,1,0:T(1,128)} %bitcast.37), channel_id=1, replica_groups=mesh['users'=16,'seq'=8] {'users','seq'}, dimensions={0} | all-to-all | bytes 131072 | tf_op jit(solution)/shard_map/all_to_all | solution.py:447
  31.0 5.0 %shard_map.112 = (bf16[1024,512]{1,0:T(8,128)(2,1)}, s32[8,1024]{1,0:T(8,128)}, s32[8,128]{1,0:T(8,128)}, f32[64,128]{1,0:T(8,128)}) custom-call(s32[128,128]{1,0:T(8,128)} %bitcast.36, bf16[2048,512]{1,0:T(8,128)(2,1)} %table_ref.1, f32[1,512]{1,0:T(1,128)} %bitcast.39), custom_call_target="tpu_custom_call" | custom-call | flops 2147483648 | bytes 4194304 | tf_op jit(solution)/shard_map/pallas_call | solution.py:47
  36.0 24.4 %all_to_all.31 = bf16[128,8,512]{2,1,0:T(8,128)(2,1)S(1)} all-to-all(bf16[128,8,512]{2,1,0:T(8,128)(2,1)} %bitcast.34), channel_id=1, replica_groups=mesh['users'=16,'seq'=8] {'users','seq'}, dimensions={0} | all-to-all | bytes 2097152 | tf_op jit(solution)/shard_map/all_to_all | solution.py:447
  60.4 1.7 shard_map.113
  62.2 2.5 %copy.15 = bf16[512,2048]{0,1:T(8,128)(2,1)} copy(bf16[512,2048]{1,0:T(8,128)(2,1)S(1)} %copy-done.1) | data formatting | bytes 4194304 | tf_op args[3]
  66.4 4.0 %fusion.2.dg_ref = f32[64,3072]{1,0:T(8,128)} fusion(bf16[512,512]{1,0:T(8,128)(2,1)S(1)} %copy-done, s32[]{:T(128)S(6)} %select_n.7, bf16[1,3072,512]{2,1,0:T(8,128)(2,1)} %all-gather.8.cloned.1.call-done), kind=kOutput, calls=%fused_computation.5 | convolution fusion | flops 201326592 | bytes 3997700 | tf_op jit(solution)/shard_map/dot_general | solution.py:34
  70.4 16.4 %all-gather.6.cloned.1.call-done.xin_ref.xin_hbm = bf16[3072,512]{1,0:T(8,128)(2,1)} async-done(((bf16[384,512]{1,0:T(8,128)(2,1)}), bf16[3072,512]{1,0:T(8,128)(2,1)}) %all-gather.6.cloned.1.call-update) | async-done | bytes 3145744 | tf_op jit(solution)/shard_map/all_gather | solution.py:500
  86.8 10.4 %shard_map.114 = (bf16[64,3072]{1,0:T(8,128)(2,1)}, bf16[64,3072]{1,0:T(8,128)(2,1)}, bf16[3072,128]{1,0:T(8,128)(2,1)}, f32[256,3072]{1,0:T(8,128)}, f32[64,307...) custom-call(bf16[3072,512]{1,0:T(8,128)(2,1)} %all-gather.6.cloned.1.call-done.xin_ref.xin_hbm, ...), custom_call_target="tpu_custom_call" | custom-call | flops 8589934592 | bytes 12582912 | tf_op jit(solution)/shard_map/pallas_call | solution.py:47
  97.2 12.4 %all_to_all.32.stats_ref = f32[8,4,3072]{2,1,0:T(4,128)} all-to-all(f32[8,4,3072]{2,1,0:T(4,128)} %get-tuple-element.44), channel_id=1, replica_groups=mesh['users'=16,'seq'=8] {'seq'}, dimensions={0} | all-to-all | bytes 786432 | tf_op jit(solution)/shard_map/all_to_all | solution.py:447
  109.6 16.9 %backward.1 = (bf16[320,384]{1,0:T(8,128)(2,1)}, bf16[320,384]{1,0:T(8,128)(2,1)}, bf16[320,384]{1,0:T(8,128)(2,1)}, bf16[320,384]{1,0:T(8,128)(2,1)}, bf16[320,...) custom-call(s32[8,128]{1,0:T(8,128)} %get-tuple-element.38.bounds_re, ...), custom_call_target="tpu_custom_call" | custom-call | flops 34359738368 | bytes 16777216 | tf_op jit(solution)/shard_map/backward/pallas_call | solution.py:532
  126.6 21.4 %all_to_all.33 = f32[16,40,256]{2,1,0:T(8,128)} all-to-all(f32[16,40,256]{2,1,0:T(8,128)} %get-tuple-element.60), channel_id=1, replica_groups=mesh['users'=16,'seq'=8] {'users'}, dimensions={0} | all-to-all | bytes 1310720 | tf_op jit(solution)/shard_map/all_to_all | solution.py:447
  149.2 11.2 %all_to_all.34 = bf16[16,40,256]{2,1,0:T(8,128)(2,1)} all-to-all(bf16[16,40,256]{2,1,0:T(8,128)(2,1)S(1)} %broadcast_in_dim.10), channel_id=1, replica_groups=mesh['users'=16,'seq'=8] {'users'}, dimensions={0} | all-to-all | bytes 655360 | tf_op jit(solution)/shard_map/all_to_all | solution.py:447
  160.4 3.6 %collective-permute-start = (bf16[320,384]{1,0:T(8,128)(2,1)}, bf16[320,384]{1,0:T(8,128)(2,1)S(1)}, u32[]{:S(2)}, u32[]{:S(2)}) collective-permute-start(bf16[320,384]{1,0:T(8,128)(2,1)} %get-tuple-element.49), channel_id=1, source_target_pairs={{0,1},{1,2},{2,3},{3,4},{4,5},{5,6},{6,7},{7,0},{8,9},{9,10},{10,1... | collective-permute-start | bytes 737288 | tf_op jit(solution)/shard_map/ppermute | solution.py:565
  164.0 2.1 collective-permute-start.2
  167.6 2.6 %collective-permute-start.4 = (bf16[320,384]{1,0:T(8,128)(2,1)}, bf16[320,384]{1,0:T(8,128)(2,1)S(1)}, u32[]{:S(2)}, u32[]{:S(2)}) collective-permute-start(bf16[320,384]{1,0:T(8,128)(2,1)} %get-tuple-element.53), channel_id=1, source_target_pairs={{0,5},{1,6},{2,7},{3,0},{4,1},{5,2},{6,3},{7,4},{8,13},{9,14},{10,... | collective-permute-start | bytes 737288 | tf_op jit(solution)/shard_map/ppermute | solution.py:565
  171.8 11.4 %collective-permute-done.1.refs_2_ = bf16[320,384]{1,0:T(8,128)(2,1)S(1)} collective-permute-done((bf16[320,384]{1,0:T(8,128)(2,1)}, bf16[320,384]{1,0:T(8,128)(2,1)S(1)}, u32[]{:S(2)}, u32[]{:S(2)}) %collective-permute-start.1) | collective-permute-done | bytes 245792 | tf_op jit(solution)/shard_map/ppermute | solution.py:565
  183.2 6.8 %collective-permute-done.2.refs_3_ = bf16[320,384]{1,0:T(8,128)(2,1)S(1)} collective-permute-done((bf16[320,384]{1,0:T(8,128)(2,1)}, bf16[320,384]{1,0:T(8,128)(2,1)S(1)}, u32[]{:S(2)}, u32[]{:S(2)}) %collective-permute-start.2) | collective-permute-done | bytes 245792 | tf_op jit(solution)/shard_map/ppermute | solution.py:565
  190.0 7.9 %collective-permute-done.3.refs_4_ = bf16[320,384]{1,0:T(8,128)(2,1)S(1)} collective-permute-done((bf16[320,384]{1,0:T(8,128)(2,1)}, bf16[320,384]{1,0:T(8,128)(2,1)S(1)}, u32[]{:S(2)}, u32[]{:S(2)}) %collective-permute-start.3) | collective-permute-done | bytes 245792 | tf_op jit(solution)/shard_map/ppermute | solution.py:565
  200.4 4.2 %shard_map.115 = (bf16[1024,512]{1,0:T(8,128)(2,1)}, bf16[512,384]{1,0:T(8,128)(2,1)}) custom-call(bf16[320,384]{1,0:T(8,128)(2,1)} %get-tuple-element.48.refs_0_, bf16[320,384]{1,0:T(8,128)(2,1)S(1)} %collective-permute-done.refs_1_, bf16[320,384]{1,0:T(8,128)(2,1)S(1)} %collective-permute-done.1.refs_2_, ...), custom_call_target="tpu_custom_call" | custom-call | flops 805306368 | bytes 6291456 | tf_op jit(solution)/shard_map/pallas_call | solution.py:47
  204.5 4.9 %all-to-all-start.3 = ((bf16[128,8,512]{2,1,0:T(8,128)(2,1)}), bf16[128,8,512]{2,1,0:T(8,128)(2,1)S(1)}, u32[]{:S(2)}, u32[]{:S(2)}) async-start(bf16[128,8,512]{2,1,0:T(8,128)(2,1)} %bitcast.33), calls=%async_computation.3 | async-start | bytes 2097152 | tf_op jit(solution)/shard_map/all_to_all | solution.py:447
  209.4 2.1 fusion.1
  211.6 16.9 %all-to-all-done.3 = bf16[128,8,512]{2,1,0:T(8,128)(2,1)S(1)} async-done(((bf16[128,8,512]{2,1,0:T(8,128)(2,1)}), bf16[128,8,512]{2,1,0:T(8,128)(2,1)S(1)}, u32[]{:S(2)}, u32[]{:S(2)}) %all-to-all-start.3) | async-done | bytes 1048608 | tf_op jit(solution)/shard_map/all_to_all | solution.py:447
  228.4 6.8 %shard_map.116 = (f32[2048,512]{1,0:T(8,128)}, f32[512,2048]{1,0:T(8,128)}, f32[8,8,8,512]{3,2,1,0:T(8,128)}) custom-call(s32[8,1024]{1,0:T(8,128)S(1)} %copy-done.7, bf16[1024,512]{1,0:T(8,128)(2,1)S(1)} %bitcast.27, bf16[8,16,40,256]{3,2,1,0:T(8,128)(2,1)} %bitcast.38), custom_call_target="tpu_custom_call" | custom-call | flops 2147483648 | bytes 15728640 | tf_op jit(solution)/shard_map/pallas_call | solution.py:47
  (37 shorter events, 9.2 us)
Async XLA Ops:
  7.2 59.2 %copy-start = (bf16[512,512]{1,0:T(8,128)(2,1)S(1)}, bf16[512,512]{1,0:T(8,128)(2,1)}, u32[]{:S(2)}) copy-start(bf16[512,512]{1,0:T(8,128)(2,1)} %param.12) | copy-start | bytes 1572868
  7.2 59.2 %all-gather.8.cloned.1.call-start = ((), (), s32[]{:S(2)}) async-start(), calls=%async_computation.7 | async-start | bytes 3538944 | tf_op jit(solution)/shard_map/all_gather | solution.py:466
  7.9 78.9 %all-gather.6.cloned.1.call-start = ((), (), s32[]{:S(2)}) async-start(), calls=%async_computation.6 | async-start | bytes 3538944 | tf_op jit(solution)/shard_map/all_gather | solution.py:500
  31.0 29.4 %copy-start.5 = (f32[512]{0:T(512)S(1)}, f32[512]{0:T(512)}, u32[]{:S(2)}) copy-start(f32[512]{0:T(512)} %param.13) | copy-start | bytes 6148
  31.0 29.4 %copy-start.6 = (s32[384,128]{1,0:T(8,128)S(1)}, s32[384,128]{1,0:T(8,128)}, u32[]{:S(2)}) copy-start(s32[384,128]{1,0:T(8,128)} %get-tuple-element.36.col_ref) | copy-start | bytes 589828
  36.0 26.2 %copy-start.1 = (bf16[512,2048]{1,0:T(8,128)(2,1)S(1)}, bf16[512,2048]{1,0:T(8,128)(2,1)}, u32[]{:S(2)}) copy-start(bf16[512,2048]{1,0:T(8,128)(2,1)} %refs_8_.1) | copy-start | bytes 6291460
  62.1 166.4 %all-gather.10.cloned.1.call-start = ((), (), s32[]{:S(2)}) async-start(), calls=%async_computation.8 | async-start | bytes 2949120 | tf_op jit(solution)/shard_map/all_gather | solution.py:570
  126.5 73.8 %copy-start.2 = (bf16[1,384,512]{2,1,0:T(8,128)(2,1)S(1)}, bf16[1,384,512]{2,1,0:T(8,128)(2,1)}, u32[]{:S(2)}) copy-start(bf16[1,384,512]{2,1,0:T(8,128)(2,1)} %param.15) | copy-start | bytes 1179652
  126.6 73.8 %copy-start.3 = (bf16[384,512]{1,0:T(8,128)(2,1)S(1)}, bf16[384,512]{1,0:T(8,128)(2,1)}, u32[]{:S(2)}) copy-start(bf16[384,512]{1,0:T(8,128)(2,1)} %get-tuple-element.37.refs_10_) | copy-start | bytes 1179652
  126.6 73.8 %copy-start.4 = (s32[8,384]{1,0:T(8,128)S(1)}, s32[8,384]{1,0:T(8,128)}, u32[]{:S(2)}) copy-start(s32[8,384]{1,0:T(8,128)} %get-tuple-element.56.refs_12_) | copy-start | bytes 36868
  160.4 9.8 %collective-permute-start = (bf16[320,384]{1,0:T(8,128)(2,1)}, bf16[320,384]{1,0:T(8,128)(2,1)S(1)}, u32[]{:S(2)}, u32[]{:S(2)}) collective-permute-start(bf16[320,384]{1,0:T(8,128)(2,1)} %get-tuple-element.49), channel_id=1, source_target_pairs={{0,1},{1,2},{2,3},{3,4},{4,5},{5,6},{6,7},{7,0},{8,9},{9,10},{10,1... | collective-permute-start | bytes 737288 | tf_op jit(solution)/shard_map/ppermute | solution.py:565
  164.0 19.2 %collective-permute-start.1 = (bf16[320,384]{1,0:T(8,128)(2,1)}, bf16[320,384]{1,0:T(8,128)(2,1)S(1)}, u32[]{:S(2)}, u32[]{:S(2)}) collective-permute-start(bf16[320,384]{1,0:T(8,128)(2,1)} %get-tuple-element.50), channel_id=1, source_target_pairs={{0,2},{1,3},{2,4},{3,5},{4,6},{5,7},{6,0},{7,1},{8,10},{9,11},{10,... | collective-permute-start | bytes 737288 | tf_op jit(solution)/shard_map/ppermute | solution.py:565
  164.0 26.0 %collective-permute-start.2 = (bf16[320,384]{1,0:T(8,128)(2,1)}, bf16[320,384]{1,0:T(8,128)(2,1)S(1)}, u32[]{:S(2)}, u32[]{:S(2)}) collective-permute-start(bf16[320,384]{1,0:T(8,128)(2,1)} %get-tuple-element.51), channel_id=1, source_target_pairs={{0,3},{1,4},{2,5},{3,6},{4,7},{5,0},{6,1},{7,2},{8,11},{9,12},{10,... | collective-permute-start | bytes 737288 | tf_op jit(solution)/shard_map/ppermute | solution.py:565
  166.1 31.8 %collective-permute-start.3 = (bf16[320,384]{1,0:T(8,128)(2,1)}, bf16[320,384]{1,0:T(8,128)(2,1)S(1)}, u32[]{:S(2)}, u32[]{:S(2)}) collective-permute-start(bf16[320,384]{1,0:T(8,128)(2,1)} %get-tuple-element.52), channel_id=1, source_target_pairs={{0,4},{1,5},{2,6},{3,7},{4,0},{5,1},{6,2},{7,3},{8,12},{9,13},{10,... | collective-permute-start | bytes 737288 | tf_op jit(solution)/shard_map/ppermute | solution.py:565
  167.6 31.0 %collective-permute-start.4 = (bf16[320,384]{1,0:T(8,128)(2,1)}, bf16[320,384]{1,0:T(8,128)(2,1)S(1)}, u32[]{:S(2)}, u32[]{:S(2)}) collective-permute-start(bf16[320,384]{1,0:T(8,128)(2,1)} %get-tuple-element.53), channel_id=1, source_target_pairs={{0,5},{1,6},{2,7},{3,0},{4,1},{5,2},{6,3},{7,4},{8,13},{9,14},{10,... | collective-permute-start | bytes 737288 | tf_op jit(solution)/shard_map/ppermute | solution.py:565
  170.2 29.5 %collective-permute-start.5 = (bf16[320,384]{1,0:T(8,128)(2,1)}, bf16[320,384]{1,0:T(8,128)(2,1)S(1)}, u32[]{:S(2)}, u32[]{:S(2)}) collective-permute-start(bf16[320,384]{1,0:T(8,128)(2,1)} %get-tuple-element.54), channel_id=1, source_target_pairs={{0,6},{1,7},{2,0},{3,1},{4,2},{5,3},{6,4},{7,5},{8,14},{9,15},{10,... | collective-permute-start | bytes 737288 | tf_op jit(solution)/shard_map/ppermute | solution.py:565
  183.2 17.1 %collective-permute-start.6 = (bf16[320,384]{1,0:T(8,128)(2,1)}, bf16[320,384]{1,0:T(8,128)(2,1)S(1)}, u32[]{:S(2)}, u32[]{:S(2)}) collective-permute-start(bf16[320,384]{1,0:T(8,128)(2,1)} %get-tuple-element.55), channel_id=1, source_target_pairs={{0,7},{1,0},{2,1},{3,2},{4,3},{5,4},{6,5},{7,6},{8,15},{9,8},{10,9... | collective-permute-start | bytes 737288 | tf_op jit(solution)/shard_map/ppermute | solution.py:565
  200.4 28.1 %copy-start.7 = (s32[8,1024]{1,0:T(8,128)S(1)}, s32[8,1024]{1,0:T(8,128)}, u32[]{:S(2)}) copy-start(s32[8,1024]{1,0:T(8,128)} %get-tuple-element.58.row_ref) | copy-start | bytes 98308
  204.5 23.9 %all-to-all-start.3 = ((bf16[128,8,512]{2,1,0:T(8,128)(2,1)}), bf16[128,8,512]{2,1,0:T(8,128)(2,1)S(1)}, u32[]{:S(2)}, u32[]{:S(2)}) async-start(bf16[128,8,512]{2,1,0:T(8,128)(2,1)} %bitcast.33), calls=%async_computation.3 | async-start | bytes 2097152 | tf_op jit(solution)/shard_map/all_to_all | solution.py:447
Sparse Core Ops, SparseCore 0:
  9.7 32.1 all-gather.7
  62.2 24.5 all-gather.5
  160.5 41.2 all-gather.9

commit v7 on v6

--- a/solution.py
+++ b/solution.py
@@ -347,7 +347,16 @@
 
 def rows_kernel(*refs):
     got = refs[:HEADS]
-    win_ref, gain_ref, fetched_ref, cot_ref, row_ref, out_hbm, gated_hbm, whole, gated_ref, out_ref, sems = refs[HEADS:]
+    win_hbm, gain_ref, fetched_ref, cot_ref, row_ref, out_hbm, gated_hbm, whole, gated_ref, out_ref, sems = refs[
+        HEADS:-2
+    ]
+    win_ref, win_sems = refs[-2:]
+    chunks = win_sems.shape[0]
+    tall = win_ref.shape[0] // chunks
+    strips = [pl.ds(c * tall, tall) for c in range(chunks)]
+    brought = [pltpu.make_async_copy(win_hbm.at[r], win_ref.at[r], win_sems.at[c]) for c, r in enumerate(strips)]
+    for load in brought:
+        load.start()
     d = HEAD_DIM
     width = fetched_ref.shape[1]
     me = lax.axis_index("seq")
@@ -367,7 +376,11 @@
         load.wait()
     copies = [pltpu.make_async_copy(gated_ref, gated_hbm, sems.at[0])]
     copies[0].start()
-    dxin = jnp.transpose(mm(win_ref[...], whole[...]))
+    columns = []
+    for load, strip in zip(brought, strips):
+        load.wait()
+        columns.append(jnp.transpose(mm(win_ref[strip, :], whole[...])))
+    dxin = jnp.concatenate(columns, axis=1)
     normed, inverse = normalize(fetched_ref[...].astype(f32))
     f = dxin * gain_ref[...]
     drow = inverse * (
@@ -571,12 +584,13 @@
     outgoing, gated_mine = call(
         rows_kernel,
         (pltpu.HBM((slots, width), bf16), pltpu.HBM((width, count), bf16)),
-        (pltpu.with_memory_space_constraint(pieces[0], pltpu.HBM), *pieces[1:], weight_in, gain_row, fetched, upstream, slot_row),
-        mib=24, in_specs=[pl.BlockSpec(memory_space=pltpu.HBM)] + [pl.BlockSpec(memory_space=pltpu.VMEM)] * (HEADS + 4),
+        (pltpu.with_memory_space_constraint(pieces[0], pltpu.HBM), *pieces[1:], pltpu.with_memory_space_constraint(weight_in, pltpu.HBM), gain_row, fetched, upstream, slot_row),
+        mib=24, in_specs=[pl.BlockSpec(memory_space=pltpu.HBM)] + [pl.BlockSpec(memory_space=pltpu.VMEM)] * (HEADS - 1)
+        + [pl.BlockSpec(memory_space=pltpu.HBM)] + [pl.BlockSpec(memory_space=pltpu.VMEM)] * 4,
         out_specs=[pl.BlockSpec(memory_space=pltpu.HBM)] * 2,
         scratch=[
             pltpu.VMEM((4 * width, count), bf16), pltpu.VMEM((width, count), bf16), pltpu.VMEM((slots, width), bf16),
-            pltpu.SemaphoreType.DMA((10,)),
+            pltpu.SemaphoreType.DMA((10,)), pltpu.VMEM((width, 4 * width), bf16), pltpu.SemaphoreType.DMA((4,)),
         ],
         flops=2 * count * width * 4 * width, moved=6 << 20,
     )

time: 243 us -> 242 us (level)
  transfers between devices with their start and end apart: 11 -> 11, of which waited for: 8 -> 8; matrix products, arithmetic and copies ran while one was open for 4% -> 4% of each run, Pallas kernels for 5% -> 6%
where the time goes in v7:
time: 242 us; the launch traced here: 241 us
  blocking collectives  90.3 us (37%)
  waiting for transfers between devices  62.3 us (26%)
  Pallas kernels  47.8 us (20%)
  starting transfers between devices  16.5 us (7%)
  between operations  13.9 us (6%)
  matrix products  6.12 us (3%)
  local copies, waits for them, and re-layouts  3.58 us (1%)
    all_to_all x5, blocking collectives, exchange(): return lax.all_to_all(x, axis, split_axis=0, concat_axis=0, tiled=True)  90.3 us
    pallas_call x6, Pallas kernels, call(): pl.pallas_call(kernel, out_shape=out_shape, scratch_shapes=scratch, compi...  30.9 us
    ppermute x7, waiting for transfers between devices, layer_step(): lax.ppermute(result[s], 'seq', [(i, (i + s) % seq) for i in range(seq)])  28.3 us
    pallas_call x1, Pallas kernels, layer_step(): pl.pallas_call(functools.partial(backward_kernel, blocks), out_shape=[str...  16.9 us
    all_to_all x1, waiting for transfers between devices, exchange(): return lax.all_to_all(x, axis, split_axis=0, concat_axis=0, tiled=True)  16.9 us
    all_gather x1, waiting for transfers between devices, layer_step(): xin_all = lax.all_gather(xin, 'seq', axis=0, tiled=True)  16.4 us
    ppermute x7, starting transfers between devices, layer_step(): lax.ppermute(result[s], 'seq', [(i, (i + s) % seq) for i in range(seq)])  11.6 us
  transfers between devices with their start and end apart: 11, of which 8 were waited for; matrix products, arithmetic and copies ran while one was open for 4% of the time, Pallas kernels for 6%

profile of v7, /device:TPU:1, one launch (start us, length us, event | category | flops | bytes accessed | tf_op | source)
XLA Modules:
  0.0 241.3 jit_solution(6366093346151267076)
XLA Ops:
  8.0 1.8 shard_map.111
  9.8 21.3 %all_to_all.30 = s32[128,1,128]{2,1,0:T(1,128)} all-to-all(s32[128,1,128]{2,1,0:T(1,128)} %bitcast.37), channel_id=1, replica_groups=mesh['users'=16,'seq'=8] {'users','seq'}, dimensions={0} | all-to-all | bytes 131072 | tf_op jit(solution)/shard_map/all_to_all | solution.py:460
  31.1 5.0 %shard_map.112 = (bf16[1024,512]{1,0:T(8,128)(2,1)}, s32[8,1024]{1,0:T(8,128)}, s32[8,128]{1,0:T(8,128)}, f32[64,128]{1,0:T(8,128)}) custom-call(s32[128,128]{1,0:T(8,128)} %bitcast.36, bf16[2048,512]{1,0:T(8,128)(2,1)} %table_ref.1, f32[1,512]{1,0:T(1,128)} %bitcast.39), custom_call_target="tpu_custom_call" | custom-call | flops 2147483648 | bytes 4194304 | tf_op jit(solution)/shard_map/pallas_call | solution.py:47
  36.2 24.1 %all_to_all.31 = bf16[128,8,512]{2,1,0:T(8,128)(2,1)S(1)} all-to-all(bf16[128,8,512]{2,1,0:T(8,128)(2,1)} %bitcast.34), channel_id=1, replica_groups=mesh['users'=16,'seq'=8] {'users','seq'}, dimensions={0} | all-to-all | bytes 2097152 | tf_op jit(solution)/shard_map/all_to_all | solution.py:460
  62.0 2.5 %copy.15 = bf16[512,2048]{0,1:T(8,128)(2,1)} copy(bf16[512,2048]{1,0:T(8,128)(2,1)S(1)} %copy-done.7) | data formatting | bytes 4194304 | tf_op args[3]
  66.3 4.0 %fusion.2.dg_ref = f32[64,3072]{1,0:T(8,128)} fusion(bf16[512,512]{1,0:T(8,128)(2,1)S(1)} %copy-done, s32[]{:T(128)S(6)} %select_n.7, bf16[1,3072,512]{2,1,0:T(8,128)(2,1)} %all-gather.8.cloned.1.call-done), kind=kOutput, calls=%fused_computation.5 | convolution fusion | flops 201326592 | bytes 3997700 | tf_op jit(solution)/shard_map/dot_general | solution.py:34
  70.2 16.4 %all-gather.6.cloned.1.call-done.xin_ref.xin_hbm = bf16[3072,512]{1,0:T(8,128)(2,1)} async-done(((bf16[384,512]{1,0:T(8,128)(2,1)}), bf16[3072,512]{1,0:T(8,128)(2,1)}) %all-gather.6.cloned.1.call-update) | async-done | bytes 3145744 | tf_op jit(solution)/shard_map/all_gather | solution.py:513
  86.6 10.4 %shard_map.114 = (bf16[64,3072]{1,0:T(8,128)(2,1)}, bf16[64,3072]{1,0:T(8,128)(2,1)}, bf16[3072,128]{1,0:T(8,128)(2,1)}, f32[256,3072]{1,0:T(8,128)}, f32[64,307...) custom-call(bf16[3072,512]{1,0:T(8,128)(2,1)} %all-gather.6.cloned.1.call-done.xin_ref.xin_hbm, ...), custom_call_target="tpu_custom_call" | custom-call | flops 8589934592 | bytes 12582912 | tf_op jit(solution)/shard_map/pallas_call | solution.py:47
  97.0 12.4 %all_to_all.32.stats_ref = f32[8,4,3072]{2,1,0:T(4,128)} all-to-all(f32[8,4,3072]{2,1,0:T(4,128)} %get-tuple-element.44), channel_id=1, replica_groups=mesh['users'=16,'seq'=8] {'seq'}, dimensions={0} | all-to-all | bytes 786432 | tf_op jit(solution)/shard_map/all_to_all | solution.py:460
  109.4 16.9 %backward.1 = (bf16[320,384]{1,0:T(8,128)(2,1)}, bf16[320,384]{1,0:T(8,128)(2,1)}, bf16[320,384]{1,0:T(8,128)(2,1)}, bf16[320,384]{1,0:T(8,128)(2,1)}, bf16[320,...) custom-call(s32[8,128]{1,0:T(8,128)} %get-tuple-element.38.bounds_re, ...), custom_call_target="tpu_custom_call" | custom-call | flops 34359738368 | bytes 16777216 | tf_op jit(solution)/shard_map/backward/pallas_call | solution.py:545
  126.5 21.3 %all_to_all.33 = f32[16,40,256]{2,1,0:T(8,128)S(1)} all-to-all(f32[16,40,256]{2,1,0:T(8,128)} %get-tuple-element.60), channel_id=1, replica_groups=mesh['users'=16,'seq'=8] {'users'}, dimensions={0} | all-to-all | bytes 1310720 | tf_op jit(solution)/shard_map/all_to_all | solution.py:460
  147.8 11.2 %all_to_all.34 = bf16[16,40,256]{2,1,0:T(8,128)(2,1)} all-to-all(bf16[16,40,256]{2,1,0:T(8,128)(2,1)S(1)} %broadcast_in_dim.10), channel_id=1, replica_groups=mesh['users'=16,'seq'=8] {'users'}, dimensions={0} | all-to-all | bytes 655360 | tf_op jit(solution)/shard_map/all_to_all | solution.py:460
  159.0 3.6 %collective-permute-start = (bf16[320,384]{1,0:T(8,128)(2,1)}, bf16[320,384]{1,0:T(8,128)(2,1)S(1)}, u32[]{:S(2)}, u32[]{:S(2)}) collective-permute-start(bf16[320,384]{1,0:T(8,128)(2,1)} %get-tuple-element.49), channel_id=1, source_target_pairs={{0,1},{1,2},{2,3},{3,4},{4,5},{5,6},{6,7},{7,0},{8,9},{9,10},{10,1... | collective-permute-start | bytes 737288 | tf_op jit(solution)/shard_map/ppermute | solution.py:578
  162.7 2.1 collective-permute-start.2
  166.3 2.5 %collective-permute-start.4 = (bf16[320,384]{1,0:T(8,128)(2,1)S(1)}, bf16[320,384]{1,0:T(8,128)(2,1)S(1)}, u32[]{:S(2)}, u32[]{:S(2)}) collective-permute-start(bf16[320,384]{1,0:T(8,128)(2,1)S(1)} %copy-done.10), channel_id=1, source_target_pairs={{0,5},{1,6},{2,7},{3,0},{4,1},{5,2},{6,3},{7,4},{8,13},{9,14},{10,... | collective-permute-start | bytes 737288 | tf_op jit(solution)/shard_map/ppermute | solution.py:578
  168.9 1.8 collective-permute-start.5
  170.7 11.6 %collective-permute-done.1.refs_2_ = bf16[320,384]{1,0:T(8,128)(2,1)S(1)} collective-permute-done((bf16[320,384]{1,0:T(8,128)(2,1)S(1)}, bf16[320,384]{1,0:T(8,128)(2,1)S(1)}, u32[]{:S(2)}, u32[]{:S(2)}) %collective-permute-start.1) | collective-permute-done | bytes 245792 | tf_op jit(solution)/shard_map/ppermute | solution.py:578
  182.3 6.7 %collective-permute-done.2.refs_3_ = bf16[320,384]{1,0:T(8,128)(2,1)S(1)} collective-permute-done((bf16[320,384]{1,0:T(8,128)(2,1)S(1)}, bf16[320,384]{1,0:T(8,128)(2,1)S(1)}, u32[]{:S(2)}, u32[]{:S(2)}) %collective-permute-start.2) | collective-permute-done | bytes 245792 | tf_op jit(solution)/shard_map/ppermute | solution.py:578
  188.9 7.9 %collective-permute-done.3.refs_4_ = bf16[320,384]{1,0:T(8,128)(2,1)S(1)} collective-permute-done((bf16[320,384]{1,0:T(8,128)(2,1)S(1)}, bf16[320,384]{1,0:T(8,128)(2,1)S(1)}, u32[]{:S(2)}, u32[]{:S(2)}) %collective-permute-start.3) | collective-permute-done | bytes 245792 | tf_op jit(solution)/shard_map/ppermute | solution.py:578
  199.0 5.2 %shard_map.115 = (bf16[1024,512]{1,0:T(8,128)(2,1)}, bf16[512,384]{1,0:T(8,128)(2,1)}) custom-call(bf16[320,384]{1,0:T(8,128)(2,1)} %get-tuple-element.48.refs_0_, bf16[320,384]{1,0:T(8,128)(2,1)S(1)} %collective-permute-done.refs_1_, bf16[320,384]{1,0:T(8,128)(2,1)S(1)} %collective-permute-done.1.refs_2_, ...), custom_call_target="tpu_custom_call" | custom-call | flops 805306368 | bytes 6291456 | tf_op jit(solution)/shard_map/pallas_call | solution.py:47
  204.2 4.8 %all-to-all-start.3 = ((bf16[128,8,512]{2,1,0:T(8,128)(2,1)}), bf16[128,8,512]{2,1,0:T(8,128)(2,1)S(1)}, u32[]{:S(2)}, u32[]{:S(2)}) async-start(bf16[128,8,512]{2,1,0:T(8,128)(2,1)} %bitcast.33), calls=%async_computation.3 | async-start | bytes 2097152 | tf_op jit(solution)/shard_map/all_to_all | solution.py:460
  208.9 2.1 fusion.1
  211.1 16.9 %all-to-all-done.3 = bf16[128,8,512]{2,1,0:T(8,128)(2,1)S(1)} async-done(((bf16[128,8,512]{2,1,0:T(8,128)(2,1)}), bf16[128,8,512]{2,1,0:T(8,128)(2,1)S(1)}, u32[]{:S(2)}, u32[]{:S(2)}) %all-to-all-start.3) | async-done | bytes 1048608 | tf_op jit(solution)/shard_map/all_to_all | solution.py:460
  228.0 6.8 %shard_map.116 = (f32[2048,512]{1,0:T(8,128)}, f32[512,2048]{1,0:T(8,128)}, f32[8,8,8,512]{3,2,1,0:T(8,128)}) custom-call(s32[8,1024]{1,0:T(8,128)S(1)} %copy-done.6, bf16[1024,512]{1,0:T(8,128)(2,1)S(1)} %bitcast.27, bf16[8,16,40,256]{3,2,1,0:T(8,128)(2,1)} %bitcast.38), custom_call_target="tpu_custom_call" | custom-call | flops 2147483648 | bytes 15728640 | tf_op jit(solution)/shard_map/pallas_call | solution.py:47
  (49 shorter events, 8.0 us)
Async XLA Ops:
  7.2 59.1 %copy-start = (bf16[512,512]{1,0:T(8,128)(2,1)S(1)}, bf16[512,512]{1,0:T(8,128)(2,1)}, u32[]{:S(2)}) copy-start(bf16[512,512]{1,0:T(8,128)(2,1)} %param.12) | copy-start | bytes 1572868
  7.2 59.1 %all-gather.8.cloned.1.call-start = ((), (), s32[]{:S(2)}) async-start(), calls=%async_computation.7 | async-start | bytes 3538944 | tf_op jit(solution)/shard_map/all_gather | solution.py:479
  7.9 78.7 %all-gather.6.cloned.1.call-start = ((), (), s32[]{:S(2)}) async-start(), calls=%async_computation.6 | async-start | bytes 3538944 | tf_op jit(solution)/shard_map/all_gather | solution.py:513
  31.1 29.1 %copy-start.4 = (f32[512]{0:T(512)S(1)}, f32[512]{0:T(512)}, u32[]{:S(2)}) copy-start(f32[512]{0:T(512)} %param.13) | copy-start | bytes 6148
  31.1 29.1 %copy-start.5 = (s32[384,128]{1,0:T(8,128)S(1)}, s32[384,128]{1,0:T(8,128)}, u32[]{:S(2)}) copy-start(s32[384,128]{1,0:T(8,128)} %get-tuple-element.36.col_ref) | copy-start | bytes 589828
  61.9 166.0 %all-gather.10.cloned.1.call-start = ((), (), s32[]{:S(2)}) async-start(), calls=%async_computation.8 | async-start | bytes 2949120 | tf_op jit(solution)/shard_map/all_gather | solution.py:583
  126.4 36.3 %copy-start.13 = (bf16[320,384]{1,0:T(8,128)(2,1)S(1)}, bf16[320,384]{1,0:T(8,128)(2,1)}, u32[]{:S(2)}) copy-start(bf16[320,384]{1,0:T(8,128)(2,1)} %get-tuple-element.50) | copy-start | bytes 737284
  126.4 36.3 %copy-start.12 = (bf16[320,384]{1,0:T(8,128)(2,1)S(1)}, bf16[320,384]{1,0:T(8,128)(2,1)}, u32[]{:S(2)}) copy-start(bf16[320,384]{1,0:T(8,128)(2,1)} %get-tuple-element.51) | copy-start | bytes 737284
  126.4 38.4 %copy-start.11 = (bf16[320,384]{1,0:T(8,128)(2,1)S(1)}, bf16[320,384]{1,0:T(8,128)(2,1)}, u32[]{:S(2)}) copy-start(bf16[320,384]{1,0:T(8,128)(2,1)} %get-tuple-element.52) | copy-start | bytes 737284
  126.4 39.9 %copy-start.10 = (bf16[320,384]{1,0:T(8,128)(2,1)S(1)}, bf16[320,384]{1,0:T(8,128)(2,1)}, u32[]{:S(2)}) copy-start(bf16[320,384]{1,0:T(8,128)(2,1)} %get-tuple-element.53) | copy-start | bytes 737284
  126.4 42.5 %copy-start.9 = (bf16[320,384]{1,0:T(8,128)(2,1)S(1)}, bf16[320,384]{1,0:T(8,128)(2,1)}, u32[]{:S(2)}) copy-start(bf16[320,384]{1,0:T(8,128)(2,1)} %get-tuple-element.54) | copy-start | bytes 737284
  126.4 55.8 %copy-start.8 = (bf16[320,384]{1,0:T(8,128)(2,1)S(1)}, bf16[320,384]{1,0:T(8,128)(2,1)}, u32[]{:S(2)}) copy-start(bf16[320,384]{1,0:T(8,128)(2,1)} %get-tuple-element.55) | copy-start | bytes 737284
  126.4 72.5 %copy-start.1 = (bf16[1,384,512]{2,1,0:T(8,128)(2,1)S(1)}, bf16[1,384,512]{2,1,0:T(8,128)(2,1)}, u32[]{:S(2)}) copy-start(bf16[1,384,512]{2,1,0:T(8,128)(2,1)} %param.15) | copy-start | bytes 1179652
  126.4 72.5 %copy-start.2 = (bf16[384,512]{1,0:T(8,128)(2,1)S(1)}, bf16[384,512]{1,0:T(8,128)(2,1)}, u32[]{:S(2)}) copy-start(bf16[384,512]{1,0:T(8,128)(2,1)} %get-tuple-element.37.refs_10_) | copy-start | bytes 1179652
  126.5 72.5 %copy-start.3 = (s32[8,384]{1,0:T(8,128)S(1)}, s32[8,384]{1,0:T(8,128)}, u32[]{:S(2)}) copy-start(s32[8,384]{1,0:T(8,128)} %get-tuple-element.56.refs_12_) | copy-start | bytes 36868
  159.0 9.8 %collective-permute-start = (bf16[320,384]{1,0:T(8,128)(2,1)}, bf16[320,384]{1,0:T(8,128)(2,1)S(1)}, u32[]{:S(2)}, u32[]{:S(2)}) collective-permute-start(bf16[320,384]{1,0:T(8,128)(2,1)} %get-tuple-element.49), channel_id=1, source_target_pairs={{0,1},{1,2},{2,3},{3,4},{4,5},{5,6},{6,7},{7,0},{8,9},{9,10},{10,1... | collective-permute-start | bytes 737288 | tf_op jit(solution)/shard_map/ppermute | solution.py:578
  162.7 19.6 %collective-permute-start.1 = (bf16[320,384]{1,0:T(8,128)(2,1)S(1)}, bf16[320,384]{1,0:T(8,128)(2,1)S(1)}, u32[]{:S(2)}, u32[]{:S(2)}) collective-permute-start(bf16[320,384]{1,0:T(8,128)(2,1)S(1)} %copy-done.13), channel_id=1, source_target_pairs={{0,2},{1,3},{2,4},{3,5},{4,6},{5,7},{6,0},{7,1},{8,10},{9,11},{10,... | collective-permute-start | bytes 737288 | tf_op jit(solution)/shard_map/ppermute | solution.py:578
  162.7 26.3 %collective-permute-start.2 = (bf16[320,384]{1,0:T(8,128)(2,1)S(1)}, bf16[320,384]{1,0:T(8,128)(2,1)S(1)}, u32[]{:S(2)}, u32[]{:S(2)}) collective-permute-start(bf16[320,384]{1,0:T(8,128)(2,1)S(1)} %copy-done.12), channel_id=1, source_target_pairs={{0,3},{1,4},{2,5},{3,6},{4,7},{5,0},{6,1},{7,2},{8,11},{9,12},{10,... | collective-permute-start | bytes 737288 | tf_op jit(solution)/shard_map/ppermute | solution.py:578
  164.8 32.0 %collective-permute-start.3 = (bf16[320,384]{1,0:T(8,128)(2,1)S(1)}, bf16[320,384]{1,0:T(8,128)(2,1)S(1)}, u32[]{:S(2)}, u32[]{:S(2)}) collective-permute-start(bf16[320,384]{1,0:T(8,128)(2,1)S(1)} %copy-done.11), channel_id=1, source_target_pairs={{0,4},{1,5},{2,6},{3,7},{4,0},{5,1},{6,2},{7,3},{8,12},{9,13},{10,... | collective-permute-start | bytes 737288 | tf_op jit(solution)/shard_map/ppermute | solution.py:578
  166.3 30.9 %collective-permute-start.4 = (bf16[320,384]{1,0:T(8,128)(2,1)S(1)}, bf16[320,384]{1,0:T(8,128)(2,1)S(1)}, u32[]{:S(2)}, u32[]{:S(2)}) collective-permute-start(bf16[320,384]{1,0:T(8,128)(2,1)S(1)} %copy-done.10), channel_id=1, source_target_pairs={{0,5},{1,6},{2,7},{3,0},{4,1},{5,2},{6,3},{7,4},{8,13},{9,14},{10,... | collective-permute-start | bytes 737288 | tf_op jit(solution)/shard_map/ppermute | solution.py:578
  168.9 29.2 %collective-permute-start.5 = (bf16[320,384]{1,0:T(8,128)(2,1)S(1)}, bf16[320,384]{1,0:T(8,128)(2,1)S(1)}, u32[]{:S(2)}, u32[]{:S(2)}) collective-permute-start(bf16[320,384]{1,0:T(8,128)(2,1)S(1)} %copy-done.9), channel_id=1, source_target_pairs={{0,6},{1,7},{2,0},{3,1},{4,2},{5,3},{6,4},{7,5},{8,14},{9,15},{10,... | collective-permute-start | bytes 737288 | tf_op jit(solution)/shard_map/ppermute | solution.py:578
  182.3 16.7 %collective-permute-start.6 = (bf16[320,384]{1,0:T(8,128)(2,1)S(1)}, bf16[320,384]{1,0:T(8,128)(2,1)S(1)}, u32[]{:S(2)}, u32[]{:S(2)}) collective-permute-start(bf16[320,384]{1,0:T(8,128)(2,1)S(1)} %copy-done.8), channel_id=1, source_target_pairs={{0,7},{1,0},{2,1},{3,2},{4,3},{5,4},{6,5},{7,6},{8,15},{9,8},{10,9... | collective-permute-start | bytes 737288 | tf_op jit(solution)/shard_map/ppermute | solution.py:578
  198.9 29.0 %copy-start.6 = (s32[8,1024]{1,0:T(8,128)S(1)}, s32[8,1024]{1,0:T(8,128)}, u32[]{:S(2)}) copy-start(s32[8,1024]{1,0:T(8,128)} %get-tuple-element.58.row_ref) | copy-start | bytes 98308
  204.2 23.8 %all-to-all-start.3 = ((bf16[128,8,512]{2,1,0:T(8,128)(2,1)}), bf16[128,8,512]{2,1,0:T(8,128)(2,1)S(1)}, u32[]{:S(2)}, u32[]{:S(2)}) async-start(bf16[128,8,512]{2,1,0:T(8,128)(2,1)} %bitcast.33), calls=%async_computation.3 | async-start | bytes 2097152 | tf_op jit(solution)/shard_map/all_to_all | solution.py:460
  (1 other events, 25.8 us)
Sparse Core Ops, SparseCore 0:
  9.7 32.1 all-gather.7
  62.0 24.5 all-gather.5
  159.2 41.2 all-gather.9
